TPU v7x, 32 devices: a whole 2x2x4 slice. The times are simulated.
32 devices in a mesh: book: 2 (over y), seq: 4 (over x, core), sub: 4 (over z).
Axes of the slice: x: 2, y: 2, z: 4, core: 2. Of those that a mesh axis runs over, the one named last changes fastest.
Arguments:
- queries: bfloat16 [16384, 2048], P(('book', 'seq'), 'sub'), parts along dimension 0, may hold values from -4 to 1920
- keys: bfloat16 [16384, 2048], P(('book', 'seq'), 'sub'), parts along dimension 0, may hold values from -6 to 4
- values: bfloat16 [16384, 2048], P(('book', 'seq'), 'sub'), parts along dimension 0, may hold values from -6 to 6
- decay: float32 [8, 8], P('book', 'sub'), parts along dimension 0, may hold values from 0.05 to 1
- gate: float32 [8], P('sub'), may hold values from -0.5 to 3
- summary: bfloat16 [512, 2048], P(('book', 'seq')), parts along dimension 0, may hold values from -6 to 6
- wq_sum: bfloat16 [2048, 2048], P(None, 'sub'), may hold values from -0.25 to 0.25
- wo_sum: bfloat16 [2048, 2048], P('sub'), may hold values from -0.125 to 0.125
Outputs:
- attended: bfloat16 [16384, 2048], P(('book', 'seq'), 'sub'), parts along dimension 0
- summarized: bfloat16 [512, 2048], P(('book', 'seq')), parts along dimension 0
There are 2 independent parts, one for each index of `book`. A program takes and returns all parts, laid end to end along the dimension named above; an argument that names none is the same for every part. Nothing has to cross between parts.
All inputs are finite; a program needn't handle non-finite values.
Results may differ from a plain program's by a relative error of at most 0.019.
Values may be sent and summed in bfloat16 or wider, within the bound.
No kernel may reach another device: no remote copies, remote signals or barrier semaphores. Data moves between devices by JAX's collectives and lax.ppermute only.
A program may use at most 128 MiB of HBM per device.

v0:
```python
import jax
import jax.numpy as jnp
from jax import lax
from jax.sharding import PartitionSpec as P

SEG = 2048
STEPS = 4


top_precision = lax.Precision.HIGHEST


def carried_in(value, axis, join, neutral):
    count, mine = (lax.axis_size(axis), lax.axis_index(axis))
    pieces = jax.tree.map(lambda part: lax.all_gather(part, axis), value)
    so_far = jax.tree.map(
        lambda part, zero: jnp.full_like(part, 0) + jnp.asarray(zero, part.dtype), value, neutral
    )

    def step(position, so_far):
        longer = join(so_far, jax.tree.map(lambda part: part[position], pieces))
        return jax.tree.map(lambda new, old: jnp.where(position < mine, new, old), longer, so_far)

    return lax.fori_loop(0, count - 1, step, so_far)


def broadcast(x, axis, root):
    mine = lax.axis_index(axis) == root
    return lax.psum(jnp.where(mine, x, jnp.zeros_like(x)), axis)


def feature_map(inputs):
    return jax.nn.elu(inputs) + 1.0


def head_rms(inputs):
    return inputs * lax.rsqrt(jnp.mean(inputs * inputs, axis=-1, keepdims=True) + 1e-06)


def memory_read(lifted, memory, normalizer):
    numerator = jnp.einsum("qhd,hde->qhe", lifted, memory, precision=top_precision)
    denominator = jnp.einsum("qhd,hd->qh", lifted, normalizer, precision=top_precision) + 1.0
    return numerator / denominator[..., None]


def segment_attention(q_part, k_part, v_part):
    length = q_part.shape[0]
    block_rows = min(512, length)
    score_scale = q_part.shape[2] ** (-0.5)
    columns = jnp.arange(length)
    pieces = []
    for first_row in range(0, length, block_rows):
        scores = (
            jnp.einsum(
                "qhd,khd->hqk",
                q_part[first_row : first_row + block_rows],
                k_part,
                preferred_element_type=jnp.float32,
            )
            * score_scale
        )
        rows_here = first_row + jnp.arange(block_rows)
        scores = jnp.where(columns[None, None, :] <= rows_here[None, :, None], scores, -jnp.inf)
        weights = jax.nn.softmax(scores, axis=-1).astype(jnp.bfloat16)
        pieces.append(
            jnp.einsum("hqk,khd->qhd", weights, v_part, preferred_element_type=jnp.float32)
        )
    return jnp.concatenate(pieces, axis=0)


def on_device(queries, keys, values, decay, gate, summary, wq_sum, wo_sum):
    head_count = gate.shape[0]
    head_width = queries.shape[1] // head_count
    seg_count = queries.shape[0] // SEG
    position = lax.axis_index("seq")
    devices = lax.axis_size("seq")
    q_seg = queries.reshape(seg_count, SEG, head_count, head_width)
    k_seg = keys.reshape(seg_count, SEG, head_count, head_width)
    v_seg = values.reshape(seg_count, SEG, head_count, head_width)
    lifted_keys = feature_map(k_seg.astype(jnp.float32))
    updates = jnp.einsum(
        "jqhd,jqhe->jhde", lifted_keys, v_seg.astype(jnp.float32), precision=top_precision
    )
    key_sums = jnp.sum(lifted_keys, axis=1)
    local_decay = lax.dynamic_slice_in_dim(decay, position * seg_count, seg_count, 0)
    empty_memory = jnp.zeros((head_count, head_width, head_width), jnp.float32)
    empty_norm = jnp.zeros((head_count, head_width), jnp.float32)

    def accumulate(running, inputs_now):
        seg_decay, update, key_total = inputs_now
        return (
            (
                seg_decay[:, None, None] * running[0] + update,
                seg_decay[:, None] * running[1] + key_total,
            ),
            None,
        )

    (own_memory, own_norm), _ = lax.scan(
        accumulate, (empty_memory, empty_norm), (local_decay, updates, key_sums)
    )
    own_decay = jnp.prod(local_decay, axis=0)

    def combine(earlier, later):
        return (
            earlier[0] * later[0],
            later[0][:, None, None] * earlier[1] + later[1],
            later[0][:, None] * earlier[2] + later[2],
        )

    identity = (jnp.ones((head_count,), jnp.float32), empty_memory, empty_norm)
    _, prior_memory, prior_norm = carried_in(
        (own_decay, own_memory, own_norm), "seq", combine, identity
    )
    ending_memory = own_decay[:, None, None] * prior_memory + own_memory
    ending_norm = own_decay[:, None] * prior_norm + own_norm
    final_memory, final_norm = (
        broadcast(ending_memory, "seq", devices - 1),
        broadcast(ending_norm, "seq", devices - 1),
    )
    blend_weight = jax.nn.sigmoid(gate)[None, :, None]

    def one_segment(running, inputs_now):
        memory, normalizer = running
        q_part, k_part, v_part, seg_decay, update, key_total = inputs_now
        recalled = memory_read(feature_map(q_part.astype(jnp.float32)), memory, normalizer)
        local_out = segment_attention(q_part, k_part, v_part)
        mixed = head_rms(blend_weight * recalled + (1.0 - blend_weight) * local_out).astype(
            jnp.bfloat16
        )
        return (
            (
                seg_decay[:, None, None] * memory + update,
                seg_decay[:, None] * normalizer + key_total,
            ),
            mixed,
        )

    _, attended = lax.scan(
        one_segment,
        (prior_memory, prior_norm),
        (q_seg, k_seg, v_seg, local_decay, updates, key_sums),
    )
    attended = attended.reshape(seg_count * SEG, head_count * head_width)
    summary_state = summary
    row_count = summary.shape[0]
    for decode_step in range(STEPS):
        lifted = feature_map(
            jnp.dot(summary_state, wq_sum, preferred_element_type=jnp.float32).reshape(
                row_count, head_count, head_width
            )
        )
        recalled = head_rms(memory_read(lifted, final_memory, final_norm)).astype(jnp.bfloat16)
        partial_out = jnp.dot(
            recalled.reshape(row_count, head_count * head_width),
            wo_sum,
            preferred_element_type=jnp.float32,
        )
        summed = lax.psum(partial_out.astype(jnp.bfloat16), "sub").astype(jnp.float32)
        summary_state = (summary_state.astype(jnp.float32) + summed).astype(jnp.bfloat16)
    return (attended, summary_state)


def solution(mesh):
    placed = (
        P(("book", "seq"), "sub"),
        P(("book", "seq"), "sub"),
        P(("book", "seq"), "sub"),
        P("book", "sub"),
        P("sub"),
        P(("book", "seq"), None),
        P(None, "sub"),
        P("sub", None),
    )
    return jax.shard_map(
        on_device,
        mesh=mesh,
        in_specs=placed,
        out_specs=(P(("book", "seq"), "sub"), P(("book", "seq"), None)),
        check_vma=False,
    )
```

profile of v0, /device:TPU:0, one launch (start us, length us, event | category | flops | bytes accessed | tf_op | source)
XLA Modules:
  0.0 366.3 jit_solution(7190378475324766708)
XLA Ops:
  8.3 7.9 %fusion.73 = f32[2,256,256]{2,1,0:T(8,128)} fusion(bf16[256,2,8,256]{3,2,1,0:T(8,128)(2,1)} %bitcast.224, bf16[256,2,8,256]{3,2,1,0:T(8,128)(2,1)} %bitcast.186, f32[2]{0:T(128)S(1)} %broadcast_multiply_fusion), kind=kOutput, calls=%fused_computation.95 | convolution fusion | flops 3226599424 | bytes 4718600 | tf_op jit(solution)/shard_map/jqhd,jqhe->jhde/dot_general | solution.py:81
  29.7 6.4 %fusion.46 = f32[2,512,2048]{2,1,0:T(8,128)} fusion(bf16[512,2,256]{0,2,1:T(8,128)(2,1)} %bitcast.197, bf16[256,2,8,256]{3,2,1,0:T(8,128)(2,1)} %bitcast.187), kind=kOutput, calls=%fused_computation.76 | convolution fusion | flops 1073741824 | bytes 11010048 | tf_op jit(solution)/shard_map/while/body/eval_jaxpr/qhd,khd->hqk/dot_general | solution.py:54
  39.8 6.4 %fusion.48 = f32[2,512,2048]{2,1,0:T(8,128)} fusion(bf16[512,2,256]{0,2,1:T(8,128)(2,1)} %bitcast.198, bf16[256,2,8,256]{3,2,1,0:T(8,128)(2,1)} %bitcast.188), kind=kOutput, calls=%fused_computation.78 | convolution fusion | flops 1073741824 | bytes 11010048 | tf_op jit(solution)/shard_map/while/body/eval_jaxpr/qhd,khd->hqk/dot_general | solution.py:54
  49.8 6.4 %fusion.50 = f32[2,512,2048]{2,1,0:T(8,128)} fusion(bf16[512,2,256]{0,2,1:T(8,128)(2,1)} %bitcast.199, bf16[256,2,8,256]{3,2,1,0:T(8,128)(2,1)} %bitcast.189), kind=kOutput, calls=%fused_computation.80 | convolution fusion | flops 1073741824 | bytes 11010048 | tf_op jit(solution)/shard_map/while/body/eval_jaxpr/qhd,khd->hqk/dot_general | solution.py:54
  58.9 6.4 %fusion.52 = f32[2,512,2048]{2,1,0:T(8,128)} fusion(bf16[512,2,256]{0,2,1:T(8,128)(2,1)} %bitcast.200, bf16[256,2,8,256]{3,2,1,0:T(8,128)(2,1)} %bitcast.190), kind=kOutput, calls=%fused_computation.82 | convolution fusion | flops 1073741824 | bytes 11010048 | tf_op jit(solution)/shard_map/while/body/eval_jaxpr/qhd,khd->hqk/dot_general | solution.py:54
  65.8 6.0 %all-gather.1 = f32[4,1,2]{2,1,0:T(1,128)} all-gather(f32[1,1,2]{2,1,0:T(1,128)S(1)} %bitcast.214), channel_id=1, replica_groups=mesh['book'=2,'seq'=4,'sub'=4] {'seq'}, dimensions={0}, use_global_device_ids=true | all-gather | bytes 40 | tf_op jit(solution)/shard_map/all_gather | solution.py:15
  71.9 5.6 %all_gather.14 = f32[4,2,256]{2,1,0:T(2,128)S(1)} all-gather(f32[1,2,256]{2,1,0:T(2,128)S(1)} %broadcast_add_fusion), channel_id=1, replica_groups=mesh['book'=2,'seq'=4,'sub'=4] {'seq'}, dimensions={0}, use_global_device_ids=true | all-gather | bytes 10240 | tf_op jit(solution)/shard_map/all_gather | solution.py:15
  77.5 13.3 %fusion.171 = (f32[2,512]{1,0:T(2,128)S(1)}, f32[2,512,2048]{2,1,0:T(8,128)}) fusion(f32[2,512,2048]{2,1,0:T(8,128)} %fusion.46, pred[512,2048]{1,0:T(8,128)(4,1)} %iota_compare_fusion), kind=kOutput, calls=%fused_computation.225 | output fusion | flops 12584959 | bytes 17829888 | tf_op jit(solution)/shard_map/while/body/eval_jaxpr/sub | solution.py:64
  90.7 6.5 %fusion.61 = f32[512,2,256]{0,2,1:T(8,128)} fusion(f32[2,512,2048]{2,1,0:T(8,128)} %get-tuple-element.252, f32[2,512]{1,0:T(2,128)S(1)} %get-tuple-element.251, bf16[256,2,8,256]{3,2,1,0:T(8,128)(2,1)} %bitcast.225), kind=kOutput, calls=%fused_computation.91 | convolution fusion | flops 1077936128 | bytes 11538432 | tf_op jit(solution)/shard_map/while/body/eval_jaxpr/hqk,khd->qhd/dot_general | solution.py:66
  97.2 8.6 %fusion.172 = (f32[2,512]{1,0:T(2,128)S(1)}, f32[2,512,2048]{2,1,0:T(8,128)}) fusion(f32[2,512,2048]{2,1,0:T(8,128)S(1)} %bitcast.193, pred[512,2048]{1,0:T(8,128)(4,1)} %iota_compare_fusion.1), kind=kOutput, calls=%fused_computation.226 | output fusion | flops 12584959 | bytes 17829888 | tf_op jit(solution)/shard_map/while/body/eval_jaxpr/sub | solution.py:64
  105.8 6.5 %fusion.64 = f32[512,2,256]{0,2,1:T(8,128)} fusion(f32[2,512,2048]{2,1,0:T(8,128)} %get-tuple-element.254, f32[2,512]{1,0:T(2,128)S(1)} %get-tuple-element.253, bf16[256,2,8,256]{3,2,1,0:T(8,128)(2,1)} %bitcast.226), kind=kOutput, calls=%fused_computation.92 | convolution fusion | flops 1077936128 | bytes 11538432 | tf_op jit(solution)/shard_map/while/body/eval_jaxpr/hqk,khd->qhd/dot_general | solution.py:66
  112.4 13.0 %fusion.173 = (f32[2,512]{1,0:T(2,128)S(1)}, f32[2,512,2048]{2,1,0:T(8,128)}) fusion(f32[2,512,2048]{2,1,0:T(8,128)} %fusion.50, pred[512,2048]{1,0:T(8,128)(4,1)S(1)} %copy-done.6), kind=kOutput, calls=%fused_computation.227 | output fusion | flops 12584959 | bytes 17829888 | tf_op jit(solution)/shard_map/while/body/eval_jaxpr/sub | solution.py:64
  125.8 12.7 %fusion.174 = (f32[2,512]{1,0:T(2,128)S(1)}, f32[2,512,2048]{2,1,0:T(8,128)}) fusion(f32[2,512,2048]{2,1,0:T(8,128)} %fusion.52, pred[512,2048]{1,0:T(8,128)(4,1)S(1)} %copy-done.5), kind=kOutput, calls=%fused_computation.228 | output fusion | flops 12584959 | bytes 17829888 | tf_op jit(solution)/shard_map/while/body/eval_jaxpr/sub | solution.py:64
  138.6 6.0 %fusion.67 = f32[512,2,256]{0,2,1:T(8,128)} fusion(f32[2,512,2048]{2,1,0:T(8,128)} %get-tuple-element.256, f32[2,512]{1,0:T(2,128)S(1)} %get-tuple-element.255, bf16[256,2,8,256]{3,2,1,0:T(8,128)(2,1)S(1)} %bitcast.227), kind=kOutput, calls=%fused_computation.93 | convolution fusion | flops 1077936128 | bytes 11538432 | tf_op jit(solution)/shard_map/while/body/eval_jaxpr/hqk,khd->qhd/dot_general | solution.py:66
  147.1 5.9 %while.10 = (s32[]{:T(128)}, f32[2,256,256]{2,1,0:T(8,128)S(1)}, f32[2,256]{1,0:T(2,128)S(1)}, s32[]{:T(128)}, f32[4,2]{1,0:T(4,128)}, /*index=5*/f32[4,2,256,25...) while((s32[]{:T(128)}, f32[2,256,256]{2,1,0:T(8,128)S(1)}, f32[2,256]{1,0:T(2,128)S(1)}, ...), condition=%wide.region_2.3_spmd.clone, body=%wide.region_1.2_spmd.clone.sunk | while | flops 526340 | bytes 1579175 | solution.py:24
  153.8 7.3 %psum.43 = f32[2,256]{1,0:T(2,128)S(1)} all-reduce(f32[2,256]{1,0:T(2,128)S(1)} %add_select_fusion.1), channel_id=1, replica_groups=mesh['book'=2,'seq'=4,'sub'=4] {'seq'}, use_global_device_ids=true, to_apply=%region_13.14 | all-reduce | flops 512 | bytes 4096 | tf_op jit(solution)/shard_map/psum | solution.py:29
  163.2 7.0 %fusion.38 = f32[2,1,2048]{2,1,0:T(1,128)S(1)} fusion(f32[256,2,8,256]{3,2,1,0:T(8,128)} %bitcast.194, f32[2,256,1]{1,0,2:T(2,128)S(1)} %bitcast.213), kind=kOutput, calls=%fused_computation.66 | convolution fusion | flops 16777216 | bytes 4212736 | tf_op jit(solution)/shard_map/while/body/eval_jaxpr/qhd,hd->qh/dot_general | solution.py:42
  170.4 26.0 %all-reduce.6.cloned.1.call-done = f32[2,256,256]{2,1,0:T(8,128)} async-done(((f32[2,256,256]{2,1,0:T(8,128)}), f32[2,256,256]{2,1,0:T(8,128)}) %all-reduce.6.cloned.1.call-update) | async-done | bytes 524304 | tf_op jit(solution)/shard_map/psum | solution.py:29
  199.5 35.4 %all-reduce.8.cloned.1.call-done = bf16[64,2048]{1,0:T(8,128)(2,1)} async-done(((bf16[64,2048]{1,0:T(8,128)(2,1)}), bf16[64,2048]{1,0:T(8,128)(2,1)}) %all-reduce.8.cloned.1.call-update) | async-done | bytes 262160 | tf_op jit(solution)/shard_map/psum | solution.py:159
  240.5 17.1 %multiply_reduce_fusion = (f32[2048,2]{0,1:T(2,128)S(1)}, f32[2048,2,256]{0,2,1:T(8,128)}) fusion(f32[512,2,256]{0,2,1:T(8,128)} %fusion.61, f32[512,2,256]{0,2,1:T(8,128)} %fusion.64, f32[512,2,256]{0,2,1:T(8,128)} %fusion.67, f32[512,2,256]{0,2,1:T(8,128)} %fusion.70, f32[2]{0:T(128)S(1)} %copy-done.13, f32[2048,2]{0,1:T(2,128)S(1)} %fusion.134, ...), kind=kOutput, calls=%fused_computation.45 | convolution fusion | flops 3234852864 | bytes 13139984 | tf_op jit(solution)/shard_map/while/body/eval_jaxpr/qhd,hde->qhe/dot_general | solution.py:41
  257.6 17.8 %all-reduce.10.cloned.1.call-done = bf16[64,2048]{1,0:T(8,128)(2,1)} async-done(((bf16[64,2048]{1,0:T(8,128)(2,1)}), bf16[64,2048]{1,0:T(8,128)(2,1)}) %all-reduce.10.cloned.1.call-update) | async-done | bytes 262160 | tf_op jit(solution)/shard_map/psum | solution.py:159
  281.8 35.2 %all-reduce.12.cloned.1.call-done = bf16[64,2048]{1,0:T(8,128)(2,1)} async-done(((bf16[64,2048]{1,0:T(8,128)(2,1)}), bf16[64,2048]{1,0:T(8,128)(2,1)}) %all-reduce.12.cloned.1.call-update) | async-done | bytes 262160 | tf_op jit(solution)/shard_map/psum | solution.py:159
  322.4 4.1 %multiply_convert_fusion = bf16[2048,2,256]{0,2,1:T(8,128)(2,1)} fusion(f32[2048,2,256]{0,2,1:T(8,128)} %get-tuple-element.260, f32[2048,2]{0,1:T(2,128)S(1)} %add_rsqrt_fusion), kind=kLoop, calls=%fused_computation.44 | loop fusion | flops 2097152 | bytes 6307840 | tf_op jit(solution)/shard_map/while/body/eval_jaxpr/convert_element_type | solution.py:128
  330.3 27.2 %all-reduce.14.cloned.1.call-done = bf16[64,2048]{1,0:T(8,128)(2,1)} async-done(((bf16[64,2048]{1,0:T(8,128)(2,1)}), bf16[64,2048]{1,0:T(8,128)(2,1)}) %all-reduce.14.cloned.1.call-update) | async-done | bytes 262160 | tf_op jit(solution)/shard_map/psum | solution.py:159
  (121 shorter events, 63.1 us)
Async XLA Ops:
  7.2 191.0 %copy-start = (bf16[512,2048]{1,0:T(8,128)(2,1)S(1)}, bf16[512,2048]{1,0:T(8,128)(2,1)}, u32[]{:S(2)}) copy-start(bf16[512,2048]{1,0:T(8,128)(2,1)} %param.17) | copy-start | bytes 6291460
  7.2 140.0 %all-gather.4.cloned.1.call-start = ((), (), s32[]{:S(2)}) async-start(), calls=%async_computation.5 | async-start | bytes 2621440 | tf_op jit(solution)/shard_map/all_gather | solution.py:15
  8.2 57.6 %copy-start.9 = (f32[2]{0:T(128)}, f32[2]{0:T(128)S(1)}, u32[]{:S(2)}) copy-start(f32[2]{0:T(128)S(1)} %dynamic-slice_reduce_fusion) | copy-start | bytes 28
  8.2 63.6 %copy-start.10 = (f32[2]{0:T(128)}, f32[2]{0:T(128)S(1)}, u32[]{:S(2)}) copy-start(f32[2]{0:T(128)S(1)} %broadcast_multiply_fusion) | copy-start | bytes 28
  16.2 180.3 %all-reduce.6.cloned.1.call-start = ((), (), s32[]{:S(2)}) async-start(), calls=%async_computation | async-start | bytes 1048576 | tf_op jit(solution)/shard_map/psum | solution.py:29
  16.7 4.2 %copy-start.2 = (bf16[2048,512]{1,0:T(8,128)(2,1)S(1)}, bf16[2048,512]{1,0:T(8,128)(2,1)}, u32[]{:S(2)}) copy-start(bf16[2048,512]{1,0:T(8,128)(2,1)} %param.10) | copy-start | bytes 6291460
  58.9 6.4 %copy-start.12 = (f32[2]{0:T(128)S(1)}, f32[2]{0:T(128)}, u32[]{:S(2)}) copy-start(f32[2]{0:T(128)} %param.14) | copy-start | bytes 28
  77.5 19.8 %slice-start = ((s8[8388608]{0:T(1024)(128)(4,1)}), s8[4194304]{0:T(1024)(128)(4,1)S(1)}, s32[]{:S(2)}) async-start(s8[8388608]{0:T(1024)(128)(4,1)} %bitcast.192), calls=%async_computation.6 | async-start | bytes 8388608
  90.7 6.5 %slice-start.1 = ((s8[8388608]{0:T(1024)(128)(4,1)}), s8[4194304]{0:T(1024)(128)(4,1)S(1)}, s32[]{:S(2)}) async-start(s8[8388608]{0:T(1024)(128)(4,1)} %bitcast.192), calls=%async_computation.7 | async-start | bytes 8388608
  105.8 6.5 %copy-start.6 = (pred[512,2048]{1,0:T(8,128)(4,1)S(1)}, pred[512,2048]{1,0:T(8,128)(4,1)}, u32[]{:S(2)}) copy-start(pred[512,2048]{1,0:T(8,128)(4,1)} %iota_compare_fusion.2) | copy-start | bytes 3145732
  112.3 13.0 %copy-start.1 = (bf16[2048,512]{1,0:T(8,128)(2,1)S(1)}, bf16[2048,512]{1,0:T(8,128)(2,1)}, u32[]{:S(2)}) copy-start(bf16[2048,512]{1,0:T(8,128)(2,1)} %param.16) | copy-start | bytes 6291460
  112.3 13.0 %copy-start.3 = (bf16[64,2048]{1,0:T(8,128)(2,1)S(1)}, bf16[64,2048]{1,0:T(8,128)(2,1)}, u32[]{:S(2)}) copy-start(bf16[64,2048]{1,0:T(8,128)(2,1)} %param.15) | copy-start | bytes 786436
  112.3 13.5 %copy-start.5 = (pred[512,2048]{1,0:T(8,128)(4,1)S(1)}, pred[512,2048]{1,0:T(8,128)(4,1)}, u32[]{:S(2)}) copy-start(pred[512,2048]{1,0:T(8,128)(4,1)} %iota_compare_fusion.3) | copy-start | bytes 3145732
  125.8 12.8 %copy-start.11 = (bf16[2048,512]{1,0:T(8,128)(2,1)S(1)}, bf16[2048,512]{1,0:T(8,128)(2,1)}, u32[]{:S(2)}) copy-start(bf16[2048,512]{1,0:T(8,128)(2,1)} %param.12) | copy-start | bytes 6291460
  138.6 6.0 %copy-start.15 = (f32[2,512,2048]{2,1,0:T(8,128)S(1)}, f32[2,512,2048]{2,1,0:T(8,128)}, u32[]{:S(2)}) copy-start(f32[2,512,2048]{2,1,0:T(8,128)} %get-tuple-element.258) | copy-start | bytes 25165828
  147.1 14.0 %copy-start.4 = (f32[2,256,256]{2,1,0:T(8,128)S(1)}, f32[2,256,256]{2,1,0:T(8,128)}, u32[]{:S(2)}) copy-start(f32[2,256,256]{2,1,0:T(8,128)} %fusion.73) | copy-start | bytes 1572868
  162.8 72.1 %all-reduce.8.cloned.1.call-start = ((), (), s32[]{:S(2)}) async-start(), calls=%async_computation.1 | async-start | bytes 524288 | tf_op jit(solution)/shard_map/psum | solution.py:159
  199.4 41.1 %copy-start.13 = (f32[2]{0:T(128)S(1)}, f32[2]{0:T(128)}, u32[]{:S(2)}) copy-start(f32[2]{0:T(128)} %get-tuple-element.245) | copy-start | bytes 28
  199.4 41.1 %copy-start.14 = (f32[2]{0:T(128)S(1)}, f32[2]{0:T(128)}, u32[]{:S(2)}) copy-start(f32[2]{0:T(128)} %get-tuple-element.246) | copy-start | bytes 28
  199.4 76.0 %all-reduce.10.cloned.1.call-start = ((), (), s32[]{:S(2)}) async-start(), calls=%async_computation.2 | async-start | bytes 524288 | tf_op jit(solution)/shard_map/psum | solution.py:159
  240.2 76.8 %all-reduce.12.cloned.1.call-start = ((), (), s32[]{:S(2)}) async-start(), calls=%async_computation.3 | async-start | bytes 524288 | tf_op jit(solution)/shard_map/psum | solution.py:159
  240.5 35.0 %copy-start.7 = (bf16[64,2048]{1,0:T(8,128)(2,1)S(1)}, bf16[64,2048]{1,0:T(8,128)(2,1)}, u32[]{:S(2)}) copy-start(bf16[64,2048]{1,0:T(8,128)(2,1)} %all-reduce.8.cloned.1.call-done) | copy-start | bytes 786436
  281.8 75.8 %all-reduce.14.cloned.1.call-start = ((), (), s32[]{:S(2)}) async-start(), calls=%async_computation.4 | async-start | bytes 524288 | tf_op jit(solution)/shard_map/psum | solution.py:159
  322.3 35.2 %copy-start.8 = (bf16[64,2048]{1,0:T(8,128)(2,1)S(1)}, bf16[64,2048]{1,0:T(8,128)(2,1)}, u32[]{:S(2)}) copy-start(bf16[64,2048]{1,0:T(8,128)(2,1)} %all-reduce.12.cloned.1.call-done) | copy-start | bytes 786436
Sparse Core Ops, SparseCore 0:
  16.3 25.2 all-gather.3
  162.9 33.5 all-reduce.5
  199.5 35.3 all-reduce.7
  240.3 35.0 all-reduce.9
  281.9 35.0 all-reduce.11
  322.5 35.0 all-reduce.13
where the time goes:
time: 372 us; the launch traced here: 366 us
  waiting for transfers between devices  142 us (38%)
  matrix products  98.1 us (26%)
  other arithmetic  74.1 us (20%)
  blocking collectives  18.9 us (5%)
  local copies, waits for them, and re-layouts  17.6 us (5%)
  between operations  14.6 us (4%)
    psum x4, waiting for transfers between devices, on_device(): lax.psum(partial_out.astype(jnp.bfloat16), 'sub').astype(jnp.float32)  116 us
    sub x4, other arithmetic, segment_attention(): weights = jax.nn.softmax(scores, axis=-1).astype(jnp.bfloat16)  47.5 us
    psum x1, waiting for transfers between devices, broadcast(): return lax.psum(jnp.where(mine, x, jnp.zeros_like(x)), axis)  26 us
    dot_general x4, matrix products, segment_attention(): jnp.einsum('qhd,khd->hqk', q_part[first_row:first_row + block_rows], k_pa...  25.5 us
    dot_general x5, matrix products, memory_read(): jnp.einsum('qhd,hde->qhe', lifted, memory, precision=top_precision)  23.6 us
    dot_general x4, matrix products, segment_attention(): jnp.einsum('hqk,khd->qhd', weights, v_part, preferred_element_type=jnp.fl...  21.6 us
    all_gather x2, blocking collectives, carried_in(): pieces = jax.tree.map(lambda part: lax.all_gather(part, axis), value)  11.6 us
    unnamed x41, local copies, waits for them, and re-layouts  11.2 us
  transfers between devices with their start and end apart: 6, of which 5 were waited for; matrix products, arithmetic and copies ran while one was open for 41% of the time, Pallas kernels for 0%

commit v1 on v0

v1 whole, which is shorter than its diff:
```python
import functools

import jax
import jax.numpy as jnp
from jax import lax
from jax.experimental import pallas as pl
from jax.experimental.pallas import tpu as pltpu
from jax.sharding import PartitionSpec as P

SEG = 2048
STEPS = 4
EPS = 1e-06
LOG2E = 1.4426950408889634
PAD = 16


def lift(x):
    return jnp.where(x > 0.0, x + 1.0, jnp.exp(jnp.minimum(x, 0.0)))


def dot(a, b, dims):
    return lax.dot_general(a, b, (dims, ((), ())), preferred_element_type=jnp.float32)


def update_kernel(heads, width, k_ref, v_ref, u_ref, acc, norm):
    step = pl.program_id(0)

    @pl.when(step == 0)
    def _():
        acc[...] = jnp.zeros_like(acc)
        norm[...] = jnp.zeros_like(norm)

    for h in range(heads):
        cols = slice(h * width, (h + 1) * width)
        lifted = lift(k_ref[:, cols].astype(jnp.float32))
        norm[h, 0:1, :] += jnp.sum(lifted, axis=0, keepdims=True)
        acc[h] += dot(lifted.astype(jnp.bfloat16), v_ref[:, cols], ((0,), (0,)))

    @pl.when(step == pl.num_programs(0) - 1)
    def _():
        for h in range(heads):
            u_ref[h, :width, :] = acc[h].astype(jnp.bfloat16)
            u_ref[h, width:, :] = jnp.broadcast_to(norm[h, 0:1, :], (PAD, width)).astype(
                jnp.bfloat16
            )


def memory_update(keys, values, heads, width):
    rows = keys.shape[0]
    block = 512
    return pl.pallas_call(
        functools.partial(update_kernel, heads, width),
        grid=(rows // block,),
        in_specs=[pl.BlockSpec((block, heads * width), lambda i: (i, 0))] * 2,
        out_specs=pl.BlockSpec((heads, width + PAD, width), lambda i: (0, 0, 0)),
        out_shape=jax.ShapeDtypeStruct((heads, width + PAD, width), jnp.bfloat16),
        scratch_shapes=[
            pltpu.VMEM((heads, width, width), jnp.float32),
            pltpu.VMEM((heads, 8, width), jnp.float32),
        ],
        compiler_params=pltpu.CompilerParams(vmem_limit_bytes=16 << 20),
        cost_estimate=pl.CostEstimate(
            flops=2 * rows * heads * width * width,
            transcendentals=rows * heads * width,
            bytes_accessed=4 * rows * heads * width,
        ),
    )(keys, values)


def attention_kernel(heads, width, first, tile, gate_ref, q_ref, k_ref, v_ref, m_ref, *rest):
    o_ref = rest[-1]
    rows = q_ref.shape[0]
    factor = LOG2E * width ** (-0.5)
    blocks = (first + rows) // tile
    row = lax.broadcasted_iota(jnp.int32, (rows, tile), 0)
    col = lax.broadcasted_iota(jnp.int32, (rows, tile), 1)
    for h in range(heads):
        cols = slice(h * width, (h + 1) * width)
        q = q_ref[:, cols]
        scores = []
        for j in range(blocks):
            s = dot(q, k_ref[j * tile : (j + 1) * tile, cols], ((1,), (1,))) * factor
            if (j + 1) * tile > first + 1:
                s = jnp.where(col + j * tile <= row + first, s, -jnp.inf)
            scores.append(s)
        top = scores[0]
        for s in scores[1:]:
            top = jnp.maximum(top, s)
        top = jnp.max(top, axis=1, keepdims=True)
        total = jnp.zeros((rows, 1), jnp.float32)
        mixed = jnp.zeros((rows, width), jnp.float32)
        for j in range(blocks):
            p = jnp.exp2(scores[j] - top)
            total += jnp.sum(p, axis=1, keepdims=True)
            mixed += dot(p.astype(jnp.bfloat16), v_ref[j * tile : (j + 1) * tile, cols], ((1,), (0,)))
        lifted = lift(q.astype(jnp.float32)).astype(jnp.bfloat16)
        numerator = dot(lifted, m_ref[h, :width, :], ((1,), (0,)))
        norm = m_ref[h, width : width + 1, :].astype(jnp.float32)
        denominator = jnp.sum(lifted.astype(jnp.float32) * norm, axis=1, keepdims=True) + 1.0
        blend = 1.0 / (1.0 + jnp.exp(jnp.full((1, 1), -gate_ref[h], jnp.float32)))
        mixed = mixed * ((1.0 - blend) / total) + numerator * (blend / denominator)
        mean = jnp.mean(mixed * mixed, axis=1, keepdims=True)
        o_ref[:, cols] = (mixed * lax.rsqrt(mean + EPS)).astype(jnp.bfloat16)


def attention_piece(q, k, v, memory, gate, out, heads, width, first, rows):
    total, lanes = q.shape
    span = first + rows
    row_spec = pl.BlockSpec((rows, lanes), lambda i: (first // rows, 0))
    span_spec = pl.BlockSpec((span, lanes), lambda i: (0, 0))
    args = [gate, q, k, v, memory]
    specs = [
        pl.BlockSpec(memory_space=pltpu.SMEM),
        row_spec,
        span_spec,
        span_spec,
        pl.BlockSpec(memory.shape, lambda i: (0, 0, 0)),
    ]
    aliases = {}
    if out is not None:
        args.append(out)
        specs.append(pl.BlockSpec(memory_space=pl.ANY))
        aliases = {5: 0}
    return pl.pallas_call(
        functools.partial(attention_kernel, heads, width, first, 512),
        grid=(1,),
        in_specs=specs,
        out_specs=row_spec,
        out_shape=jax.ShapeDtypeStruct((total, lanes), jnp.bfloat16),
        input_output_aliases=aliases,
        compiler_params=pltpu.CompilerParams(vmem_limit_bytes=40 << 20),
        cost_estimate=pl.CostEstimate(
            flops=4 * rows * span * lanes,
            transcendentals=rows * span * heads,
            bytes_accessed=2 * lanes * (2 * rows + 2 * span),
        ),
    )(*args)


def step_kernel(heads, width, parts, *refs):
    state_refs, (wq_ref, wo_ref, m_ref), out_refs = refs[:parts], refs[parts : parts + 3], refs[parts + 3 :]
    size = state_refs[0].shape[0]
    state = jnp.concatenate([r[...] for r in state_refs], axis=0)
    reads = []
    for h in range(heads):
        cols = slice(h * width, (h + 1) * width)
        lifted = lift(dot(state, wq_ref[:, cols], ((1,), (0,)))).astype(jnp.bfloat16)
        numerator = dot(lifted, m_ref[h, :width, :], ((1,), (0,)))
        norm = m_ref[h, width : width + 1, :].astype(jnp.float32)
        denominator = jnp.sum(lifted.astype(jnp.float32) * norm, axis=1, keepdims=True) + 1.0
        read = numerator / denominator
        mean = jnp.mean(read * read, axis=1, keepdims=True)
        reads.append((read * lax.rsqrt(mean + EPS)).astype(jnp.bfloat16))
    partial = dot(jnp.concatenate(reads, axis=1), wo_ref[...], ((1,), (0,)))
    for j in range(parts):
        out_refs[j][...] = partial[j * size : (j + 1) * size].astype(jnp.bfloat16)


def summary_step(pieces, wq, wo, memory, heads, width):
    parts = len(pieces)
    shape = pieces[0].shape
    rows = parts * shape[0]
    return pl.pallas_call(
        functools.partial(step_kernel, heads, width, parts),
        in_specs=[pl.BlockSpec(memory_space=pltpu.VMEM)] * (parts + 3),
        out_specs=[pl.BlockSpec(memory_space=pltpu.VMEM)] * parts,
        out_shape=[jax.ShapeDtypeStruct(shape, jnp.bfloat16)] * parts,
        compiler_params=pltpu.CompilerParams(vmem_limit_bytes=16 << 20),
        cost_estimate=pl.CostEstimate(
            flops=2 * rows * (wq.size + wo.size),
            transcendentals=rows * heads * width,
            bytes_accessed=2 * (wq.size + wo.size) + 4 * rows * shape[1],
        ),
    )(*pieces, wq, wo, memory)


def partner(x, axis, flip):
    return lax.ppermute(x, axis, [(i, i ^ flip) for i in range(lax.axis_size(axis))])


def scan_memory(own, decay, axis):
    count, me = lax.axis_size(axis), lax.axis_index(axis)
    shape = own.shape
    total, prior = own, jnp.zeros_like(own)
    order = jnp.arange(count)
    level = 1
    while level < count:
        mine = (order // level) == (me // level)
        theirs = (order // level) == ((me ^ level) // level)

        def product(mask):
            return jnp.prod(jnp.where(mask[:, None], decay, 1.0), axis=0)[:, None, None]

        got = partner(total, axis, level).astype(jnp.float32)
        later = (me & level) != 0
        before_me = product(mine & (order < me))
        kept = total.astype(jnp.float32)
        prior = jnp.where(later, before_me * got + prior.astype(jnp.float32), prior.astype(jnp.float32)).astype(
            jnp.bfloat16
        )
        total = jnp.where(later, product(mine) * got + kept, product(theirs) * kept + got).astype(jnp.bfloat16)
        level *= 2
    return total, prior


def on_device(queries, keys, values, decay, gate, summary, wq_sum, wo_sum):
    heads = gate.shape[0]
    width = queries.shape[1] // heads
    parts, me = lax.axis_size("sub"), lax.axis_index("sub")

    own = memory_update(keys, values, heads, width)
    final, prior = scan_memory(own, decay, "seq")

    piece_rows = summary.shape[0] // parts
    pieces = [
        lax.dynamic_slice_in_dim(summary, (me ^ j) * piece_rows, piece_rows, 0) for j in range(parts)
    ]
    attended = None
    chunk = 512
    firsts = list(range(0, SEG, chunk))
    for step in range(STEPS):
        partial = summary_step(pieces, wq_sum, wo_sum, final, heads, width)
        got = [partner(partial[j], "sub", j) for j in range(parts - 1, 0, -1)]
        if step < len(firsts):
            attended = attention_piece(
                queries, keys, values, prior, gate, attended, heads, width, firsts[step], chunk
            )
        new = pieces[0].astype(jnp.float32) + partial[0].astype(jnp.float32)
        for g in got:
            new = new + g.astype(jnp.float32)
        new = new.astype(jnp.bfloat16)
        pieces = [new] + [partner(new, "sub", j) for j in range(parts - 1, 0, -1)][::-1]
    out = jnp.zeros_like(summary)
    for j in range(parts):
        out = lax.dynamic_update_slice_in_dim(out, pieces[j], (me ^ j) * piece_rows, 0)
    return (attended, out)


def solution(mesh):
    placed = (
        P(("book", "seq"), "sub"),
        P(("book", "seq"), "sub"),
        P(("book", "seq"), "sub"),
        P("book", "sub"),
        P("sub"),
        P(("book", "seq"), None),
        P(None, "sub"),
        P("sub", None),
    )
    return jax.shard_map(
        on_device,
        mesh=mesh,
        in_specs=placed,
        out_specs=(P(("book", "seq"), "sub"), P(("book", "seq"), None)),
        check_vma=False,
    )
```

time: 372 us -> 103 us (0.28); the launches traced: 366 us -> 103 us
  waiting for transfers between devices: 142 us -> 31.1 us
  matrix products: 98.1 us -> 0 us
  other arithmetic: 74.1 us -> 1 us
  starting transfers between devices: 1.35 us -> 39.2 us
  Pallas kernels: 0 us -> 25.1 us
  blocking collectives: 18.9 us -> 0 us
  between operations: 14.6 us -> 0.83 us
  local copies, waits for them, and re-layouts: 17.6 us -> 5.57 us
    psum x5 -> x0, waiting for transfers between devices: 142 us -> none  [the longest x4 116 us: on_device(): lax.psum(partial_out.astype(jnp.bfloat16), 'sub').astype(jnp.float32)]
    dot_general x27 -> x0, matrix products: 98.1 us -> none  [the longest x4 25.5 us: segment_attention(): jnp.einsum('qhd,khd->hqk', q_part[first_row:first_row + block_rows], k_pa...]
    sub x5 -> x0, other arithmetic: 48.1 us -> none  [the longest x4 47.5 us: segment_attention(): weights = jax.nn.softmax(scores, axis=-1).astype(jnp.bfloat16)]
    ppermute x0 -> x26, starting transfers between devices: none -> 39.2 us  [partner(): lax.ppermute(x, axis, [(i, i ^ flip) for i in range(lax.axis_size(axis))])]
    ppermute x0 -> x26, waiting for transfers between devices: none -> 31.1 us  [partner(): lax.ppermute(x, axis, [(i, i ^ flip) for i in range(lax.axis_size(axis))])]
    pallas_call x0 -> x9, Pallas kernels: none -> 25.1 us  [the longest x4 17 us: attention_piece(): pl.pallas_call(functools.partial(attention_kernel, heads, width, first, 5...]
    all_gather x2 -> x0, blocking collectives: 11.6 us -> none  [carried_in(): pieces = jax.tree.map(lambda part: lax.all_gather(part, axis), value)]
    convert_element_type x4 -> x5, other arithmetic: 9.37 us -> 0.73 us  [the longest x2 0.59 us: scan_memory(): jnp.where(later, product(mine) * got + kept, product(theirs) * kept + got)]
  transfers between devices with their start and end apart: 6 -> 26, of which waited for: 5 -> 14; matrix products, arithmetic and copies ran while one was open for 41% -> 0% of each run, Pallas kernels for 0% -> 17%
where the time goes in v1:
time: 103 us
  starting transfers between devices  39.2 us (38%)
  waiting for transfers between devices  31.1 us (30%)
  Pallas kernels  25.1 us (24%)
  local copies, waits for them, and re-layouts  5.57 us (5%)
    ppermute x26, starting transfers between devices, partner(): lax.ppermute(x, axis, [(i, i ^ flip) for i in range(lax.axis_size(axis))])  39.2 us
    ppermute x26, waiting for transfers between devices, partner(): lax.ppermute(x, axis, [(i, i ^ flip) for i in range(lax.axis_size(axis))])  31.1 us
    pallas_call x4, Pallas kernels, attention_piece(): pl.pallas_call(functools.partial(attention_kernel, heads, width, first, 5...  17 us
    pallas_call x4, Pallas kernels, summary_step(): pl.pallas_call(functools.partial(step_kernel, heads, width, parts), in_sp...  5.87 us
    unnamed x24, local copies, waits for them, and re-layouts  5.5 us
    pallas_call x1, Pallas kernels, memory_update(): pl.pallas_call(functools.partial(update_kernel, heads, width), grid=(rows...  2.18 us
  transfers between devices with their start and end apart: 26, of which 14 were waited for; matrix products, arithmetic and copies ran while one was open for 0% of the time, Pallas kernels for 17%

profile of v1, /device:TPU:0, one launch (start us, length us, event | category | flops | bytes accessed | tf_op | source)
XLA Modules:
  0.0 102.8 jit_solution(17650255871192738691)
XLA Ops:
  3.8 2.2 %shard_map.95 = bf16[2,272,256]{2,1,0:T(8,128)(2,1)S(1)} custom-call(bf16[2048,512]{1,0:T(8,128)(2,1)S(1)} %copy-done, bf16[2048,512]{1,0:T(8,128)(2,1)S(1)} %copy-done.2), custom_call_target="tpu_custom_call" | custom-call | flops 536870912 | bytes 4194304 | tf_op jit(solution)/shard_map/pallas_call | solution.py:51
  8.0 2.9 %collective-permute-start.1 = (bf16[2,272,256]{2,1,0:T(8,128)(2,1)S(1)}, bf16[2,272,256]{2,1,0:T(8,128)(2,1)S(1)}, u32[]{:S(2)}, u32[]{:S(2)}) collective-permute-start(bf16[2,272,256]{2,1,0:T(8,128)(2,1)S(1)} %fusion.1), channel_id=1, source_target_pairs={{0,8},{4,12},{8,0},{12,4},{1,9},{5,13},{9,1},{13,5},{2,10},{6,14},... | collective-permute-start | bytes 835592 | tf_op jit(solution)/shard_map/ppermute | solution.py:178
  10.9 6.9 %collective-permute-done.1 = bf16[2,272,256]{2,1,0:T(8,128)(2,1)S(1)} collective-permute-done((bf16[2,272,256]{2,1,0:T(8,128)(2,1)S(1)}, bf16[2,272,256]{2,1,0:T(8,128)(2,1)S(1)}, u32[]{:S(2)}, u32[]{:S(2)}) %collective-permute-start.1) | collective-permute-done | bytes 278560 | tf_op jit(solution)/shard_map/ppermute | solution.py:178
  21.3 3.9 %collective-permute-start.2 = (bf16[16,2048]{1,0:T(8,128)(2,1)S(1)}, bf16[16,2048]{1,0:T(8,128)(2,1)S(1)}, u32[]{:S(2)}, u32[]{:S(2)}) collective-permute-start(bf16[16,2048]{1,0:T(8,128)(2,1)S(1)} %get-tuple-element.19), channel_id=1, source_target_pairs={{0,3},{1,2},{2,1},{3,0},{4,7},{5,6},{6,5},{7,4},{8,11},{9,10},{10,... | collective-permute-start | bytes 196616 | tf_op jit(solution)/shard_map/ppermute | solution.py:178
  25.8 2.4 %collective-permute-done.2 = bf16[16,2048]{1,0:T(8,128)(2,1)S(1)} collective-permute-done((bf16[16,2048]{1,0:T(8,128)(2,1)S(1)}, bf16[16,2048]{1,0:T(8,128)(2,1)S(1)}, u32[]{:S(2)}, u32[]{:S(2)}) %collective-permute-start.2) | collective-permute-done | bytes 65568 | tf_op jit(solution)/shard_map/ppermute | solution.py:178
  28.2 2.3 %collective-permute-done.3 = bf16[16,2048]{1,0:T(8,128)(2,1)S(1)} collective-permute-done((bf16[16,2048]{1,0:T(8,128)(2,1)S(1)}, bf16[16,2048]{1,0:T(8,128)(2,1)S(1)}, u32[]{:S(2)}, u32[]{:S(2)}) %collective-permute-start.3) | collective-permute-done | bytes 65568 | tf_op jit(solution)/shard_map/ppermute | solution.py:178
  30.5 2.6 %collective-permute-start.7 = (bf16[16,2048]{1,0:T(8,128)(2,1)S(1)}, bf16[16,2048]{1,0:T(8,128)(2,1)S(1)}, u32[]{:S(2)}, u32[]{:S(2)}) collective-permute-start(bf16[16,2048]{1,0:T(8,128)(2,1)S(1)} %add_convert_fusion.3.refs_0_), channel_id=1, source_target_pairs={{0,3},{1,2},{2,1},{3,0},{4,7},{5,6},{6,5},{7,4},{8,11},{9,10},{10,... | collective-permute-start | bytes 196616 | tf_op jit(solution)/shard_map/ppermute | solution.py:178
  39.9 2.2 %collective-permute-start.8 = (bf16[16,2048]{1,0:T(8,128)(2,1)S(1)}, bf16[16,2048]{1,0:T(8,128)(2,1)S(1)}, u32[]{:S(2)}, u32[]{:S(2)}) collective-permute-start(bf16[16,2048]{1,0:T(8,128)(2,1)S(1)} %get-tuple-element.23), channel_id=1, source_target_pairs={{0,3},{1,2},{2,1},{3,0},{4,7},{5,6},{6,5},{7,4},{8,11},{9,10},{10,... | collective-permute-start | bytes 196616 | tf_op jit(solution)/shard_map/ppermute | solution.py:178
  42.3 2.1 %collective-permute-start.10 = (bf16[16,2048]{1,0:T(8,128)(2,1)S(1)}, bf16[16,2048]{1,0:T(8,128)(2,1)S(1)}, u32[]{:S(2)}, u32[]{:S(2)}) collective-permute-start(bf16[16,2048]{1,0:T(8,128)(2,1)S(1)} %get-tuple-element.25), channel_id=1, source_target_pairs={{0,1},{1,0},{2,3},{3,2},{4,5},{5,4},{6,7},{7,6},{8,9},{9,8},{10,11... | collective-permute-start | bytes 196616 | tf_op jit(solution)/shard_map/ppermute | solution.py:178
  46.1 2.6 %collective-permute-done.9 = bf16[16,2048]{1,0:T(8,128)(2,1)S(1)} collective-permute-done((bf16[16,2048]{1,0:T(8,128)(2,1)S(1)}, bf16[16,2048]{1,0:T(8,128)(2,1)S(1)}, u32[]{:S(2)}, u32[]{:S(2)}) %collective-permute-start.9) | collective-permute-done | bytes 65568 | tf_op jit(solution)/shard_map/ppermute | solution.py:178
  48.8 2.1 %collective-permute-start.13 = (bf16[16,2048]{1,0:T(8,128)(2,1)S(1)}, bf16[16,2048]{1,0:T(8,128)(2,1)S(1)}, u32[]{:S(2)}, u32[]{:S(2)}) collective-permute-start(bf16[16,2048]{1,0:T(8,128)(2,1)S(1)} %add_convert_fusion.2.refs_0_), channel_id=1, source_target_pairs={{0,3},{1,2},{2,1},{3,0},{4,7},{5,6},{6,5},{7,4},{8,11},{9,10},{10,... | collective-permute-start | bytes 196616 | tf_op jit(solution)/shard_map/ppermute | solution.py:178
  50.9 2.3 %collective-permute-start.11 = (bf16[16,2048]{1,0:T(8,128)(2,1)S(1)}, bf16[16,2048]{1,0:T(8,128)(2,1)S(1)}, u32[]{:S(2)}, u32[]{:S(2)}) collective-permute-start(bf16[16,2048]{1,0:T(8,128)(2,1)S(1)} %add_convert_fusion.2.refs_0_), channel_id=1, source_target_pairs={{0,1},{1,0},{2,3},{3,2},{4,5},{5,4},{6,7},{7,6},{8,9},{9,8},{10,11... | collective-permute-start | bytes 196616 | tf_op jit(solution)/shard_map/ppermute | solution.py:178
  55.0 3.5 %collective-permute-done.12.refs_2_ = bf16[16,2048]{1,0:T(8,128)(2,1)S(1)} collective-permute-done((bf16[16,2048]{1,0:T(8,128)(2,1)S(1)}, bf16[16,2048]{1,0:T(8,128)(2,1)S(1)}, u32[]{:S(2)}, u32[]{:S(2)}) %collective-permute-start.12) | collective-permute-done | bytes 65568 | tf_op jit(solution)/shard_map/ppermute | solution.py:178
  60.0 2.1 %collective-permute-start.14 = (bf16[16,2048]{1,0:T(8,128)(2,1)S(1)}, bf16[16,2048]{1,0:T(8,128)(2,1)S(1)}, u32[]{:S(2)}, u32[]{:S(2)}) collective-permute-start(bf16[16,2048]{1,0:T(8,128)(2,1)S(1)} %get-tuple-element.27), channel_id=1, source_target_pairs={{0,3},{1,2},{2,1},{3,0},{4,7},{5,6},{6,5},{7,4},{8,11},{9,10},{10,... | collective-permute-start | bytes 196616 | tf_op jit(solution)/shard_map/ppermute | solution.py:178
  62.1 2.3 %collective-permute-start.16 = (bf16[16,2048]{1,0:T(8,128)(2,1)S(1)}, bf16[16,2048]{1,0:T(8,128)(2,1)S(1)}, u32[]{:S(2)}, u32[]{:S(2)}) collective-permute-start(bf16[16,2048]{1,0:T(8,128)(2,1)S(1)} %get-tuple-element.29), channel_id=1, source_target_pairs={{0,1},{1,0},{2,3},{3,2},{4,5},{5,4},{6,7},{7,6},{8,9},{9,8},{10,11... | collective-permute-start | bytes 196616 | tf_op jit(solution)/shard_map/ppermute | solution.py:178
  64.4 2.8 %shard_map.96.rest_0_ = bf16[2048,512]{1,0:T(8,128)(2,1)} custom-call(f32[2]{0:T(128)S(1)} %copy-done.8, bf16[2048,512]{1,0:T(8,128)(2,1)S(1)} %copy-done.7, bf16[2048,512]{1,0:T(8,128)(2,1)S(1)} %copy-done.1, bf16[2048,512]{1,0:T(8,128)(2,1)S(1)} %copy-done.3, bf16[2,272,256]{2,1,0:T(8,128)(2,1)S(1)} %get-tuple-element.43.m_ref), custom_call_target="tpu_custom_call" | custom-call | flops 536870912 | bytes 2097152 | tf_op jit(solution)/shard_map/pallas_call | solution.py:124
  70.3 2.3 %collective-permute-start.17 = (bf16[16,2048]{1,0:T(8,128)(2,1)S(1)}, bf16[16,2048]{1,0:T(8,128)(2,1)S(1)}, u32[]{:S(2)}, u32[]{:S(2)}) collective-permute-start(bf16[16,2048]{1,0:T(8,128)(2,1)S(1)} %add_convert_fusion.1.refs_0_), channel_id=1, source_target_pairs={{0,1},{1,0},{2,3},{3,2},{4,5},{5,4},{6,7},{7,6},{8,9},{9,8},{10,11... | collective-permute-start | bytes 196616 | tf_op jit(solution)/shard_map/ppermute | solution.py:178
  72.6 3.7 %shard_map.97.rest_0_ = bf16[2048,512]{1,0:T(8,128)(2,1)} custom-call(f32[2]{0:T(128)S(1)} %copy-done.8, bf16[2048,512]{1,0:T(8,128)(2,1)S(1)} %copy-done.7, bf16[2048,512]{1,0:T(8,128)(2,1)S(1)} %copy-done.1, bf16[2048,512]{1,0:T(8,128)(2,1)S(1)} %copy-done.3, bf16[2,272,256]{2,1,0:T(8,128)(2,1)S(1)} %get-tuple-element.43.m_ref, ...), custom_call_target="tpu_custom_call", output_to_operand_aliasing={{}: (5, {})} | custom-call | flops 1073741824 | bytes 3145728 | tf_op jit(solution)/shard_map/pallas_call | solution.py:124
  78.2 2.1 %collective-permute-start.20 = (bf16[16,2048]{1,0:T(8,128)(2,1)S(1)}, bf16[16,2048]{1,0:T(8,128)(2,1)S(1)}, u32[]{:S(2)}, u32[]{:S(2)}) collective-permute-start(bf16[16,2048]{1,0:T(8,128)(2,1)S(1)} %get-tuple-element.31), channel_id=1, source_target_pairs={{0,3},{1,2},{2,1},{3,0},{4,7},{5,6},{6,5},{7,4},{8,11},{9,10},{10,... | collective-permute-start | bytes 196616 | tf_op jit(solution)/shard_map/ppermute | solution.py:178
  80.3 2.3 %collective-permute-start.22 = (bf16[16,2048]{1,0:T(8,128)(2,1)S(1)}, bf16[16,2048]{1,0:T(8,128)(2,1)S(1)}, u32[]{:S(2)}, u32[]{:S(2)}) collective-permute-start(bf16[16,2048]{1,0:T(8,128)(2,1)S(1)} %get-tuple-element.33), channel_id=1, source_target_pairs={{0,1},{1,0},{2,3},{3,2},{4,5},{5,4},{6,7},{7,6},{8,9},{9,8},{10,11... | collective-permute-start | bytes 196616 | tf_op jit(solution)/shard_map/ppermute | solution.py:178
  82.7 4.9 %shard_map.98.rest_0_ = bf16[2048,512]{1,0:T(8,128)(2,1)} custom-call(f32[2]{0:T(128)S(1)} %copy-done.8, bf16[2048,512]{1,0:T(8,128)(2,1)S(1)} %copy-done.7, bf16[2048,512]{1,0:T(8,128)(2,1)S(1)} %copy-done.1, bf16[2048,512]{1,0:T(8,128)(2,1)S(1)} %copy-done.3, bf16[2,272,256]{2,1,0:T(8,128)(2,1)S(1)} %get-tuple-element.43.m_ref, ...), custom_call_target="tpu_custom_call", output_to_operand_aliasing={{}: (5, {})} | custom-call | flops 1610612736 | bytes 4194304 | tf_op jit(solution)/shard_map/pallas_call | solution.py:124
  87.7 5.6 %shard_map.99 = bf16[2048,512]{1,0:T(8,128)(2,1)} custom-call(f32[2]{0:T(128)S(1)} %copy-done.8, bf16[2048,512]{1,0:T(8,128)(2,1)S(1)} %copy-done.7, bf16[2048,512]{1,0:T(8,128)(2,1)S(1)} %copy-done.1, bf16[2048,512]{1,0:T(8,128)(2,1)S(1)} %copy-done.3, bf16[2,272,256]{2,1,0:T(8,128)(2,1)S(1)} %get-tuple-element.43.m_ref, ...), custom_call_target="tpu_custom_call", output_to_operand_aliasing={{}: (5, {})} | custom-call | flops 2147483648 | bytes 5242880 | tf_op jit(solution)/shard_map/pallas_call | solution.py:124
  93.4 2.6 %collective-permute-start.24 = (bf16[16,2048]{1,0:T(8,128)(2,1)S(1)}, bf16[16,2048]{1,0:T(8,128)(2,1)S(1)}, u32[]{:S(2)}, u32[]{:S(2)}) collective-permute-start(bf16[16,2048]{1,0:T(8,128)(2,1)S(1)} %get-tuple-element.41), channel_id=1, source_target_pairs={{0,2},{1,3},{2,0},{3,1},{4,6},{5,7},{6,4},{7,5},{8,10},{9,11},{10,... | collective-permute-start | bytes 196616 | tf_op jit(solution)/shard_map/ppermute | solution.py:178
  98.6 3.5 %collective-permute-done.25 = bf16[16,2048]{1,0:T(8,128)(2,1)S(1)} collective-permute-done((bf16[16,2048]{1,0:T(8,128)(2,1)S(1)}, bf16[16,2048]{1,0:T(8,128)(2,1)S(1)}, u32[]{:S(2)}, u32[]{:S(2)}) %collective-permute-start.25) | collective-permute-done | bytes 65568 | tf_op jit(solution)/shard_map/ppermute | solution.py:178
  (76 shorter events, 29.6 us)
Async XLA Ops:
  8.0 9.9 %collective-permute-start.1 = (bf16[2,272,256]{2,1,0:T(8,128)(2,1)S(1)}, bf16[2,272,256]{2,1,0:T(8,128)(2,1)S(1)}, u32[]{:S(2)}, u32[]{:S(2)}) collective-permute-start(bf16[2,272,256]{2,1,0:T(8,128)(2,1)S(1)} %fusion.1), channel_id=1, source_target_pairs={{0,8},{4,12},{8,0},{12,4},{1,9},{5,13},{9,1},{13,5},{2,10},{6,14},... | collective-permute-start | bytes 835592 | tf_op jit(solution)/shard_map/ppermute | solution.py:178
  21.3 6.9 %collective-permute-start.2 = (bf16[16,2048]{1,0:T(8,128)(2,1)S(1)}, bf16[16,2048]{1,0:T(8,128)(2,1)S(1)}, u32[]{:S(2)}, u32[]{:S(2)}) collective-permute-start(bf16[16,2048]{1,0:T(8,128)(2,1)S(1)} %get-tuple-element.19), channel_id=1, source_target_pairs={{0,3},{1,2},{2,1},{3,0},{4,7},{5,6},{6,5},{7,4},{8,11},{9,10},{10,... | collective-permute-start | bytes 196616 | tf_op jit(solution)/shard_map/ppermute | solution.py:178
  25.2 5.3 %collective-permute-start.3 = (bf16[16,2048]{1,0:T(8,128)(2,1)S(1)}, bf16[16,2048]{1,0:T(8,128)(2,1)S(1)}, u32[]{:S(2)}, u32[]{:S(2)}) collective-permute-start(bf16[16,2048]{1,0:T(8,128)(2,1)S(1)} %get-tuple-element.20), channel_id=1, source_target_pairs={{0,2},{1,3},{2,0},{3,1},{4,6},{5,7},{6,4},{7,5},{8,10},{9,11},{10,... | collective-permute-start | bytes 196616 | tf_op jit(solution)/shard_map/ppermute | solution.py:178
  25.2 5.3 %collective-permute-start.4 = (bf16[16,2048]{1,0:T(8,128)(2,1)S(1)}, bf16[16,2048]{1,0:T(8,128)(2,1)S(1)}, u32[]{:S(2)}, u32[]{:S(2)}) collective-permute-start(bf16[16,2048]{1,0:T(8,128)(2,1)S(1)} %get-tuple-element.21), channel_id=1, source_target_pairs={{0,1},{1,0},{2,3},{3,2},{4,5},{5,4},{6,7},{7,6},{8,9},{9,8},{10,11... | collective-permute-start | bytes 196616 | tf_op jit(solution)/shard_map/ppermute | solution.py:178
  30.5 6.3 %collective-permute-start.7 = (bf16[16,2048]{1,0:T(8,128)(2,1)S(1)}, bf16[16,2048]{1,0:T(8,128)(2,1)S(1)}, u32[]{:S(2)}, u32[]{:S(2)}) collective-permute-start(bf16[16,2048]{1,0:T(8,128)(2,1)S(1)} %add_convert_fusion.3.refs_0_), channel_id=1, source_target_pairs={{0,3},{1,2},{2,1},{3,0},{4,7},{5,6},{6,5},{7,4},{8,11},{9,10},{10,... | collective-permute-start | bytes 196616 | tf_op jit(solution)/shard_map/ppermute | solution.py:178
  33.1 5.4 %collective-permute-start.6 = (bf16[16,2048]{1,0:T(8,128)(2,1)S(1)}, bf16[16,2048]{1,0:T(8,128)(2,1)S(1)}, u32[]{:S(2)}, u32[]{:S(2)}) collective-permute-start(bf16[16,2048]{1,0:T(8,128)(2,1)S(1)} %add_convert_fusion.3.refs_0_), channel_id=1, source_target_pairs={{0,2},{1,3},{2,0},{3,1},{4,6},{5,7},{6,4},{7,5},{8,10},{9,11},{10,... | collective-permute-start | bytes 196616 | tf_op jit(solution)/shard_map/ppermute | solution.py:178
  33.1 5.4 %collective-permute-start.5 = (bf16[16,2048]{1,0:T(8,128)(2,1)S(1)}, bf16[16,2048]{1,0:T(8,128)(2,1)S(1)}, u32[]{:S(2)}, u32[]{:S(2)}) collective-permute-start(bf16[16,2048]{1,0:T(8,128)(2,1)S(1)} %add_convert_fusion.3.refs_0_), channel_id=1, source_target_pairs={{0,1},{1,0},{2,3},{3,2},{4,5},{5,4},{6,7},{7,6},{8,9},{9,8},{10,11... | collective-permute-start | bytes 196616 | tf_op jit(solution)/shard_map/ppermute | solution.py:178
  39.9 6.1 %collective-permute-start.8 = (bf16[16,2048]{1,0:T(8,128)(2,1)S(1)}, bf16[16,2048]{1,0:T(8,128)(2,1)S(1)}, u32[]{:S(2)}, u32[]{:S(2)}) collective-permute-start(bf16[16,2048]{1,0:T(8,128)(2,1)S(1)} %get-tuple-element.23), channel_id=1, source_target_pairs={{0,3},{1,2},{2,1},{3,0},{4,7},{5,6},{6,5},{7,4},{8,11},{9,10},{10,... | collective-permute-start | bytes 196616 | tf_op jit(solution)/shard_map/ppermute | solution.py:178
  42.1 6.6 %collective-permute-start.9 = (bf16[16,2048]{1,0:T(8,128)(2,1)S(1)}, bf16[16,2048]{1,0:T(8,128)(2,1)S(1)}, u32[]{:S(2)}, u32[]{:S(2)}) collective-permute-start(bf16[16,2048]{1,0:T(8,128)(2,1)S(1)} %get-tuple-element.24), channel_id=1, source_target_pairs={{0,2},{1,3},{2,0},{3,1},{4,6},{5,7},{6,4},{7,5},{8,10},{9,11},{10,... | collective-permute-start | bytes 196616 | tf_op jit(solution)/shard_map/ppermute | solution.py:178
  42.3 6.4 %collective-permute-start.10 = (bf16[16,2048]{1,0:T(8,128)(2,1)S(1)}, bf16[16,2048]{1,0:T(8,128)(2,1)S(1)}, u32[]{:S(2)}, u32[]{:S(2)}) collective-permute-start(bf16[16,2048]{1,0:T(8,128)(2,1)S(1)} %get-tuple-element.25), channel_id=1, source_target_pairs={{0,1},{1,0},{2,3},{3,2},{4,5},{5,4},{6,7},{7,6},{8,9},{9,8},{10,11... | collective-permute-start | bytes 196616 | tf_op jit(solution)/shard_map/ppermute | solution.py:178
  48.8 6.2 %collective-permute-start.13 = (bf16[16,2048]{1,0:T(8,128)(2,1)S(1)}, bf16[16,2048]{1,0:T(8,128)(2,1)S(1)}, u32[]{:S(2)}, u32[]{:S(2)}) collective-permute-start(bf16[16,2048]{1,0:T(8,128)(2,1)S(1)} %add_convert_fusion.2.refs_0_), channel_id=1, source_target_pairs={{0,3},{1,2},{2,1},{3,0},{4,7},{5,6},{6,5},{7,4},{8,11},{9,10},{10,... | collective-permute-start | bytes 196616 | tf_op jit(solution)/shard_map/ppermute | solution.py:178
  50.9 7.6 %collective-permute-start.12 = (bf16[16,2048]{1,0:T(8,128)(2,1)S(1)}, bf16[16,2048]{1,0:T(8,128)(2,1)S(1)}, u32[]{:S(2)}, u32[]{:S(2)}) collective-permute-start(bf16[16,2048]{1,0:T(8,128)(2,1)S(1)} %add_convert_fusion.2.refs_0_), channel_id=1, source_target_pairs={{0,2},{1,3},{2,0},{3,1},{4,6},{5,7},{6,4},{7,5},{8,10},{9,11},{10,... | collective-permute-start | bytes 196616 | tf_op jit(solution)/shard_map/ppermute | solution.py:178
  50.9 7.6 %collective-permute-start.11 = (bf16[16,2048]{1,0:T(8,128)(2,1)S(1)}, bf16[16,2048]{1,0:T(8,128)(2,1)S(1)}, u32[]{:S(2)}, u32[]{:S(2)}) collective-permute-start(bf16[16,2048]{1,0:T(8,128)(2,1)S(1)} %add_convert_fusion.2.refs_0_), channel_id=1, source_target_pairs={{0,1},{1,0},{2,3},{3,2},{4,5},{5,4},{6,7},{7,6},{8,9},{9,8},{10,11... | collective-permute-start | bytes 196616 | tf_op jit(solution)/shard_map/ppermute | solution.py:178
  60.0 7.3 %collective-permute-start.14 = (bf16[16,2048]{1,0:T(8,128)(2,1)S(1)}, bf16[16,2048]{1,0:T(8,128)(2,1)S(1)}, u32[]{:S(2)}, u32[]{:S(2)}) collective-permute-start(bf16[16,2048]{1,0:T(8,128)(2,1)S(1)} %get-tuple-element.27), channel_id=1, source_target_pairs={{0,3},{1,2},{2,1},{3,0},{4,7},{5,6},{6,5},{7,4},{8,11},{9,10},{10,... | collective-permute-start | bytes 196616 | tf_op jit(solution)/shard_map/ppermute | solution.py:178
  62.1 5.9 %collective-permute-start.15 = (bf16[16,2048]{1,0:T(8,128)(2,1)S(1)}, bf16[16,2048]{1,0:T(8,128)(2,1)S(1)}, u32[]{:S(2)}, u32[]{:S(2)}) collective-permute-start(bf16[16,2048]{1,0:T(8,128)(2,1)S(1)} %get-tuple-element.28), channel_id=1, source_target_pairs={{0,2},{1,3},{2,0},{3,1},{4,6},{5,7},{6,4},{7,5},{8,10},{9,11},{10,... | collective-permute-start | bytes 196616 | tf_op jit(solution)/shard_map/ppermute | solution.py:178
  62.1 5.9 %collective-permute-start.16 = (bf16[16,2048]{1,0:T(8,128)(2,1)S(1)}, bf16[16,2048]{1,0:T(8,128)(2,1)S(1)}, u32[]{:S(2)}, u32[]{:S(2)}) collective-permute-start(bf16[16,2048]{1,0:T(8,128)(2,1)S(1)} %get-tuple-element.29), channel_id=1, source_target_pairs={{0,1},{1,0},{2,3},{3,2},{4,5},{5,4},{6,7},{7,6},{8,9},{9,8},{10,11... | collective-permute-start | bytes 196616 | tf_op jit(solution)/shard_map/ppermute | solution.py:178
  68.1 8.2 %collective-permute-start.19 = (bf16[16,2048]{1,0:T(8,128)(2,1)S(1)}, bf16[16,2048]{1,0:T(8,128)(2,1)S(1)}, u32[]{:S(2)}, u32[]{:S(2)}) collective-permute-start(bf16[16,2048]{1,0:T(8,128)(2,1)S(1)} %add_convert_fusion.1.refs_0_), channel_id=1, source_target_pairs={{0,3},{1,2},{2,1},{3,0},{4,7},{5,6},{6,5},{7,4},{8,11},{9,10},{10,... | collective-permute-start | bytes 196616 | tf_op jit(solution)/shard_map/ppermute | solution.py:178
  70.1 6.6 %collective-permute-start.18 = (bf16[16,2048]{1,0:T(8,128)(2,1)S(1)}, bf16[16,2048]{1,0:T(8,128)(2,1)S(1)}, u32[]{:S(2)}, u32[]{:S(2)}) collective-permute-start(bf16[16,2048]{1,0:T(8,128)(2,1)S(1)} %add_convert_fusion.1.refs_0_), channel_id=1, source_target_pairs={{0,2},{1,3},{2,0},{3,1},{4,6},{5,7},{6,4},{7,5},{8,10},{9,11},{10,... | collective-permute-start | bytes 196616 | tf_op jit(solution)/shard_map/ppermute | solution.py:178
  70.3 6.5 %collective-permute-start.17 = (bf16[16,2048]{1,0:T(8,128)(2,1)S(1)}, bf16[16,2048]{1,0:T(8,128)(2,1)S(1)}, u32[]{:S(2)}, u32[]{:S(2)}) collective-permute-start(bf16[16,2048]{1,0:T(8,128)(2,1)S(1)} %add_convert_fusion.1.refs_0_), channel_id=1, source_target_pairs={{0,1},{1,0},{2,3},{3,2},{4,5},{5,4},{6,7},{7,6},{8,9},{9,8},{10,11... | collective-permute-start | bytes 196616 | tf_op jit(solution)/shard_map/ppermute | solution.py:178
  78.2 9.3 %collective-permute-start.20 = (bf16[16,2048]{1,0:T(8,128)(2,1)S(1)}, bf16[16,2048]{1,0:T(8,128)(2,1)S(1)}, u32[]{:S(2)}, u32[]{:S(2)}) collective-permute-start(bf16[16,2048]{1,0:T(8,128)(2,1)S(1)} %get-tuple-element.31), channel_id=1, source_target_pairs={{0,3},{1,2},{2,1},{3,0},{4,7},{5,6},{6,5},{7,4},{8,11},{9,10},{10,... | collective-permute-start | bytes 196616 | tf_op jit(solution)/shard_map/ppermute | solution.py:178
  80.3 7.2 %collective-permute-start.21 = (bf16[16,2048]{1,0:T(8,128)(2,1)S(1)}, bf16[16,2048]{1,0:T(8,128)(2,1)S(1)}, u32[]{:S(2)}, u32[]{:S(2)}) collective-permute-start(bf16[16,2048]{1,0:T(8,128)(2,1)S(1)} %get-tuple-element.32), channel_id=1, source_target_pairs={{0,2},{1,3},{2,0},{3,1},{4,6},{5,7},{6,4},{7,5},{8,10},{9,11},{10,... | collective-permute-start | bytes 196616 | tf_op jit(solution)/shard_map/ppermute | solution.py:178
  80.3 7.2 %collective-permute-start.22 = (bf16[16,2048]{1,0:T(8,128)(2,1)S(1)}, bf16[16,2048]{1,0:T(8,128)(2,1)S(1)}, u32[]{:S(2)}, u32[]{:S(2)}) collective-permute-start(bf16[16,2048]{1,0:T(8,128)(2,1)S(1)} %get-tuple-element.33), channel_id=1, source_target_pairs={{0,1},{1,0},{2,3},{3,2},{4,5},{5,4},{6,7},{7,6},{8,9},{9,8},{10,11... | collective-permute-start | bytes 196616 | tf_op jit(solution)/shard_map/ppermute | solution.py:178
  87.7 10.1 %collective-permute-start.23 = (bf16[16,2048]{1,0:T(8,128)(2,1)S(1)}, bf16[16,2048]{1,0:T(8,128)(2,1)S(1)}, u32[]{:S(2)}, u32[]{:S(2)}) collective-permute-start(bf16[16,2048]{1,0:T(8,128)(2,1)S(1)} %get-tuple-element.41), channel_id=1, source_target_pairs={{0,1},{1,0},{2,3},{3,2},{4,5},{5,4},{6,7},{7,6},{8,9},{9,8},{10,11... | collective-permute-start | bytes 196616 | tf_op jit(solution)/shard_map/ppermute | solution.py:178
  96.0 6.1 %collective-permute-start.25 = (bf16[16,2048]{1,0:T(8,128)(2,1)S(1)}, bf16[16,2048]{1,0:T(8,128)(2,1)S(1)}, u32[]{:S(2)}, u32[]{:S(2)}) collective-permute-start(bf16[16,2048]{1,0:T(8,128)(2,1)S(1)} %get-tuple-element.41), channel_id=1, source_target_pairs={{0,3},{1,2},{2,1},{3,0},{4,7},{5,6},{6,5},{7,4},{8,11},{9,10},{10,... | collective-permute-start | bytes 196616 | tf_op jit(solution)/shard_map/ppermute | solution.py:178
  (14 other events, 116.1 us)

commit v2 on v1

--- a/solution.py
+++ b/solution.py
@@ -58,7 +58,7 @@
             pltpu.VMEM((heads, width, width), jnp.float32),
             pltpu.VMEM((heads, 8, width), jnp.float32),
         ],
-        compiler_params=pltpu.CompilerParams(vmem_limit_bytes=16 << 20),
+        compiler_params=pltpu.CompilerParams(vmem_limit_bytes=60 << 20),
         cost_estimate=pl.CostEstimate(
             flops=2 * rows * heads * width * width,
             transcendentals=rows * heads * width,
@@ -217,19 +217,27 @@
     ]
     attended = None
     chunk = 512
-    firsts = list(range(0, SEG, chunk))
+    waiting = list(range(0, SEG, chunk))
+
+    def fill(after, attended):
+        if not waiting:
+            return attended
+        tied, _ = lax.optimization_barrier((gate, after))
+        return attention_piece(queries, keys, values, prior, tied, attended, heads, width, waiting.pop(0), chunk)
+
     for step in range(STEPS):
         partial = summary_step(pieces, wq_sum, wo_sum, final, heads, width)
         got = [partner(partial[j], "sub", j) for j in range(parts - 1, 0, -1)]
-        if step < len(firsts):
-            attended = attention_piece(
-                queries, keys, values, prior, gate, attended, heads, width, firsts[step], chunk
-            )
+        attended = fill(partial[0], attended)
+        got, attended = lax.optimization_barrier((got, attended))
         new = pieces[0].astype(jnp.float32) + partial[0].astype(jnp.float32)
         for g in got:
             new = new + g.astype(jnp.float32)
         new = new.astype(jnp.bfloat16)
-        pieces = [new] + [partner(new, "sub", j) for j in range(parts - 1, 0, -1)][::-1]
+        got = [partner(new, "sub", j) for j in range(parts - 1, 0, -1)][::-1]
+        attended = fill(new, attended)
+        got, attended = lax.optimization_barrier((got, attended))
+        pieces = [new] + got
     out = jnp.zeros_like(summary)
     for j in range(parts):
         out = lax.dynamic_update_slice_in_dim(out, pieces[j], (me ^ j) * piece_rows, 0)

time: 103 us -> 102 us (level)
  Pallas kernels: 25.1 us -> 27.7 us
  waiting for transfers between devices: 31.1 us -> 28.8 us
  local copies, waits for them, and re-layouts: 5.57 us -> 3.97 us
    pallas_call x1, Pallas kernels: 2.18 us -> 4.89 us  [memory_update(): pl.pallas_call(functools.partial(update_kernel, heads, width), grid=(rows...]
    ppermute x26, waiting for transfers between devices: 31.1 us -> 28.8 us  [partner(): lax.ppermute(x, axis, [(i, i ^ flip) for i in range(lax.axis_size(axis))])]
    unnamed x24 -> x22, local copies, waits for them, and re-layouts: 5.5 us -> 3.9 us
  transfers between devices with their start and end apart: 26 -> 26, of which waited for: 14 -> 12; matrix products, arithmetic and copies ran while one was open for 0% -> 0% of each run, Pallas kernels for 17% -> 17%
where the time goes in v2:
time: 102 us
  starting transfers between devices  38.2 us (37%)
  waiting for transfers between devices  28.8 us (28%)
  Pallas kernels  27.7 us (27%)
  local copies, waits for them, and re-layouts  3.97 us (4%)
  other arithmetic  1.95 us (2%)
    ppermute x26, starting transfers between devices, partner(): lax.ppermute(x, axis, [(i, i ^ flip) for i in range(lax.axis_size(axis))])  38.2 us
    ppermute x26, waiting for transfers between devices, partner(): lax.ppermute(x, axis, [(i, i ^ flip) for i in range(lax.axis_size(axis))])  28.8 us
    pallas_call x4, Pallas kernels, attention_piece(): pl.pallas_call(functools.partial(attention_kernel, heads, width, first, 5...  17 us
    pallas_call x4, Pallas kernels, summary_step(): pl.pallas_call(functools.partial(step_kernel, heads, width, parts), in_sp...  5.87 us
    pallas_call x1, Pallas kernels, memory_update(): pl.pallas_call(functools.partial(update_kernel, heads, width), grid=(rows...  4.89 us
    unnamed x22, local copies, waits for them, and re-layouts  3.9 us
  transfers between devices with their start and end apart: 26, of which 12 were waited for; matrix products, arithmetic and copies ran while one was open for 0% of the time, Pallas kernels for 17%

profile of v2, /device:TPU:0, one launch (start us, length us, event | category | flops | bytes accessed | tf_op | source)
XLA Modules:
  0.0 101.6 jit_solution(3582847810679346177)
XLA Ops:
  0.6 4.9 %shard_map.95 = bf16[2,272,256]{2,1,0:T(8,128)(2,1)} custom-call(bf16[2048,512]{1,0:T(8,128)(2,1)} %k_ref.9, bf16[2048,512]{1,0:T(8,128)(2,1)} %v_ref.9), custom_call_target="tpu_custom_call" | custom-call | flops 536870912 | bytes 4194304 | tf_op jit(solution)/shard_map/pallas_call | solution.py:51
  8.6 2.9 %collective-permute-start.1 = (bf16[2,272,256]{2,1,0:T(8,128)(2,1)S(1)}, bf16[2,272,256]{2,1,0:T(8,128)(2,1)S(1)}, u32[]{:S(2)}, u32[]{:S(2)}) collective-permute-start(bf16[2,272,256]{2,1,0:T(8,128)(2,1)S(1)} %fusion.1), channel_id=1, source_target_pairs={{0,8},{4,12},{8,0},{12,4},{1,9},{5,13},{9,1},{13,5},{2,10},{6,14},... | collective-permute-start | bytes 835592 | tf_op jit(solution)/shard_map/ppermute | solution.py:178
  11.5 6.9 %collective-permute-done.1 = bf16[2,272,256]{2,1,0:T(8,128)(2,1)S(1)} collective-permute-done((bf16[2,272,256]{2,1,0:T(8,128)(2,1)S(1)}, bf16[2,272,256]{2,1,0:T(8,128)(2,1)S(1)}, u32[]{:S(2)}, u32[]{:S(2)}) %collective-permute-start.1) | collective-permute-done | bytes 278560 | tf_op jit(solution)/shard_map/ppermute | solution.py:178
  21.9 3.9 %collective-permute-start.2 = (bf16[16,2048]{1,0:T(8,128)(2,1)S(1)}, bf16[16,2048]{1,0:T(8,128)(2,1)S(1)}, u32[]{:S(2)}, u32[]{:S(2)}) collective-permute-start(bf16[16,2048]{1,0:T(8,128)(2,1)S(1)} %get-tuple-element.55), channel_id=1, source_target_pairs={{0,3},{1,2},{2,1},{3,0},{4,7},{5,6},{6,5},{7,4},{8,11},{9,10},{10,... | collective-permute-start | bytes 196616 | tf_op jit(solution)/shard_map/ppermute | solution.py:178
  28.1 2.8 %shard_map.97.rest_0_ = bf16[2048,512]{1,0:T(8,128)(2,1)} custom-call(f32[2]{0:T(128)S(1)} %copy-done.7, bf16[2048,512]{1,0:T(8,128)(2,1)S(1)} %copy-done.5, bf16[2048,512]{1,0:T(8,128)(2,1)S(1)} %copy-done, bf16[2048,512]{1,0:T(8,128)(2,1)S(1)} %copy-done.1, bf16[2,272,256]{2,1,0:T(8,128)(2,1)S(1)} %get-tuple-element.114.m_ref), custom_call_target="tpu_custom_call" | custom-call | flops 536870912 | bytes 2097152 | tf_op jit(solution)/shard_map/pallas_call | solution.py:124
  32.4 2.9 %collective-permute-start.6 = (bf16[16,2048]{1,0:T(8,128)(2,1)S(1)}, bf16[16,2048]{1,0:T(8,128)(2,1)S(1)}, u32[]{:S(2)}, u32[]{:S(2)}) collective-permute-start(bf16[16,2048]{1,0:T(8,128)(2,1)S(1)} %add_convert_fusion.3.refs_0_), channel_id=1, source_target_pairs={{0,2},{1,3},{2,0},{3,1},{4,6},{5,7},{6,4},{7,5},{8,10},{9,11},{10,... | collective-permute-start | bytes 196616 | tf_op jit(solution)/shard_map/ppermute | solution.py:178
  35.6 3.7 %shard_map.98.rest_0_ = bf16[2048,512]{1,0:T(8,128)(2,1)} custom-call(f32[2]{0:T(128)S(1)} %copy-done.7, bf16[2048,512]{1,0:T(8,128)(2,1)S(1)} %copy-done.6, bf16[2048,512]{1,0:T(8,128)(2,1)S(1)} %copy-done, bf16[2048,512]{1,0:T(8,128)(2,1)S(1)} %copy-done.1, bf16[2,272,256]{2,1,0:T(8,128)(2,1)S(1)} %get-tuple-element.114.m_ref, ...), custom_call_target="tpu_custom_call", output_to_operand_aliasing={{}: (5, {})} | custom-call | flops 1073741824 | bytes 3145728 | tf_op jit(solution)/shard_map/pallas_call | solution.py:124
  39.3 2.0 %collective-permute-done.7.refs_3_ = bf16[16,2048]{1,0:T(8,128)(2,1)S(1)} collective-permute-done((bf16[16,2048]{1,0:T(8,128)(2,1)S(1)}, bf16[16,2048]{1,0:T(8,128)(2,1)S(1)}, u32[]{:S(2)}, u32[]{:S(2)}) %collective-permute-start.7) | collective-permute-done | bytes 65568 | tf_op jit(solution)/shard_map/ppermute | solution.py:178
  42.9 1.8 %collective-permute-start.8 = (bf16[16,2048]{1,0:T(8,128)(2,1)S(1)}, bf16[16,2048]{1,0:T(8,128)(2,1)S(1)}, u32[]{:S(2)}, u32[]{:S(2)}) collective-permute-start(bf16[16,2048]{1,0:T(8,128)(2,1)S(1)} %get-tuple-element.68), channel_id=1, source_target_pairs={{0,3},{1,2},{2,1},{3,0},{4,7},{5,6},{6,5},{7,4},{8,11},{9,10},{10,... | collective-permute-start | bytes 196616 | tf_op jit(solution)/shard_map/ppermute | solution.py:178
  46.4 4.7 %shard_map.100.rest_0_ = bf16[2048,512]{1,0:T(8,128)(2,1)} custom-call(f32[2]{0:T(128)S(1)} %copy-done.7, bf16[2048,512]{1,0:T(8,128)(2,1)S(1)} %copy-done.6, bf16[2048,512]{1,0:T(8,128)(2,1)S(1)} %copy-done, bf16[2048,512]{1,0:T(8,128)(2,1)S(1)} %copy-done.1, bf16[2,272,256]{2,1,0:T(8,128)(2,1)S(1)} %get-tuple-element.114.m_ref, ...), custom_call_target="tpu_custom_call", output_to_operand_aliasing={{}: (5, {})} | custom-call | flops 1610612736 | bytes 4194304 | tf_op jit(solution)/shard_map/pallas_call | solution.py:124
  53.5 2.2 %collective-permute-start.13 = (bf16[16,2048]{1,0:T(8,128)(2,1)S(1)}, bf16[16,2048]{1,0:T(8,128)(2,1)S(1)}, u32[]{:S(2)}, u32[]{:S(2)}) collective-permute-start(bf16[16,2048]{1,0:T(8,128)(2,1)S(1)} %add_convert_fusion.2.refs_0_), channel_id=1, source_target_pairs={{0,3},{1,2},{2,1},{3,0},{4,7},{5,6},{6,5},{7,4},{8,11},{9,10},{10,... | collective-permute-start | bytes 196616 | tf_op jit(solution)/shard_map/ppermute | solution.py:178
  55.6 5.8 %shard_map.101 = bf16[2048,512]{1,0:T(8,128)(2,1)} custom-call(f32[2]{0:T(128)S(1)} %copy-done.7, bf16[2048,512]{1,0:T(8,128)(2,1)S(1)} %copy-done.6, bf16[2048,512]{1,0:T(8,128)(2,1)S(1)} %copy-done, bf16[2048,512]{1,0:T(8,128)(2,1)S(1)} %copy-done.1, bf16[2,272,256]{2,1,0:T(8,128)(2,1)S(1)} %get-tuple-element.114.m_ref, ...), custom_call_target="tpu_custom_call", output_to_operand_aliasing={{}: (5, {})} | custom-call | flops 2147483648 | bytes 5242880 | tf_op jit(solution)/shard_map/pallas_call | solution.py:124
  62.9 1.7 %collective-permute-start.14 = (bf16[16,2048]{1,0:T(8,128)(2,1)S(1)}, bf16[16,2048]{1,0:T(8,128)(2,1)S(1)}, u32[]{:S(2)}, u32[]{:S(2)}) collective-permute-start(bf16[16,2048]{1,0:T(8,128)(2,1)S(1)} %get-tuple-element.82), channel_id=1, source_target_pairs={{0,3},{1,2},{2,1},{3,0},{4,7},{5,6},{6,5},{7,4},{8,11},{9,10},{10,... | collective-permute-start | bytes 196616 | tf_op jit(solution)/shard_map/ppermute | solution.py:178
  64.6 2.7 %collective-permute-start.16 = (bf16[16,2048]{1,0:T(8,128)(2,1)S(1)}, bf16[16,2048]{1,0:T(8,128)(2,1)S(1)}, u32[]{:S(2)}, u32[]{:S(2)}) collective-permute-start(bf16[16,2048]{1,0:T(8,128)(2,1)S(1)} %get-tuple-element.84), channel_id=1, source_target_pairs={{0,1},{1,0},{2,3},{3,2},{4,5},{5,4},{6,7},{7,6},{8,9},{9,8},{10,11... | collective-permute-start | bytes 196616 | tf_op jit(solution)/shard_map/ppermute | solution.py:178
  67.4 2.2 %collective-permute-done.14 = bf16[16,2048]{1,0:T(8,128)(2,1)S(1)} collective-permute-done((bf16[16,2048]{1,0:T(8,128)(2,1)S(1)}, bf16[16,2048]{1,0:T(8,128)(2,1)S(1)}, u32[]{:S(2)}, u32[]{:S(2)}) %collective-permute-start.14) | collective-permute-done | bytes 65568 | tf_op jit(solution)/shard_map/ppermute | solution.py:178
  69.6 3.3 %collective-permute-done.15 = bf16[16,2048]{1,0:T(8,128)(2,1)S(1)} collective-permute-done((bf16[16,2048]{1,0:T(8,128)(2,1)S(1)}, bf16[16,2048]{1,0:T(8,128)(2,1)S(1)}, u32[]{:S(2)}, u32[]{:S(2)}) %collective-permute-start.15) | collective-permute-done | bytes 65568 | tf_op jit(solution)/shard_map/ppermute | solution.py:178
  73.1 2.5 %collective-permute-start.18 = (bf16[16,2048]{1,0:T(8,128)(2,1)S(1)}, bf16[16,2048]{1,0:T(8,128)(2,1)S(1)}, u32[]{:S(2)}, u32[]{:S(2)}) collective-permute-start(bf16[16,2048]{1,0:T(8,128)(2,1)S(1)} %add_convert_fusion.1.refs_0_), channel_id=1, source_target_pairs={{0,2},{1,3},{2,0},{3,1},{4,6},{5,7},{6,4},{7,5},{8,10},{9,11},{10,... | collective-permute-start | bytes 196616 | tf_op jit(solution)/shard_map/ppermute | solution.py:178
  75.5 1.9 %collective-permute-start.19 = (bf16[16,2048]{1,0:T(8,128)(2,1)S(1)}, bf16[16,2048]{1,0:T(8,128)(2,1)S(1)}, u32[]{:S(2)}, u32[]{:S(2)}) collective-permute-start(bf16[16,2048]{1,0:T(8,128)(2,1)S(1)} %add_convert_fusion.1.refs_0_), channel_id=1, source_target_pairs={{0,3},{1,2},{2,1},{3,0},{4,7},{5,6},{6,5},{7,4},{8,11},{9,10},{10,... | collective-permute-start | bytes 196616 | tf_op jit(solution)/shard_map/ppermute | solution.py:178
  77.4 3.5 %collective-permute-done.18.refs_2_ = bf16[16,2048]{1,0:T(8,128)(2,1)S(1)} collective-permute-done((bf16[16,2048]{1,0:T(8,128)(2,1)S(1)}, bf16[16,2048]{1,0:T(8,128)(2,1)S(1)}, u32[]{:S(2)}, u32[]{:S(2)}) %collective-permute-start.18) | collective-permute-done | bytes 65568 | tf_op jit(solution)/shard_map/ppermute | solution.py:178
  83.6 1.8 %collective-permute-start.20 = (bf16[16,2048]{1,0:T(8,128)(2,1)S(1)}, bf16[16,2048]{1,0:T(8,128)(2,1)S(1)}, u32[]{:S(2)}, u32[]{:S(2)}) collective-permute-start(bf16[16,2048]{1,0:T(8,128)(2,1)S(1)} %get-tuple-element.94), channel_id=1, source_target_pairs={{0,3},{1,2},{2,1},{3,0},{4,7},{5,6},{6,5},{7,4},{8,11},{9,10},{10,... | collective-permute-start | bytes 196616 | tf_op jit(solution)/shard_map/ppermute | solution.py:178
  88.0 2.5 %collective-permute-done.20 = bf16[16,2048]{1,0:T(8,128)(2,1)S(1)} collective-permute-done((bf16[16,2048]{1,0:T(8,128)(2,1)S(1)}, bf16[16,2048]{1,0:T(8,128)(2,1)S(1)}, u32[]{:S(2)}, u32[]{:S(2)}) %collective-permute-start.20) | collective-permute-done | bytes 65568 | tf_op jit(solution)/shard_map/ppermute | solution.py:178
  92.4 2.3 %collective-permute-start.24 = (bf16[16,2048]{1,0:T(8,128)(2,1)S(1)}, bf16[16,2048]{1,0:T(8,128)(2,1)S(1)}, u32[]{:S(2)}, u32[]{:S(2)}) collective-permute-start(bf16[16,2048]{1,0:T(8,128)(2,1)S(1)} %get-tuple-element.113), channel_id=1, source_target_pairs={{0,2},{1,3},{2,0},{3,1},{4,6},{5,7},{6,4},{7,5},{8,10},{9,11},{10,... | collective-permute-start | bytes 196616 | tf_op jit(solution)/shard_map/ppermute | solution.py:178
  94.7 1.9 %collective-permute-start.25 = (bf16[16,2048]{1,0:T(8,128)(2,1)S(1)}, bf16[16,2048]{1,0:T(8,128)(2,1)S(1)}, u32[]{:S(2)}, u32[]{:S(2)}) collective-permute-start(bf16[16,2048]{1,0:T(8,128)(2,1)S(1)} %get-tuple-element.113), channel_id=1, source_target_pairs={{0,3},{1,2},{2,1},{3,0},{4,7},{5,6},{6,5},{7,4},{8,11},{9,10},{10,... | collective-permute-start | bytes 196616 | tf_op jit(solution)/shard_map/ppermute | solution.py:178
  97.6 3.2 %collective-permute-done.25 = bf16[16,2048]{1,0:T(8,128)(2,1)S(1)} collective-permute-done((bf16[16,2048]{1,0:T(8,128)(2,1)S(1)}, bf16[16,2048]{1,0:T(8,128)(2,1)S(1)}, u32[]{:S(2)}, u32[]{:S(2)}) %collective-permute-start.25) | collective-permute-done | bytes 65568 | tf_op jit(solution)/shard_map/ppermute | solution.py:178
  (74 shorter events, 26.6 us)
Async XLA Ops:
  8.6 9.9 %collective-permute-start.1 = (bf16[2,272,256]{2,1,0:T(8,128)(2,1)S(1)}, bf16[2,272,256]{2,1,0:T(8,128)(2,1)S(1)}, u32[]{:S(2)}, u32[]{:S(2)}) collective-permute-start(bf16[2,272,256]{2,1,0:T(8,128)(2,1)S(1)} %fusion.1), channel_id=1, source_target_pairs={{0,8},{4,12},{8,0},{12,4},{1,9},{5,13},{9,1},{13,5},{2,10},{6,14},... | collective-permute-start | bytes 835592 | tf_op jit(solution)/shard_map/ppermute | solution.py:178
  21.9 9.0 %collective-permute-start.2 = (bf16[16,2048]{1,0:T(8,128)(2,1)S(1)}, bf16[16,2048]{1,0:T(8,128)(2,1)S(1)}, u32[]{:S(2)}, u32[]{:S(2)}) collective-permute-start(bf16[16,2048]{1,0:T(8,128)(2,1)S(1)} %get-tuple-element.55), channel_id=1, source_target_pairs={{0,3},{1,2},{2,1},{3,0},{4,7},{5,6},{6,5},{7,4},{8,11},{9,10},{10,... | collective-permute-start | bytes 196616 | tf_op jit(solution)/shard_map/ppermute | solution.py:178
  25.8 5.3 %collective-permute-start.3 = (bf16[16,2048]{1,0:T(8,128)(2,1)S(1)}, bf16[16,2048]{1,0:T(8,128)(2,1)S(1)}, u32[]{:S(2)}, u32[]{:S(2)}) collective-permute-start(bf16[16,2048]{1,0:T(8,128)(2,1)S(1)} %get-tuple-element.56), channel_id=1, source_target_pairs={{0,2},{1,3},{2,0},{3,1},{4,6},{5,7},{6,4},{7,5},{8,10},{9,11},{10,... | collective-permute-start | bytes 196616 | tf_op jit(solution)/shard_map/ppermute | solution.py:178
  25.8 5.3 %collective-permute-start.4 = (bf16[16,2048]{1,0:T(8,128)(2,1)S(1)}, bf16[16,2048]{1,0:T(8,128)(2,1)S(1)}, u32[]{:S(2)}, u32[]{:S(2)}) collective-permute-start(bf16[16,2048]{1,0:T(8,128)(2,1)S(1)} %get-tuple-element.57), channel_id=1, source_target_pairs={{0,1},{1,0},{2,3},{3,2},{4,5},{5,4},{6,7},{7,6},{8,9},{9,8},{10,11... | collective-permute-start | bytes 196616 | tf_op jit(solution)/shard_map/ppermute | solution.py:178
  31.2 8.2 %collective-permute-start.5 = (bf16[16,2048]{1,0:T(8,128)(2,1)S(1)}, bf16[16,2048]{1,0:T(8,128)(2,1)S(1)}, u32[]{:S(2)}, u32[]{:S(2)}) collective-permute-start(bf16[16,2048]{1,0:T(8,128)(2,1)S(1)} %add_convert_fusion.3.refs_0_), channel_id=1, source_target_pairs={{0,1},{1,0},{2,3},{3,2},{4,5},{5,4},{6,7},{7,6},{8,9},{9,8},{10,11... | collective-permute-start | bytes 196616 | tf_op jit(solution)/shard_map/ppermute | solution.py:178
  32.4 6.9 %collective-permute-start.6 = (bf16[16,2048]{1,0:T(8,128)(2,1)S(1)}, bf16[16,2048]{1,0:T(8,128)(2,1)S(1)}, u32[]{:S(2)}, u32[]{:S(2)}) collective-permute-start(bf16[16,2048]{1,0:T(8,128)(2,1)S(1)} %add_convert_fusion.3.refs_0_), channel_id=1, source_target_pairs={{0,2},{1,3},{2,0},{3,1},{4,6},{5,7},{6,4},{7,5},{8,10},{9,11},{10,... | collective-permute-start | bytes 196616 | tf_op jit(solution)/shard_map/ppermute | solution.py:178
  35.3 6.1 %collective-permute-start.7 = (bf16[16,2048]{1,0:T(8,128)(2,1)S(1)}, bf16[16,2048]{1,0:T(8,128)(2,1)S(1)}, u32[]{:S(2)}, u32[]{:S(2)}) collective-permute-start(bf16[16,2048]{1,0:T(8,128)(2,1)S(1)} %add_convert_fusion.3.refs_0_), channel_id=1, source_target_pairs={{0,3},{1,2},{2,1},{3,0},{4,7},{5,6},{6,5},{7,4},{8,11},{9,10},{10,... | collective-permute-start | bytes 196616 | tf_op jit(solution)/shard_map/ppermute | solution.py:178
  42.9 8.3 %collective-permute-start.10 = (bf16[16,2048]{1,0:T(8,128)(2,1)S(1)}, bf16[16,2048]{1,0:T(8,128)(2,1)S(1)}, u32[]{:S(2)}, u32[]{:S(2)}) collective-permute-start(bf16[16,2048]{1,0:T(8,128)(2,1)S(1)} %get-tuple-element.70), channel_id=1, source_target_pairs={{0,1},{1,0},{2,3},{3,2},{4,5},{5,4},{6,7},{7,6},{8,9},{9,8},{10,11... | collective-permute-start | bytes 196616 | tf_op jit(solution)/shard_map/ppermute | solution.py:178
  42.9 8.2 %collective-permute-start.8 = (bf16[16,2048]{1,0:T(8,128)(2,1)S(1)}, bf16[16,2048]{1,0:T(8,128)(2,1)S(1)}, u32[]{:S(2)}, u32[]{:S(2)}) collective-permute-start(bf16[16,2048]{1,0:T(8,128)(2,1)S(1)} %get-tuple-element.68), channel_id=1, source_target_pairs={{0,3},{1,2},{2,1},{3,0},{4,7},{5,6},{6,5},{7,4},{8,11},{9,10},{10,... | collective-permute-start | bytes 196616 | tf_op jit(solution)/shard_map/ppermute | solution.py:178
  44.8 6.3 %collective-permute-start.9 = (bf16[16,2048]{1,0:T(8,128)(2,1)S(1)}, bf16[16,2048]{1,0:T(8,128)(2,1)S(1)}, u32[]{:S(2)}, u32[]{:S(2)}) collective-permute-start(bf16[16,2048]{1,0:T(8,128)(2,1)S(1)} %get-tuple-element.69), channel_id=1, source_target_pairs={{0,2},{1,3},{2,0},{3,1},{4,6},{5,7},{6,4},{7,5},{8,10},{9,11},{10,... | collective-permute-start | bytes 196616 | tf_op jit(solution)/shard_map/ppermute | solution.py:178
  51.2 10.2 %collective-permute-start.11 = (bf16[16,2048]{1,0:T(8,128)(2,1)S(1)}, bf16[16,2048]{1,0:T(8,128)(2,1)S(1)}, u32[]{:S(2)}, u32[]{:S(2)}) collective-permute-start(bf16[16,2048]{1,0:T(8,128)(2,1)S(1)} %add_convert_fusion.2.refs_0_), channel_id=1, source_target_pairs={{0,1},{1,0},{2,3},{3,2},{4,5},{5,4},{6,7},{7,6},{8,9},{9,8},{10,11... | collective-permute-start | bytes 196616 | tf_op jit(solution)/shard_map/ppermute | solution.py:178
  52.2 9.2 %collective-permute-start.12 = (bf16[16,2048]{1,0:T(8,128)(2,1)S(1)}, bf16[16,2048]{1,0:T(8,128)(2,1)S(1)}, u32[]{:S(2)}, u32[]{:S(2)}) collective-permute-start(bf16[16,2048]{1,0:T(8,128)(2,1)S(1)} %add_convert_fusion.2.refs_0_), channel_id=1, source_target_pairs={{0,2},{1,3},{2,0},{3,1},{4,6},{5,7},{6,4},{7,5},{8,10},{9,11},{10,... | collective-permute-start | bytes 196616 | tf_op jit(solution)/shard_map/ppermute | solution.py:178
  53.5 8.0 %collective-permute-start.13 = (bf16[16,2048]{1,0:T(8,128)(2,1)S(1)}, bf16[16,2048]{1,0:T(8,128)(2,1)S(1)}, u32[]{:S(2)}, u32[]{:S(2)}) collective-permute-start(bf16[16,2048]{1,0:T(8,128)(2,1)S(1)} %add_convert_fusion.2.refs_0_), channel_id=1, source_target_pairs={{0,3},{1,2},{2,1},{3,0},{4,7},{5,6},{6,5},{7,4},{8,11},{9,10},{10,... | collective-permute-start | bytes 196616 | tf_op jit(solution)/shard_map/ppermute | solution.py:178
  62.9 6.7 %collective-permute-start.14 = (bf16[16,2048]{1,0:T(8,128)(2,1)S(1)}, bf16[16,2048]{1,0:T(8,128)(2,1)S(1)}, u32[]{:S(2)}, u32[]{:S(2)}) collective-permute-start(bf16[16,2048]{1,0:T(8,128)(2,1)S(1)} %get-tuple-element.82), channel_id=1, source_target_pairs={{0,3},{1,2},{2,1},{3,0},{4,7},{5,6},{6,5},{7,4},{8,11},{9,10},{10,... | collective-permute-start | bytes 196616 | tf_op jit(solution)/shard_map/ppermute | solution.py:178
  64.6 8.3 %collective-permute-start.15 = (bf16[16,2048]{1,0:T(8,128)(2,1)S(1)}, bf16[16,2048]{1,0:T(8,128)(2,1)S(1)}, u32[]{:S(2)}, u32[]{:S(2)}) collective-permute-start(bf16[16,2048]{1,0:T(8,128)(2,1)S(1)} %get-tuple-element.83), channel_id=1, source_target_pairs={{0,2},{1,3},{2,0},{3,1},{4,6},{5,7},{6,4},{7,5},{8,10},{9,11},{10,... | collective-permute-start | bytes 196616 | tf_op jit(solution)/shard_map/ppermute | solution.py:178
  64.6 8.3 %collective-permute-start.16 = (bf16[16,2048]{1,0:T(8,128)(2,1)S(1)}, bf16[16,2048]{1,0:T(8,128)(2,1)S(1)}, u32[]{:S(2)}, u32[]{:S(2)}) collective-permute-start(bf16[16,2048]{1,0:T(8,128)(2,1)S(1)} %get-tuple-element.84), channel_id=1, source_target_pairs={{0,1},{1,0},{2,3},{3,2},{4,5},{5,4},{6,7},{7,6},{8,9},{9,8},{10,11... | collective-permute-start | bytes 196616 | tf_op jit(solution)/shard_map/ppermute | solution.py:178
  73.0 4.5 %collective-permute-start.17 = (bf16[16,2048]{1,0:T(8,128)(2,1)S(1)}, bf16[16,2048]{1,0:T(8,128)(2,1)S(1)}, u32[]{:S(2)}, u32[]{:S(2)}) collective-permute-start(bf16[16,2048]{1,0:T(8,128)(2,1)S(1)} %add_convert_fusion.1.refs_0_), channel_id=1, source_target_pairs={{0,1},{1,0},{2,3},{3,2},{4,5},{5,4},{6,7},{7,6},{8,9},{9,8},{10,11... | collective-permute-start | bytes 196616 | tf_op jit(solution)/shard_map/ppermute | solution.py:178
  73.1 7.9 %collective-permute-start.18 = (bf16[16,2048]{1,0:T(8,128)(2,1)S(1)}, bf16[16,2048]{1,0:T(8,128)(2,1)S(1)}, u32[]{:S(2)}, u32[]{:S(2)}) collective-permute-start(bf16[16,2048]{1,0:T(8,128)(2,1)S(1)} %add_convert_fusion.1.refs_0_), channel_id=1, source_target_pairs={{0,2},{1,3},{2,0},{3,1},{4,6},{5,7},{6,4},{7,5},{8,10},{9,11},{10,... | collective-permute-start | bytes 196616 | tf_op jit(solution)/shard_map/ppermute | solution.py:178
  75.5 6.5 %collective-permute-start.19 = (bf16[16,2048]{1,0:T(8,128)(2,1)S(1)}, bf16[16,2048]{1,0:T(8,128)(2,1)S(1)}, u32[]{:S(2)}, u32[]{:S(2)}) collective-permute-start(bf16[16,2048]{1,0:T(8,128)(2,1)S(1)} %add_convert_fusion.1.refs_0_), channel_id=1, source_target_pairs={{0,3},{1,2},{2,1},{3,0},{4,7},{5,6},{6,5},{7,4},{8,11},{9,10},{10,... | collective-permute-start | bytes 196616 | tf_op jit(solution)/shard_map/ppermute | solution.py:178
  83.6 6.9 %collective-permute-start.20 = (bf16[16,2048]{1,0:T(8,128)(2,1)S(1)}, bf16[16,2048]{1,0:T(8,128)(2,1)S(1)}, u32[]{:S(2)}, u32[]{:S(2)}) collective-permute-start(bf16[16,2048]{1,0:T(8,128)(2,1)S(1)} %get-tuple-element.94), channel_id=1, source_target_pairs={{0,3},{1,2},{2,1},{3,0},{4,7},{5,6},{6,5},{7,4},{8,11},{9,10},{10,... | collective-permute-start | bytes 196616 | tf_op jit(solution)/shard_map/ppermute | solution.py:178
  85.4 6.7 %collective-permute-start.21 = (bf16[16,2048]{1,0:T(8,128)(2,1)S(1)}, bf16[16,2048]{1,0:T(8,128)(2,1)S(1)}, u32[]{:S(2)}, u32[]{:S(2)}) collective-permute-start(bf16[16,2048]{1,0:T(8,128)(2,1)S(1)} %get-tuple-element.95), channel_id=1, source_target_pairs={{0,2},{1,3},{2,0},{3,1},{4,6},{5,7},{6,4},{7,5},{8,10},{9,11},{10,... | collective-permute-start | bytes 196616 | tf_op jit(solution)/shard_map/ppermute | solution.py:178
  86.5 5.5 %collective-permute-start.22 = (bf16[16,2048]{1,0:T(8,128)(2,1)S(1)}, bf16[16,2048]{1,0:T(8,128)(2,1)S(1)}, u32[]{:S(2)}, u32[]{:S(2)}) collective-permute-start(bf16[16,2048]{1,0:T(8,128)(2,1)S(1)} %get-tuple-element.96), channel_id=1, source_target_pairs={{0,1},{1,0},{2,3},{3,2},{4,5},{5,4},{6,7},{7,6},{8,9},{9,8},{10,11... | collective-permute-start | bytes 196616 | tf_op jit(solution)/shard_map/ppermute | solution.py:178
  92.4 5.2 %collective-permute-start.24 = (bf16[16,2048]{1,0:T(8,128)(2,1)S(1)}, bf16[16,2048]{1,0:T(8,128)(2,1)S(1)}, u32[]{:S(2)}, u32[]{:S(2)}) collective-permute-start(bf16[16,2048]{1,0:T(8,128)(2,1)S(1)} %get-tuple-element.113), channel_id=1, source_target_pairs={{0,2},{1,3},{2,0},{3,1},{4,6},{5,7},{6,4},{7,5},{8,10},{9,11},{10,... | collective-permute-start | bytes 196616 | tf_op jit(solution)/shard_map/ppermute | solution.py:178
  94.7 6.1 %collective-permute-start.25 = (bf16[16,2048]{1,0:T(8,128)(2,1)S(1)}, bf16[16,2048]{1,0:T(8,128)(2,1)S(1)}, u32[]{:S(2)}, u32[]{:S(2)}) collective-permute-start(bf16[16,2048]{1,0:T(8,128)(2,1)S(1)} %get-tuple-element.113), channel_id=1, source_target_pairs={{0,3},{1,2},{2,1},{3,0},{4,7},{5,6},{6,5},{7,4},{8,11},{9,10},{10,... | collective-permute-start | bytes 196616 | tf_op jit(solution)/shard_map/ppermute | solution.py:178
  (13 other events, 75.7 us)

commit v3 on v1

--- a/solution.py
+++ b/solution.py
@@ -12,6 +12,8 @@
 EPS = 1e-06
 LOG2E = 1.4426950408889634
 PAD = 16
+QUERY_STAGES = (("book", 1), ("seq", 2), ("seq", 1))
+OUTPUT_STAGES = (("seq", 2), ("book", 1), ("seq", 1))
 
 
 def lift(x):
@@ -58,7 +60,7 @@
             pltpu.VMEM((heads, width, width), jnp.float32),
             pltpu.VMEM((heads, 8, width), jnp.float32),
         ],
-        compiler_params=pltpu.CompilerParams(vmem_limit_bytes=16 << 20),
+        compiler_params=pltpu.CompilerParams(vmem_limit_bytes=60 << 20),
         cost_estimate=pl.CostEstimate(
             flops=2 * rows * heads * width * width,
             transcendentals=rows * heads * width,
@@ -174,6 +176,59 @@
     )(*pieces, wq, wo, memory)
 
 
+def wide_kernel(heads, width, slices, place_ref, state_ref, wq_ref, wo_ref, m_ref, qa_ref, qb_ref, oa_ref, ob_ref, mx_ref, out_ref, acc):
+    group = heads * width
+    depth = state_ref.shape[1] // slices
+
+    def read(lifted, memory_ref, h):
+        numerator = dot(lifted, memory_ref[h, :width, :], ((1,), (0,)))
+        norm = memory_ref[h, width : width + 1, :].astype(jnp.float32)
+        denominator = jnp.sum(lifted.astype(jnp.float32) * norm, axis=1, keepdims=True) + 1.0
+        value = numerator / denominator
+        mean = jnp.mean(value * value, axis=1, keepdims=True)
+        return (value * lax.rsqrt(mean + EPS)).astype(jnp.bfloat16)
+
+    def reads(query, memory_ref):
+        lifted = lift(query).astype(jnp.bfloat16)
+        return jnp.concatenate(
+            [read(lifted[:, h * width : (h + 1) * width], memory_ref, h) for h in range(heads)], axis=1
+        )
+
+    own = reads(dot(state_ref[...], wq_ref[...], ((1,), (0,))), m_ref)
+    query = jnp.zeros((state_ref.shape[0], group), jnp.float32)
+    half = slices // 2
+    for j in range(slices):
+        block = qa_ref[j] if j < half else qb_ref[j - half]
+        at = pl.multiple_of((place_ref[0] ^ j) * depth, depth)
+        query += dot(state_ref[:, pl.ds(at, depth)], block, ((1,), (0,)))
+    other = reads(query, mx_ref)
+    acc[...] = dot(own, wo_ref[...], ((1,), (0,)))
+    for j in range(slices):
+        block = oa_ref[j] if j < half else ob_ref[j - half]
+        at = pl.multiple_of((place_ref[1] ^ j) * depth, depth)
+        acc[:, pl.ds(at, depth)] += dot(other, block, ((1,), (0,)))
+    out_ref[...] = acc[...].astype(jnp.bfloat16)
+
+
+def wide_step(place, state, wq, wo, memory, query_side, output_side, other_memory, heads, width):
+    rows, lanes = state.shape
+    slices = query_side[0].shape[0] * 2
+    vmem = pl.BlockSpec(memory_space=pltpu.VMEM)
+    return pl.pallas_call(
+        functools.partial(wide_kernel, heads, width, slices),
+        in_specs=[pl.BlockSpec(memory_space=pltpu.SMEM)] + [vmem] * 9,
+        out_specs=vmem,
+        out_shape=jax.ShapeDtypeStruct((rows, lanes), jnp.bfloat16),
+        scratch_shapes=[pltpu.VMEM((rows, lanes), jnp.float32)],
+        compiler_params=pltpu.CompilerParams(vmem_limit_bytes=24 << 20),
+        cost_estimate=pl.CostEstimate(
+            flops=4 * rows * (wq.size + wo.size),
+            transcendentals=2 * rows * heads * width,
+            bytes_accessed=4 * (wq.size + wo.size) + 4 * rows * lanes,
+        ),
+    )(place, state, wq, wo, memory, *query_side, *output_side, other_memory)
+
+
 def partner(x, axis, flip):
     return lax.ppermute(x, axis, [(i, i ^ flip) for i in range(lax.axis_size(axis))])
 
@@ -203,36 +258,99 @@
     return total, prior
 
 
+def import_slice(block, stages):
+    held = partner(block, "sub", 1)[None]
+    for axis, flip in stages[:-1]:
+        held = jnp.concatenate([held, partner(held, axis, flip)], axis=0)
+    return held, partner(held, *stages[-1])
+
+
+def slice_index(stages):
+    place = jnp.int32(0)
+    for k, (axis, flip) in enumerate(stages):
+        place += jnp.where((lax.axis_index(axis) & flip) != 0, 1 << k, 0).astype(jnp.int32)
+    return place
+
+
+def tree_sum(terms):
+    while len(terms) > 1:
+        terms = [terms[i] + terms[i + 1] for i in range(0, len(terms), 2)]
+    return terms[0]
+
+
+def wide_sum(terms):
+    return tree_sum([t.astype(jnp.float32) for t in terms])
+
+
 def on_device(queries, keys, values, decay, gate, summary, wq_sum, wo_sum):
     heads = gate.shape[0]
     width = queries.shape[1] // heads
+    model = summary.shape[1]
     parts, me = lax.axis_size("sub"), lax.axis_index("sub")
+    rows = summary.shape[0] // parts
+
+    query_stages = QUERY_STAGES
+    output_stages = OUTPUT_STAGES
+    depth = model >> len(query_stages)
+    query_place, output_place = slice_index(query_stages), slice_index(output_stages)
+    place = jnp.stack([query_place, output_place])
+    query_block = lax.dynamic_slice_in_dim(wq_sum, query_place * depth, depth, 0)
+    output_block = lax.dynamic_slice_in_dim(wo_sum, output_place * depth, depth, 1)
+
+    query_side = import_slice(query_block, query_stages)
+    output_side = import_slice(output_block, output_stages)
 
     own = memory_update(keys, values, heads, width)
     final, prior = scan_memory(own, decay, "seq")
-
-    piece_rows = summary.shape[0] // parts
-    pieces = [
-        lax.dynamic_slice_in_dim(summary, (me ^ j) * piece_rows, piece_rows, 0) for j in range(parts)
-    ]
+    other_final = partner(final, "sub", 1)
+
+    flips = [(k << 1) | (k.bit_count() & 1) for k in range(parts // 2)]
+    pieces = [lax.dynamic_slice_in_dim(summary, (me ^ j) * rows, rows, 0) for j in range(parts)]
+    chunk = 512
+    waiting = list(range(0, SEG, chunk))
     attended = None
-    chunk = 512
-    firsts = list(range(0, SEG, chunk))
-    for step in range(STEPS):
-        partial = summary_step(pieces, wq_sum, wo_sum, final, heads, width)
-        got = [partner(partial[j], "sub", j) for j in range(parts - 1, 0, -1)]
-        if step < len(firsts):
-            attended = attention_piece(
-                queries, keys, values, prior, gate, attended, heads, width, firsts[step], chunk
-            )
-        new = pieces[0].astype(jnp.float32) + partial[0].astype(jnp.float32)
-        for g in got:
-            new = new + g.astype(jnp.float32)
-        new = new.astype(jnp.bfloat16)
-        pieces = [new] + [partner(new, "sub", j) for j in range(parts - 1, 0, -1)][::-1]
+
+    def fill(after, attended, count=1):
+        for _ in range(count):
+            if waiting:
+                tied, _ = lax.optimization_barrier((gate, after))
+                attended = attention_piece(
+                    queries, keys, values, prior, tied, attended, heads, width, waiting.pop(0), chunk
+                )
+        return attended
+
+    def swap(array, flip):
+        order = [flips.index(f ^ flip) for f in flips]
+        return jnp.concatenate([array[k * rows : (k + 1) * rows] for k in order], axis=0)
+
+    state = jnp.concatenate([pieces[f] for f in flips], axis=0)
+    partial = summary_step(pieces, wq_sum, wo_sum, final, heads, width)
+    terms = [None] * parts
+    mine = jnp.concatenate([partial[f] for f in flips], axis=0)
+    for j in range(parts - 1, 0, -1):
+        sent = jnp.concatenate([partial[j ^ f] for f in flips], axis=0)
+        terms[j] = partner(sent, "sub", j)
+    attended = fill(partial[0], attended, 2)
+    terms[0] = mine
+    terms, attended = lax.optimization_barrier((terms, attended))
+    ordered = [terms[f] for f in flips] + [terms[f ^ 1] for f in flips]
+    state = (state.astype(jnp.float32) + wide_sum(ordered)).astype(jnp.bfloat16)
+
+    for step in range(1, STEPS):
+        partial = wide_step(
+            place, state, wq_sum, wo_sum, final, query_side, output_side, other_final, heads, width
+        )
+        terms = [partial] + [partner(partial, "sub", f) for f in flips[1:]]
+        attended = fill(partial, attended)
+        terms, attended = lax.optimization_barrier((terms, attended))
+        terms = [terms[0]] + [swap(t, f) for t, f in zip(terms[1:], flips[1:])]
+        state = (state.astype(jnp.float32) + wide_sum(terms)).astype(jnp.bfloat16)
+
+    other = partner(state, "sub", 1)
     out = jnp.zeros_like(summary)
-    for j in range(parts):
-        out = lax.dynamic_update_slice_in_dim(out, pieces[j], (me ^ j) * piece_rows, 0)
+    for k, f in enumerate(flips):
+        out = lax.dynamic_update_slice_in_dim(out, state[k * rows : (k + 1) * rows], (me ^ f) * rows, 0)
+        out = lax.dynamic_update_slice_in_dim(out, other[k * rows : (k + 1) * rows], (me ^ f ^ 1) * rows, 0)
     return (attended, out)
 
 

time: 103 us -> 104 us (level)
  starting transfers between devices: 39.2 us -> 23.3 us
  waiting for transfers between devices: 31.1 us -> 43.4 us
  Pallas kernels: 25.1 us -> 30.5 us
  local copies, waits for them, and re-layouts: 5.57 us -> 2.77 us
  other arithmetic: 1 us -> 2.42 us
    ppermute x26 -> x18, starting transfers between devices: 39.2 us -> 23.3 us  [partner(): lax.ppermute(x, axis, [(i, i ^ flip) for i in range(lax.axis_size(axis))])]
    ppermute x26 -> x18, waiting for transfers between devices: 31.1 us -> 43.4 us  [partner(): lax.ppermute(x, axis, [(i, i ^ flip) for i in range(lax.axis_size(axis))])]
    pallas_call x0 -> x3, Pallas kernels: none -> 7.26 us  [wide_step(): pl.pallas_call(functools.partial(wide_kernel, heads, width, slices), in_s...]
    unnamed x24 -> x16, local copies, waits for them, and re-layouts: 5.5 us -> 0.74 us
    pallas_call x4 -> x1, Pallas kernels: 5.87 us -> 1.47 us  [summary_step(): pl.pallas_call(functools.partial(step_kernel, heads, width, parts), in_sp...]
    pallas_call x1, Pallas kernels: 2.18 us -> 4.99 us  [memory_update(): pl.pallas_call(functools.partial(update_kernel, heads, width), grid=(rows...]
    dynamic_slice x1 -> x3, local copies, waits for them, and re-layouts: 0.02 us -> 1.94 us  [the longest x1 0.97 us: on_device(): lax.dynamic_slice_in_dim(wo_sum, output_place * depth, depth, 1)]
  transfers between devices with their start and end apart: 26 -> 18, of which waited for: 14 -> 9; matrix products, arithmetic and copies ran while one was open for 0% -> 4% of each run, Pallas kernels for 17% -> 18%
where the time goes in v3:
time: 104 us; the launch traced here: 103 us
  waiting for transfers between devices  43.4 us (42%)
  Pallas kernels  30.5 us (29%)
  starting transfers between devices  23.3 us (22%)
  local copies, waits for them, and re-layouts  2.77 us (3%)
  other arithmetic  2.42 us (2%)
    ppermute x18, waiting for transfers between devices, partner(): lax.ppermute(x, axis, [(i, i ^ flip) for i in range(lax.axis_size(axis))])  43.4 us
    ppermute x18, starting transfers between devices, partner(): lax.ppermute(x, axis, [(i, i ^ flip) for i in range(lax.axis_size(axis))])  23.3 us
    pallas_call x4, Pallas kernels, attention_piece(): pl.pallas_call(functools.partial(attention_kernel, heads, width, first, 5...  16.7 us
    pallas_call x3, Pallas kernels, wide_step(): pl.pallas_call(functools.partial(wide_kernel, heads, width, slices), in_s...  7.26 us
    pallas_call x1, Pallas kernels, memory_update(): pl.pallas_call(functools.partial(update_kernel, heads, width), grid=(rows...  4.99 us
  transfers between devices with their start and end apart: 18, of which 9 were waited for; matrix products, arithmetic and copies ran while one was open for 4% of the time, Pallas kernels for 18%

profile of v3, /device:TPU:0, one launch (start us, length us, event | category | flops | bytes accessed | tf_op | source)
XLA Modules:
  0.0 103.3 jit_solution(12517376385116998261)
XLA Ops:
  0.6 5.0 %shard_map.95 = bf16[2,272,256]{2,1,0:T(8,128)(2,1)} custom-call(bf16[2048,512]{1,0:T(8,128)(2,1)} %k_ref.9, bf16[2048,512]{1,0:T(8,128)(2,1)} %v_ref.9), custom_call_target="tpu_custom_call" | custom-call | flops 536870912 | bytes 4194304 | tf_op jit(solution)/shard_map/pallas_call | solution.py:53
  6.1 2.6 %collective-permute-start.5 = (bf16[256,512]{1,0:T(8,128)(2,1)S(1)}, bf16[256,512]{1,0:T(8,128)(2,1)S(1)}, u32[]{:S(2)}, u32[]{:S(2)}) collective-permute-start(bf16[256,512]{1,0:T(8,128)(2,1)S(1)} %constant_dynamic-slice_fusion.1), channel_id=1, source_target_pairs={{0,1},{1,0},{2,3},{3,2},{4,5},{5,4},{6,7},{7,6},{8,9},{9,8},{10,11... | collective-permute-start | bytes 786440 | tf_op jit(solution)/shard_map/ppermute | solution.py:233
  9.9 6.0 %collective-permute-done.5 = bf16[256,512]{1,0:T(8,128)(2,1)S(1)} collective-permute-done((bf16[256,512]{1,0:T(8,128)(2,1)S(1)}, bf16[256,512]{1,0:T(8,128)(2,1)S(1)}, u32[]{:S(2)}, u32[]{:S(2)}) %collective-permute-start.5) | collective-permute-done | bytes 262176 | tf_op jit(solution)/shard_map/ppermute | solution.py:233
  15.9 1.9 %collective-permute-start.6 = (bf16[1,256,512]{2,1,0:T(8,128)(2,1)S(1)}, bf16[1,256,512]{2,1,0:T(8,128)(2,1)S(1)}, u32[]{:S(2)}, u32[]{:S(2)}) collective-permute-start(bf16[1,256,512]{2,1,0:T(8,128)(2,1)S(1)} %bitcast.4), channel_id=1, source_target_pairs={{0,16},{16,0},{1,17},{17,1},{2,18},{18,2},{3,19},{19,3},{4,20},{20... | collective-permute-start | bytes 786440 | tf_op jit(solution)/shard_map/ppermute | solution.py:233
  18.0 3.3 %collective-permute-done.9 = bf16[512,256]{1,0:T(8,128)(2,1)S(1)} collective-permute-done((bf16[512,256]{1,0:T(8,128)(2,1)S(1)}, bf16[512,256]{1,0:T(8,128)(2,1)S(1)}, u32[]{:S(2)}, u32[]{:S(2)}) %collective-permute-start.9) | collective-permute-done | bytes 262176 | tf_op jit(solution)/shard_map/ppermute | solution.py:233
  24.7 1.7 %collective-permute-start.7 = (bf16[2,256,512]{2,1,0:T(8,128)(2,1)S(1)}, bf16[2,256,512]{2,1,0:T(8,128)(2,1)S(1)}, u32[]{:S(2)}, u32[]{:S(2)}) collective-permute-start(bf16[2,256,512]{2,1,0:T(8,128)(2,1)S(1)} %pad_maximum_fusion.2), channel_id=1, source_target_pairs={{0,8},{4,12},{8,0},{12,4},{1,9},{5,13},{9,1},{13,5},{2,10},{6,14},... | collective-permute-start | bytes 1572872 | tf_op jit(solution)/shard_map/ppermute | solution.py:233
  27.4 3.1 %collective-permute-done.10 = bf16[1,512,256]{2,1,0:T(8,128)(2,1)S(1)} collective-permute-done((bf16[1,512,256]{2,1,0:T(8,128)(2,1)S(1)}, bf16[1,512,256]{2,1,0:T(8,128)(2,1)S(1)}, u32[]{:S(2)}, u32[]{:S(2)}) %collective-permute-start.10) | collective-permute-done | bytes 262176 | tf_op jit(solution)/shard_map/ppermute | solution.py:233
  30.6 1.8 %collective-permute-start.11 = (bf16[2,512,256]{2,1,0:T(8,128)(2,1)S(1)}, bf16[2,512,256]{2,1,0:T(8,128)(2,1)S(1)}, u32[]{:S(2)}, u32[]{:S(2)}) collective-permute-start(bf16[2,512,256]{2,1,0:T(8,128)(2,1)S(1)} %pad_maximum_fusion.3), channel_id=1, source_target_pairs={{0,16},{16,0},{1,17},{17,1},{2,18},{18,2},{3,19},{19,3},{4,20},{20... | collective-permute-start | bytes 1572872 | tf_op jit(solution)/shard_map/ppermute | solution.py:233
  32.4 4.1 %collective-permute-done.1 = bf16[2,272,256]{2,1,0:T(8,128)(2,1)S(1)} collective-permute-done((bf16[2,272,256]{2,1,0:T(8,128)(2,1)S(1)}, bf16[2,272,256]{2,1,0:T(8,128)(2,1)S(1)}, u32[]{:S(2)}, u32[]{:S(2)}) %collective-permute-start.1) | collective-permute-done | bytes 278560 | tf_op jit(solution)/shard_map/ppermute | solution.py:233
  38.4 8.3 %collective-permute-done.7 = bf16[2,256,512]{2,1,0:T(8,128)(2,1)S(1)} collective-permute-done((bf16[2,256,512]{2,1,0:T(8,128)(2,1)S(1)}, bf16[2,256,512]{2,1,0:T(8,128)(2,1)S(1)}, u32[]{:S(2)}, u32[]{:S(2)}) %collective-permute-start.7) | collective-permute-done | bytes 524320 | tf_op jit(solution)/shard_map/ppermute | solution.py:233
  49.2 2.6 %collective-permute-start.3 = (bf16[32,2048]{1,0:T(8,128)(2,1)S(1)}, bf16[32,2048]{1,0:T(8,128)(2,1)S(1)}, u32[]{:S(2)}, u32[]{:S(2)}) collective-permute-start(bf16[32,2048]{1,0:T(8,128)(2,1)S(1)} %get-tuple-element.64), channel_id=1, source_target_pairs={{0,2},{1,3},{2,0},{3,1},{4,6},{5,7},{6,4},{7,5},{8,10},{9,11},{10,... | collective-permute-start | bytes 393224 | tf_op jit(solution)/shard_map/ppermute | solution.py:233
  52.1 2.8 %shard_map.97.rest_0_ = bf16[2048,512]{1,0:T(8,128)(2,1)} custom-call(f32[2]{0:T(128)S(1)} %copy-done.5, bf16[2048,512]{1,0:T(8,128)(2,1)S(1)} %copy-done.4, bf16[2048,512]{1,0:T(8,128)(2,1)S(1)} %copy-done, bf16[2048,512]{1,0:T(8,128)(2,1)S(1)} %copy-done.1, bf16[2,272,256]{2,1,0:T(8,128)(2,1)S(1)} %get-tuple-element.50.m_ref), custom_call_target="tpu_custom_call" | custom-call | flops 536870912 | bytes 2097152 | tf_op jit(solution)/shard_map/pallas_call | solution.py:126
  54.9 3.7 %shard_map.98.rest_0_ = bf16[2048,512]{1,0:T(8,128)(2,1)} custom-call(f32[2]{0:T(128)S(1)} %copy-done.5, bf16[2048,512]{1,0:T(8,128)(2,1)S(1)} %copy-done.4, bf16[2048,512]{1,0:T(8,128)(2,1)S(1)} %copy-done, bf16[2048,512]{1,0:T(8,128)(2,1)S(1)} %copy-done.1, bf16[2,272,256]{2,1,0:T(8,128)(2,1)S(1)} %get-tuple-element.50.m_ref, ...), custom_call_target="tpu_custom_call", output_to_operand_aliasing={{}: (5, {})} | custom-call | flops 1073741824 | bytes 3145728 | tf_op jit(solution)/shard_map/pallas_call | solution.py:126
  59.2 2.8 %collective-permute-done.3 = bf16[32,2048]{1,0:T(8,128)(2,1)S(1)} collective-permute-done((bf16[32,2048]{1,0:T(8,128)(2,1)S(1)}, bf16[32,2048]{1,0:T(8,128)(2,1)S(1)}, u32[]{:S(2)}, u32[]{:S(2)}) %collective-permute-start.3) | collective-permute-done | bytes 131104 | tf_op jit(solution)/shard_map/ppermute | solution.py:233
  62.2 5.2 %collective-permute-done.13.mx_ref = bf16[2,272,256]{2,1,0:T(8,128)(2,1)S(1)} collective-permute-done((bf16[2,272,256]{2,1,0:T(8,128)(2,1)S(1)}, bf16[2,272,256]{2,1,0:T(8,128)(2,1)S(1)}, u32[]{:S(2)}, u32[]{:S(2)}) %collective-permute-start.13) | collective-permute-done | bytes 278560 | tf_op jit(solution)/shard_map/ppermute | solution.py:233
  67.4 2.4 %shard_map.99 = bf16[32,2048]{1,0:T(8,128)(2,1)S(1)} custom-call(s32[2]{0:T(128)S(1)} %pad_add_fusion.place_ref, bf16[32,2048]{1,0:T(8,128)(2,1)S(1)} %add_convert_fusion.3.state_ref, bf16[2048,512]{1,0:T(8,128)(2,1)S(1)} %copy-done.2, bf16[512,2048]{1,0:T(8,128)(2,1)S(1)} %copy-done.3, bf16[2,272,256]{2,1,0:T(8,128)(2,1)S(1)} %get-tuple-element.51.refs_6_.m_ref, ...), custom_call_target="tpu_custom_call" | custom-call | flops 268435456 | bytes 8650752 | tf_op jit(solution)/shard_map/pallas_call | solution.py:217
  69.8 2.8 %collective-permute-start.14 = (bf16[32,2048]{1,0:T(8,128)(2,1)S(1)}, bf16[32,2048]{1,0:T(8,128)(2,1)S(1)}, u32[]{:S(2)}, u32[]{:S(2)}) collective-permute-start(bf16[32,2048]{1,0:T(8,128)(2,1)S(1)} %shard_map.99), channel_id=1, source_target_pairs={{0,3},{1,2},{2,1},{3,0},{4,7},{5,6},{6,5},{7,4},{8,11},{9,10},{10,... | collective-permute-start | bytes 393224 | tf_op jit(solution)/shard_map/ppermute | solution.py:233
  72.6 4.7 %shard_map.100.rest_0_ = bf16[2048,512]{1,0:T(8,128)(2,1)} custom-call(f32[2]{0:T(128)S(1)} %copy-done.5, bf16[2048,512]{1,0:T(8,128)(2,1)S(1)} %copy-done.4, bf16[2048,512]{1,0:T(8,128)(2,1)S(1)} %copy-done, bf16[2048,512]{1,0:T(8,128)(2,1)S(1)} %copy-done.1, bf16[2,272,256]{2,1,0:T(8,128)(2,1)S(1)} %get-tuple-element.50.m_ref, ...), custom_call_target="tpu_custom_call", output_to_operand_aliasing={{}: (5, {})} | custom-call | flops 1610612736 | bytes 4194304 | tf_op jit(solution)/shard_map/pallas_call | solution.py:126
  77.4 2.5 %shard_map.101 = bf16[32,2048]{1,0:T(8,128)(2,1)S(1)} custom-call(s32[2]{0:T(128)S(1)} %pad_add_fusion.place_ref, bf16[32,2048]{1,0:T(8,128)(2,1)S(1)} %add_convert_fusion.2.state_ref, bf16[2048,512]{1,0:T(8,128)(2,1)S(1)} %copy-done.2, bf16[512,2048]{1,0:T(8,128)(2,1)S(1)} %copy-done.3, bf16[2,272,256]{2,1,0:T(8,128)(2,1)S(1)} %get-tuple-element.51.refs_6_.m_ref, ...), custom_call_target="tpu_custom_call" | custom-call | flops 268435456 | bytes 8650752 | tf_op jit(solution)/shard_map/pallas_call | solution.py:217
  79.9 2.2 %collective-permute-start.15 = (bf16[32,2048]{1,0:T(8,128)(2,1)S(1)}, bf16[32,2048]{1,0:T(8,128)(2,1)S(1)}, u32[]{:S(2)}, u32[]{:S(2)}) collective-permute-start(bf16[32,2048]{1,0:T(8,128)(2,1)S(1)} %shard_map.101), channel_id=1, source_target_pairs={{0,3},{1,2},{2,1},{3,0},{4,7},{5,6},{6,5},{7,4},{8,11},{9,10},{10,... | collective-permute-start | bytes 393224 | tf_op jit(solution)/shard_map/ppermute | solution.py:233
  82.2 5.6 %shard_map.102 = bf16[2048,512]{1,0:T(8,128)(2,1)} custom-call(f32[2]{0:T(128)S(1)} %copy-done.5, bf16[2048,512]{1,0:T(8,128)(2,1)S(1)} %copy-done.4, bf16[2048,512]{1,0:T(8,128)(2,1)S(1)} %copy-done, bf16[2048,512]{1,0:T(8,128)(2,1)S(1)} %copy-done.1, bf16[2,272,256]{2,1,0:T(8,128)(2,1)S(1)} %get-tuple-element.50.m_ref, ...), custom_call_target="tpu_custom_call", output_to_operand_aliasing={{}: (5, {})} | custom-call | flops 2147483648 | bytes 5242880 | tf_op jit(solution)/shard_map/pallas_call | solution.py:126
  87.8 2.4 %shard_map.103 = bf16[32,2048]{1,0:T(8,128)(2,1)S(1)} custom-call(s32[2]{0:T(128)S(1)} %pad_add_fusion.place_ref, bf16[32,2048]{1,0:T(8,128)(2,1)S(1)} %add_convert_fusion.1.state_ref, bf16[2048,512]{1,0:T(8,128)(2,1)S(1)} %copy-done.2, bf16[512,2048]{1,0:T(8,128)(2,1)S(1)} %copy-done.3, bf16[2,272,256]{2,1,0:T(8,128)(2,1)S(1)} %get-tuple-element.51.refs_6_.m_ref, ...), custom_call_target="tpu_custom_call" | custom-call | flops 268435456 | bytes 8650752 | tf_op jit(solution)/shard_map/pallas_call | solution.py:217
  91.9 5.6 %collective-permute-done.16 = bf16[32,2048]{1,0:T(8,128)(2,1)S(1)} collective-permute-done((bf16[32,2048]{1,0:T(8,128)(2,1)S(1)}, bf16[32,2048]{1,0:T(8,128)(2,1)S(1)}, u32[]{:S(2)}, u32[]{:S(2)}) %collective-permute-start.16) | collective-permute-done | bytes 131104 | tf_op jit(solution)/shard_map/ppermute | solution.py:233
  97.7 4.9 %collective-permute-done.17 = bf16[32,2048]{1,0:T(8,128)(2,1)S(1)} collective-permute-done((bf16[32,2048]{1,0:T(8,128)(2,1)S(1)}, bf16[32,2048]{1,0:T(8,128)(2,1)S(1)}, u32[]{:S(2)}, u32[]{:S(2)}) %collective-permute-start.17) | collective-permute-done | bytes 131104 | tf_op jit(solution)/shard_map/ppermute | solution.py:233
  (65 shorter events, 14.3 us)
Async XLA Ops:
  0.6 17.2 %copy-start.7 = (f32[4,2]{0,1:T(2,128)S(1)}, f32[4,2]{0,1:T(2,128)}, u32[]{:S(2)}) copy-start(f32[4,2]{0,1:T(2,128)} %param.11) | copy-start | bytes 100
  5.6 17.4 %collective-permute-start = (bf16[2,272,256]{2,1,0:T(8,128)(2,1)}, bf16[2,272,256]{2,1,0:T(8,128)(2,1)S(1)}, u32[]{:S(2)}, u32[]{:S(2)}) collective-permute-start(bf16[2,272,256]{2,1,0:T(8,128)(2,1)} %shard_map.95), channel_id=1, source_target_pairs={{0,4},{4,0},{8,12},{12,8},{1,5},{5,1},{9,13},{13,9},{2,6},{6,2},{1... | collective-permute-start | bytes 835592 | tf_op jit(solution)/shard_map/ppermute | solution.py:233
  6.1 9.8 %collective-permute-start.5 = (bf16[256,512]{1,0:T(8,128)(2,1)S(1)}, bf16[256,512]{1,0:T(8,128)(2,1)S(1)}, u32[]{:S(2)}, u32[]{:S(2)}) collective-permute-start(bf16[256,512]{1,0:T(8,128)(2,1)S(1)} %constant_dynamic-slice_fusion.1), channel_id=1, source_target_pairs={{0,1},{1,0},{2,3},{3,2},{4,5},{5,4},{6,7},{7,6},{8,9},{9,8},{10,11... | collective-permute-start | bytes 786440 | tf_op jit(solution)/shard_map/ppermute | solution.py:233
  9.7 11.6 %collective-permute-start.9 = (bf16[512,256]{1,0:T(8,128)(2,1)S(1)}, bf16[512,256]{1,0:T(8,128)(2,1)S(1)}, u32[]{:S(2)}, u32[]{:S(2)}) collective-permute-start(bf16[512,256]{1,0:T(8,128)(2,1)S(1)} %constant_dynamic-slice_fusion), channel_id=1, source_target_pairs={{0,1},{1,0},{2,3},{3,2},{4,5},{5,4},{6,7},{7,6},{8,9},{9,8},{10,11... | collective-permute-start | bytes 786440 | tf_op jit(solution)/shard_map/ppermute | solution.py:233
  15.9 8.7 %collective-permute-start.6 = (bf16[1,256,512]{2,1,0:T(8,128)(2,1)S(1)}, bf16[1,256,512]{2,1,0:T(8,128)(2,1)S(1)}, u32[]{:S(2)}, u32[]{:S(2)}) collective-permute-start(bf16[1,256,512]{2,1,0:T(8,128)(2,1)S(1)} %bitcast.4), channel_id=1, source_target_pairs={{0,16},{16,0},{1,17},{17,1},{2,18},{18,2},{3,19},{19,3},{4,20},{20... | collective-permute-start | bytes 786440 | tf_op jit(solution)/shard_map/ppermute | solution.py:233
  21.4 9.2 %collective-permute-start.10 = (bf16[1,512,256]{2,1,0:T(8,128)(2,1)S(1)}, bf16[1,512,256]{2,1,0:T(8,128)(2,1)S(1)}, u32[]{:S(2)}, u32[]{:S(2)}) collective-permute-start(bf16[1,512,256]{2,1,0:T(8,128)(2,1)S(1)} %bitcast.7), channel_id=1, source_target_pairs={{0,8},{4,12},{8,0},{12,4},{1,9},{5,13},{9,1},{13,5},{2,10},{6,14},... | collective-permute-start | bytes 786440 | tf_op jit(solution)/shard_map/ppermute | solution.py:233
  24.2 12.6 %copy-start.3 = (bf16[512,2048]{1,0:T(8,128)(2,1)S(1)}, bf16[512,2048]{1,0:T(8,128)(2,1)}, u32[]{:S(2)}) copy-start(bf16[512,2048]{1,0:T(8,128)(2,1)} %wo_ref.5) | copy-start | bytes 6291460
  24.2 12.3 %collective-permute-start.1 = (bf16[2,272,256]{2,1,0:T(8,128)(2,1)S(1)}, bf16[2,272,256]{2,1,0:T(8,128)(2,1)S(1)}, u32[]{:S(2)}, u32[]{:S(2)}) collective-permute-start(bf16[2,272,256]{2,1,0:T(8,128)(2,1)S(1)} %fusion.1), channel_id=1, source_target_pairs={{0,8},{4,12},{8,0},{12,4},{1,9},{5,13},{9,1},{13,5},{2,10},{6,14},... | collective-permute-start | bytes 835592 | tf_op jit(solution)/shard_map/ppermute | solution.py:233
  24.7 22.0 %collective-permute-start.7 = (bf16[2,256,512]{2,1,0:T(8,128)(2,1)S(1)}, bf16[2,256,512]{2,1,0:T(8,128)(2,1)S(1)}, u32[]{:S(2)}, u32[]{:S(2)}) collective-permute-start(bf16[2,256,512]{2,1,0:T(8,128)(2,1)S(1)} %pad_maximum_fusion.2), channel_id=1, source_target_pairs={{0,8},{4,12},{8,0},{12,4},{1,9},{5,13},{9,1},{13,5},{2,10},{6,14},... | collective-permute-start | bytes 1572872 | tf_op jit(solution)/shard_map/ppermute | solution.py:233
  30.6 16.3 %collective-permute-start.11 = (bf16[2,512,256]{2,1,0:T(8,128)(2,1)S(1)}, bf16[2,512,256]{2,1,0:T(8,128)(2,1)S(1)}, u32[]{:S(2)}, u32[]{:S(2)}) collective-permute-start(bf16[2,512,256]{2,1,0:T(8,128)(2,1)S(1)} %pad_maximum_fusion.3), channel_id=1, source_target_pairs={{0,16},{16,0},{1,17},{17,1},{2,18},{18,2},{3,19},{19,3},{4,20},{20... | collective-permute-start | bytes 1572872 | tf_op jit(solution)/shard_map/ppermute | solution.py:233
  36.9 15.2 %copy-start.4 = (bf16[2048,512]{1,0:T(8,128)(2,1)S(1)}, bf16[2048,512]{1,0:T(8,128)(2,1)}, u32[]{:S(2)}) copy-start(bf16[2048,512]{1,0:T(8,128)(2,1)} %q_ref.7) | copy-start | bytes 6291460
  38.3 13.8 %copy-start = (bf16[2048,512]{1,0:T(8,128)(2,1)S(1)}, bf16[2048,512]{1,0:T(8,128)(2,1)}, u32[]{:S(2)}) copy-start(bf16[2048,512]{1,0:T(8,128)(2,1)} %k_ref.9) | copy-start | bytes 6291460
  38.4 13.8 %copy-start.1 = (bf16[2048,512]{1,0:T(8,128)(2,1)S(1)}, bf16[2048,512]{1,0:T(8,128)(2,1)}, u32[]{:S(2)}) copy-start(bf16[2048,512]{1,0:T(8,128)(2,1)} %v_ref.9) | copy-start | bytes 6291460
  38.4 13.8 %copy-start.5 = (f32[2]{0:T(128)S(1)}, f32[2]{0:T(128)}, u32[]{:S(2)}) copy-start(f32[2]{0:T(128)} %gate_ref.3) | copy-start | bytes 28
  46.8 20.6 %collective-permute-start.8 = (bf16[4,256,512]{2,1,0:T(8,128)(2,1)S(1)}, bf16[4,256,512]{2,1,0:T(8,128)(2,1)S(1)}, u32[]{:S(2)}, u32[]{:S(2)}) collective-permute-start(bf16[4,256,512]{2,1,0:T(8,128)(2,1)S(1)} %pad_maximum_fusion.qa_ref), channel_id=1, source_target_pairs={{0,4},{4,0},{8,12},{12,8},{1,5},{5,1},{9,13},{13,9},{2,6},{6,2},{1... | collective-permute-start | bytes 3145736 | tf_op jit(solution)/shard_map/ppermute | solution.py:233
  47.0 20.4 %collective-permute-start.12 = (bf16[4,512,256]{2,1,0:T(8,128)(2,1)S(1)}, bf16[4,512,256]{2,1,0:T(8,128)(2,1)S(1)}, u32[]{:S(2)}, u32[]{:S(2)}) collective-permute-start(bf16[4,512,256]{2,1,0:T(8,128)(2,1)S(1)} %pad_maximum_fusion.1.oa_ref), channel_id=1, source_target_pairs={{0,4},{4,0},{8,12},{12,8},{1,5},{5,1},{9,13},{13,9},{2,6},{6,2},{1... | collective-permute-start | bytes 3145736 | tf_op jit(solution)/shard_map/ppermute | solution.py:233
  47.6 11.0 %collective-permute-start.2 = (bf16[32,2048]{1,0:T(8,128)(2,1)S(1)}, bf16[32,2048]{1,0:T(8,128)(2,1)S(1)}, u32[]{:S(2)}, u32[]{:S(2)}) collective-permute-start(bf16[32,2048]{1,0:T(8,128)(2,1)S(1)} %get-tuple-element.65), channel_id=1, source_target_pairs={{0,1},{1,0},{2,3},{3,2},{4,5},{5,4},{6,7},{7,6},{8,9},{9,8},{10,11... | collective-permute-start | bytes 393224 | tf_op jit(solution)/shard_map/ppermute | solution.py:233
  49.2 12.9 %collective-permute-start.3 = (bf16[32,2048]{1,0:T(8,128)(2,1)S(1)}, bf16[32,2048]{1,0:T(8,128)(2,1)S(1)}, u32[]{:S(2)}, u32[]{:S(2)}) collective-permute-start(bf16[32,2048]{1,0:T(8,128)(2,1)S(1)} %get-tuple-element.64), channel_id=1, source_target_pairs={{0,2},{1,3},{2,0},{3,1},{4,6},{5,7},{6,4},{7,5},{8,10},{9,11},{10,... | collective-permute-start | bytes 393224 | tf_op jit(solution)/shard_map/ppermute | solution.py:233
  51.8 10.3 %collective-permute-start.4 = (bf16[32,2048]{1,0:T(8,128)(2,1)S(1)}, bf16[32,2048]{1,0:T(8,128)(2,1)S(1)}, u32[]{:S(2)}, u32[]{:S(2)}) collective-permute-start(bf16[32,2048]{1,0:T(8,128)(2,1)S(1)} %get-tuple-element.62), channel_id=1, source_target_pairs={{0,3},{1,2},{2,1},{3,0},{4,7},{5,6},{6,5},{7,4},{8,11},{9,10},{10,... | collective-permute-start | bytes 393224 | tf_op jit(solution)/shard_map/ppermute | solution.py:233
  58.6 8.8 %collective-permute-start.13 = (bf16[2,272,256]{2,1,0:T(8,128)(2,1)S(1)}, bf16[2,272,256]{2,1,0:T(8,128)(2,1)S(1)}, u32[]{:S(2)}, u32[]{:S(2)}) collective-permute-start(bf16[2,272,256]{2,1,0:T(8,128)(2,1)S(1)} %get-tuple-element.51.refs_6_.m_ref), channel_id=1, source_target_pairs={{0,1},{1,0},{2,3},{3,2},{4,5},{5,4},{6,7},{7,6},{8,9},{9,8},{10,11... | collective-permute-start | bytes 835592 | tf_op jit(solution)/shard_map/ppermute | solution.py:233
  69.8 7.5 %collective-permute-start.14 = (bf16[32,2048]{1,0:T(8,128)(2,1)S(1)}, bf16[32,2048]{1,0:T(8,128)(2,1)S(1)}, u32[]{:S(2)}, u32[]{:S(2)}) collective-permute-start(bf16[32,2048]{1,0:T(8,128)(2,1)S(1)} %shard_map.99), channel_id=1, source_target_pairs={{0,3},{1,2},{2,1},{3,0},{4,7},{5,6},{6,5},{7,4},{8,11},{9,10},{10,... | collective-permute-start | bytes 393224 | tf_op jit(solution)/shard_map/ppermute | solution.py:233
  79.9 7.8 %collective-permute-start.15 = (bf16[32,2048]{1,0:T(8,128)(2,1)S(1)}, bf16[32,2048]{1,0:T(8,128)(2,1)S(1)}, u32[]{:S(2)}, u32[]{:S(2)}) collective-permute-start(bf16[32,2048]{1,0:T(8,128)(2,1)S(1)} %shard_map.101), channel_id=1, source_target_pairs={{0,3},{1,2},{2,1},{3,0},{4,7},{5,6},{6,5},{7,4},{8,11},{9,10},{10,... | collective-permute-start | bytes 393224 | tf_op jit(solution)/shard_map/ppermute | solution.py:233
  90.2 7.3 %collective-permute-start.16 = (bf16[32,2048]{1,0:T(8,128)(2,1)S(1)}, bf16[32,2048]{1,0:T(8,128)(2,1)S(1)}, u32[]{:S(2)}, u32[]{:S(2)}) collective-permute-start(bf16[32,2048]{1,0:T(8,128)(2,1)S(1)} %shard_map.103), channel_id=1, source_target_pairs={{0,3},{1,2},{2,1},{3,0},{4,7},{5,6},{6,5},{7,4},{8,11},{9,10},{10,... | collective-permute-start | bytes 393224 | tf_op jit(solution)/shard_map/ppermute | solution.py:233
  97.6 5.0 %collective-permute-start.17 = (bf16[32,2048]{1,0:T(8,128)(2,1)S(1)}, bf16[32,2048]{1,0:T(8,128)(2,1)S(1)}, u32[]{:S(2)}, u32[]{:S(2)}) collective-permute-start(bf16[32,2048]{1,0:T(8,128)(2,1)S(1)} %add_convert_fusion), channel_id=1, source_target_pairs={{0,1},{1,0},{2,3},{3,2},{4,5},{5,4},{6,7},{7,6},{8,9},{9,8},{10,11... | collective-permute-start | bytes 393224 | tf_op jit(solution)/shard_map/ppermute | solution.py:233
  (2 other events, 6.2 us)

commit v4 on v1

v4 whole, which is shorter than its diff:
```python
import functools

import jax
import jax.numpy as jnp
from jax import lax
from jax.experimental import pallas as pl
from jax.experimental.pallas import tpu as pltpu
from jax.sharding import PartitionSpec as P

SEG = 2048
STEPS = 4
EPS = 1e-06
LOG2E = 1.4426950408889634
PAD = 16
UPDATE_ROWS = 512
QUERY_STAGES = (("book", 1), ("seq", 1))
OUTPUT_STAGES = (("seq", 2), ("seq", 1))


def lift(x):
    return jnp.where(x > 0.0, x + 1.0, jnp.exp(jnp.minimum(x, 0.0)))


def dot(a, b, dims):
    return lax.dot_general(a, b, (dims, ((), ())), preferred_element_type=jnp.float32)


def update_kernel(
    heads, width, block, depth, place_ref, k_hbm, v_hbm, wq_hbm, wo_hbm, u_ref, query_ref, output_ref, k_ref, v_ref, acc, norm, sems
):
    count = k_hbm.shape[0] // block
    at = [pl.multiple_of(place_ref[i] * depth, depth) for i in range(2)]
    slices = [
        pltpu.make_async_copy(wq_hbm.at[pl.ds(at[0], depth), :], query_ref, sems.at[2 * count]),
        pltpu.make_async_copy(wo_hbm.at[:, pl.ds(at[1], depth)], output_ref, sems.at[2 * count + 1]),
    ]
    copies = []
    for i in range(count):
        part = pl.ds(i * block, block)
        pair = (
            pltpu.make_async_copy(k_hbm.at[part], k_ref.at[part], sems.at[2 * i]),
            pltpu.make_async_copy(v_hbm.at[part], v_ref.at[part], sems.at[2 * i + 1]),
        )
        pair[0].start()
        pair[1].start()
        copies.append(pair)
    for copy in slices:
        copy.start()
    for i in range(count):
        part = slice(i * block, (i + 1) * block)
        copies[i][0].wait()
        copies[i][1].wait()
        for h in range(heads):
            cols = slice(h * width, (h + 1) * width)
            lifted = lift(k_ref[part, cols].astype(jnp.float32))
            total = jnp.sum(lifted, axis=0, keepdims=True)
            product = dot(lifted.astype(jnp.bfloat16), v_ref[part, cols], ((0,), (0,)))
            if i == 0:
                norm[h, 0:1, :] = total
                acc[h] = product
            else:
                norm[h, 0:1, :] += total
                acc[h] += product
    for h in range(heads):
        u_ref[h, :width, :] = acc[h].astype(jnp.bfloat16)
        u_ref[h, width:, :] = jnp.broadcast_to(norm[h, 0:1, :], (PAD, width)).astype(jnp.bfloat16)
    for copy in slices:
        copy.wait()


def memory_update(place, keys, values, wq, wo, depth, heads, width):
    rows, lanes = keys.shape
    count = rows // UPDATE_ROWS
    hbm = pl.BlockSpec(memory_space=pltpu.HBM)
    return pl.pallas_call(
        functools.partial(update_kernel, heads, width, UPDATE_ROWS, depth),
        in_specs=[pl.BlockSpec(memory_space=pltpu.SMEM)] + [hbm] * 4,
        out_specs=[pl.BlockSpec(memory_space=pltpu.VMEM)] * 3,
        out_shape=[
            jax.ShapeDtypeStruct((heads, width + PAD, width), jnp.bfloat16),
            jax.ShapeDtypeStruct((depth, wq.shape[1]), wq.dtype),
            jax.ShapeDtypeStruct((wo.shape[0], depth), wo.dtype),
        ],
        scratch_shapes=[
            pltpu.VMEM((rows, lanes), jnp.bfloat16),
            pltpu.VMEM((rows, lanes), jnp.bfloat16),
            pltpu.VMEM((heads, width, width), jnp.float32),
            pltpu.VMEM((heads, 8, width), jnp.float32),
            pltpu.SemaphoreType.DMA((2 * count + 2,)),
        ],
        compiler_params=pltpu.CompilerParams(vmem_limit_bytes=60 << 20),
        cost_estimate=pl.CostEstimate(
            flops=2 * rows * heads * width * width,
            transcendentals=rows * heads * width,
            bytes_accessed=4 * rows * heads * width,
        ),
    )(place, keys, values, wq, wo)


def lifted_query(state, wq):
    rows, depth = state.shape
    block = depth // 4
    return pl.pallas_call(
        query_kernel,
        grid=(4,),
        in_specs=[pl.BlockSpec((rows, block), lambda i: (0, i)), pl.BlockSpec((block, wq.shape[1]), lambda i: (i, 0))],
        out_specs=pl.BlockSpec((rows, wq.shape[1]), lambda i: (0, 0)),
        out_shape=jax.ShapeDtypeStruct((rows, wq.shape[1]), jnp.bfloat16),
        scratch_shapes=[pltpu.VMEM((rows, wq.shape[1]), jnp.float32)],
        compiler_params=pltpu.CompilerParams(vmem_limit_bytes=8 << 20),
        cost_estimate=pl.CostEstimate(
            flops=2 * rows * wq.size, transcendentals=rows * wq.shape[1], bytes_accessed=2 * wq.size
        ),
    )(state, wq)


def query_kernel(s_ref, w_ref, o_ref, acc):
    product = dot(s_ref[...], w_ref[...], ((1,), (0,)))

    @pl.when(pl.program_id(0) == 0)
    def _():
        acc[...] = product

    @pl.when(pl.program_id(0) != 0)
    def _():
        acc[...] += product

    @pl.when(pl.program_id(0) == pl.num_programs(0) - 1)
    def _():
        o_ref[...] = lift(acc[...]).astype(jnp.bfloat16)


def attention_kernel(heads, head, width, first, rows, tile, gate_ref, q_ref, k_ref, v_ref, m_ref, *rest):
    o_ref = rest[-1]
    at = first if q_ref.shape[0] > rows else 0
    factor = LOG2E * width ** (-0.5)
    blocks = (first + rows) // tile
    row = lax.broadcasted_iota(jnp.int32, (rows, tile), 0)
    col = lax.broadcasted_iota(jnp.int32, (rows, tile), 1)
    for h in range(head, head + heads):
        cols = slice(h * width, (h + 1) * width)
        q = q_ref[at : at + rows, cols]
        scores = []
        for j in range(blocks):
            s = dot(q, k_ref[j * tile : (j + 1) * tile, cols], ((1,), (1,))) * factor
            if (j + 1) * tile > first + 1:
                s = jnp.where(col + j * tile <= row + first, s, -jnp.inf)
            scores.append(s)
        top = scores[0]
        for s in scores[1:]:
            top = jnp.maximum(top, s)
        top = jnp.max(top, axis=1, keepdims=True)
        total = jnp.zeros((rows, 1), jnp.float32)
        mixed = jnp.zeros((rows, width), jnp.float32)
        for j in range(blocks):
            p = jnp.exp2(scores[j] - top)
            total += jnp.sum(p, axis=1, keepdims=True)
            mixed += dot(p.astype(jnp.bfloat16), v_ref[j * tile : (j + 1) * tile, cols], ((1,), (0,)))
        lifted = lift(q.astype(jnp.float32)).astype(jnp.bfloat16)
        numerator = dot(lifted, m_ref[h, :width, :], ((1,), (0,)))
        norm = m_ref[h, width : width + 1, :].astype(jnp.float32)
        denominator = jnp.sum(lifted.astype(jnp.float32) * norm, axis=1, keepdims=True) + 1.0
        blend = 1.0 / (1.0 + jnp.exp(jnp.full((1, 1), -gate_ref[h], jnp.float32)))
        mixed = mixed * ((1.0 - blend) / total) + numerator * (blend / denominator)
        mean = jnp.mean(mixed * mixed, axis=1, keepdims=True)
        out = slice((h - head) * width, (h - head + 1) * width)
        o_ref[:, out] = (mixed * lax.rsqrt(mean + EPS)).astype(jnp.bfloat16)


def attention_piece(q, k, v, memory, gate, out, width, first, rows, head, heads):
    lanes = heads * width
    span = first + rows
    vmem = pl.BlockSpec(memory_space=pltpu.VMEM)
    args = [gate, q, k, v, memory]
    specs = [pl.BlockSpec(memory_space=pltpu.SMEM)] + [vmem] * 4
    aliases = {}
    if True:
        specs[1] = pl.BlockSpec((rows, q.shape[1]), lambda i: (first // rows, 0))
        specs[2] = specs[3] = pl.BlockSpec((span, q.shape[1]), lambda i: (0, 0))
    if out is not None:
        args.append(out)
        specs.append(pl.BlockSpec(memory_space=pl.ANY))
        aliases = {5: 0}
    return pl.pallas_call(
        functools.partial(attention_kernel, heads, head, width, first, rows, 512),
        grid=(1,),
        in_specs=specs,
        out_specs=pl.BlockSpec((rows, lanes), lambda i: (first // rows, head // heads)),
        out_shape=jax.ShapeDtypeStruct(q.shape, jnp.bfloat16),
        input_output_aliases=aliases,
        compiler_params=pltpu.CompilerParams(vmem_limit_bytes=24 << 20),
        cost_estimate=pl.CostEstimate(
            flops=4 * rows * span * lanes,
            transcendentals=rows * span * heads,
            bytes_accessed=2 * lanes * (2 * rows + 2 * span),
        ),
    )(*args)


def read_memory(lifted, memory_ref, h, width):
    numerator = dot(lifted, memory_ref[h, :width, :], ((1,), (0,)))
    norm = memory_ref[h, width : width + 1, :].astype(jnp.float32)
    denominator = jnp.sum(lifted.astype(jnp.float32) * norm, axis=1, keepdims=True) + 1.0
    value = numerator / denominator
    mean = jnp.mean(value * value, axis=1, keepdims=True)
    return (value * lax.rsqrt(mean + EPS)).astype(jnp.bfloat16)


def read_heads(lifted, memory_ref, heads, width):
    return jnp.concatenate(
        [read_memory(lifted[:, h * width : (h + 1) * width], memory_ref, h, width) for h in range(heads)],
        axis=1,
    )


def first_kernel(heads, width, parts, flips, me_ref, state_ref, lifted_ref, wo_ref, m_ref, half_ref, kept_ref, sent_ref, acc):
    rows = state_ref.shape[0] // parts
    reads = read_heads(lifted_ref[...], m_ref, heads, width)
    acc[...] = dot(reads, wo_ref[...], ((1,), (0,)))
    for k, f in enumerate(flips):
        at = pl.multiple_of((me_ref[0] ^ f) * rows, rows)
        half_ref[k * rows : (k + 1) * rows, :] = state_ref[pl.ds(at, rows), :]
        for j, ref in enumerate((kept_ref, sent_ref)):
            at = pl.multiple_of((me_ref[0] ^ j ^ f) * rows, rows)
            ref[k * rows : (k + 1) * rows, :] = acc[pl.ds(at, rows), :].astype(jnp.bfloat16)


def first_step(me, state, lifted, wo, memory, heads, width, parts, flips):
    rows, lanes = state.shape
    vmem = pl.BlockSpec(memory_space=pltpu.VMEM)
    shape = jax.ShapeDtypeStruct((rows // parts * len(flips), lanes), jnp.bfloat16)
    return pl.pallas_call(
        functools.partial(first_kernel, heads, width, parts, flips),
        in_specs=[pl.BlockSpec(memory_space=pltpu.SMEM)] + [vmem] * 4,
        out_specs=[vmem] * 3,
        out_shape=[shape] * 3,
        scratch_shapes=[pltpu.VMEM((rows, lanes), jnp.float32)],
        compiler_params=pltpu.CompilerParams(vmem_limit_bytes=12 << 20),
        cost_estimate=pl.CostEstimate(
            flops=2 * rows * wo.size,
            transcendentals=rows * heads * width,
            bytes_accessed=2 * wo.size + 4 * rows * lanes,
        ),
    )(me, state, lifted, wo, memory)


def wide_kernel(heads, width, slices, place_ref, state_ref, wq_ref, wo_ref, m_ref, mx_ref, *rest):
    query_refs, output_refs, (out_ref, acc) = rest[:slices], rest[slices : 2 * slices], rest[2 * slices :]
    group = heads * width
    depth = state_ref.shape[1] // slices

    own = read_heads(lift(dot(state_ref[...], wq_ref[...], ((1,), (0,)))).astype(jnp.bfloat16), m_ref, heads, width)
    query = jnp.zeros((state_ref.shape[0], group), jnp.float32)
    for j in range(slices):
        at = pl.multiple_of((place_ref[0] ^ j) * depth, depth)
        query += dot(state_ref[:, pl.ds(at, depth)], query_refs[j][...], ((1,), (0,)))
    other = read_heads(lift(query).astype(jnp.bfloat16), mx_ref, heads, width)
    acc[...] = dot(own, wo_ref[...], ((1,), (0,)))
    for j in range(slices):
        at = pl.multiple_of((place_ref[1] ^ j) * depth, depth)
        acc[:, pl.ds(at, depth)] += dot(other, output_refs[j][...], ((1,), (0,)))
    out_ref[...] = acc[...].astype(jnp.bfloat16)


def wide_step(place, state, wq, wo, memory, query_side, output_side, other_memory, heads, width):
    rows, lanes = state.shape
    slices = len(query_side)
    vmem = pl.BlockSpec(memory_space=pltpu.VMEM)
    return pl.pallas_call(
        functools.partial(wide_kernel, heads, width, slices),
        in_specs=[pl.BlockSpec(memory_space=pltpu.SMEM)] + [vmem] * (5 + 2 * slices),
        out_specs=vmem,
        out_shape=jax.ShapeDtypeStruct((rows, lanes), jnp.bfloat16),
        scratch_shapes=[pltpu.VMEM((rows, lanes), jnp.float32)],
        compiler_params=pltpu.CompilerParams(vmem_limit_bytes=24 << 20),
        cost_estimate=pl.CostEstimate(
            flops=4 * rows * (wq.size + wo.size),
            transcendentals=2 * rows * heads * width,
            bytes_accessed=4 * (wq.size + wo.size) + 4 * rows * lanes,
        ),
    )(place, state, wq, wo, memory, other_memory, *query_side, *output_side)


def partner(x, axis, flip):
    return lax.ppermute(x, axis, [(i, i ^ flip) for i in range(lax.axis_size(axis))])


def scan_memory(own, decay, axis, beside):
    count, me = lax.axis_size(axis), lax.axis_index(axis)
    shape = own.shape
    total, prior = own, jnp.zeros_like(own)
    order = jnp.arange(count)
    level = 1
    while level < count:
        mine = (order // level) == (me // level)
        theirs = (order // level) == ((me ^ level) // level)

        def product(mask):
            return jnp.prod(jnp.where(mask[:, None], decay, 1.0), axis=0)[:, None, None]

        got = partner(total, axis, level)
        if 2 * level >= count:
            extra = beside(total)
            got, extra = lax.optimization_barrier((got, extra))
        got = got.astype(jnp.float32)
        later = (me & level) != 0
        before_me = product(mine & (order < me))
        kept = total.astype(jnp.float32)
        prior = jnp.where(later, before_me * got + prior.astype(jnp.float32), prior.astype(jnp.float32)).astype(
            jnp.bfloat16
        )
        total = jnp.where(later, product(mine) * got + kept, product(theirs) * kept + got).astype(jnp.bfloat16)
        level *= 2
    return total, prior, extra


def widen(held, axis, flip):
    return held + [partner(piece, axis, flip) for piece in held]


def after(value, *events):
    return lax.optimization_barrier((value, events))[0]


def slice_index(stages):
    place = jnp.int32(0)
    for k, (axis, flip) in enumerate(stages):
        place += jnp.where((lax.axis_index(axis) & flip) != 0, 1 << k, 0).astype(jnp.int32)
    return place


def tree_sum(terms):
    while len(terms) > 1:
        terms = [terms[i] + terms[i + 1] for i in range(0, len(terms), 2)]
    return terms[0]


def wide_sum(terms):
    return tree_sum([t.astype(jnp.float32) for t in terms])


def on_device(queries, keys, values, decay, gate, summary, wq_sum, wo_sum):
    heads = gate.shape[0]
    width = queries.shape[1] // heads
    model = summary.shape[1]
    parts, me = lax.axis_size("sub"), lax.axis_index("sub")
    rows = summary.shape[0] // parts

    flips = tuple((k << 1) | (k.bit_count() & 1) for k in range(parts // 2))

    depth = model >> len(QUERY_STAGES)
    place = jnp.stack([slice_index(QUERY_STAGES), slice_index(OUTPUT_STAGES)])
    own, query_block, output_block = memory_update(
        place, keys, values, wq_sum, wo_sum, depth, heads, width
    )
    query_block = partner(query_block, "sub", 1)
    output_block = partner(output_block, "sub", 1)

    def scan():
        return scan_memory(
            own, decay, "seq", lambda event: lifted_query(after(summary, event), wq_sum)
        )

    def skip():
        empty = jnp.zeros((heads, width + PAD, width), jnp.bfloat16)
        return empty, empty, jnp.zeros((summary.shape[0], heads * width), jnp.bfloat16)

    final, prior, lifted = lax.cond(gate[0] == gate[0], scan, skip)

    chunk = 512

    def fill(event, attended, *places):
        for first, head, count in places:
            attended = attention_piece(
                queries, keys, values, prior, after(gate, event), attended, width, first, chunk, head, count
            )
        return attended

    def swap(array, flip):
        order = [flips.index(f ^ flip) for f in flips]
        return jnp.concatenate([array[k * rows : (k + 1) * rows] for k in order], axis=0)

    def exchange(partial):
        return [partial] + [partner(partial, "sub", f) for f in flips[1:]]

    def summed(state, terms):
        terms = [terms[0]] + [swap(t, f) for t, f in zip(terms[1:], flips[1:])]
        return (state.astype(jnp.float32) + wide_sum(terms)).astype(jnp.bfloat16)

    state, kept, sent = first_step(
        me.reshape(1), summary, lifted, wo_sum, final, heads, width, parts, flips
    )
    got = partner(sent, "sub", 1)
    query_other = partner(after(query_block, kept), *QUERY_STAGES[0])
    output_other = partner(after(output_block, kept), *OUTPUT_STAGES[0])
    other_final = partner(after(final, kept), "sub", 1)
    partial = wide_sum([kept, got]).astype(jnp.bfloat16)
    terms = exchange(partial)
    attended = fill(partial, None, (chunk, 0, heads))
    terms, attended, query_other, output_other, other_final = lax.optimization_barrier(
        (terms, attended, query_other, output_other, other_final)
    )
    query_side = widen([query_block, query_other], *QUERY_STAGES[1])
    output_side = widen([output_block, output_other], *OUTPUT_STAGES[1])
    attended = fill(terms[0], attended, (0, 0, heads))
    query_side, output_side, attended = lax.optimization_barrier((query_side, output_side, attended))
    state = summed(state, terms)

    last = [[(3 * chunk, 0, heads)], [(2 * chunk, 0, heads)], []]
    for step in range(1, STEPS):
        partial = wide_step(
            place, state, wq_sum, wo_sum, final, query_side, output_side, other_final, heads, width
        )
        terms = exchange(partial)
        attended = fill(partial, attended, *last[step - 1])
        terms, attended = lax.optimization_barrier((terms, attended))
        state = summed(state, terms)

    other = partner(state, "sub", 1)
    out = jnp.zeros_like(summary)
    for k, f in enumerate(flips):
        out = lax.dynamic_update_slice_in_dim(out, state[k * rows : (k + 1) * rows], (me ^ f) * rows, 0)
        out = lax.dynamic_update_slice_in_dim(out, other[k * rows : (k + 1) * rows], (me ^ f ^ 1) * rows, 0)
    return (attended, out)


def solution(mesh):
    placed = (
        P(("book", "seq"), "sub"),
        P(("book", "seq"), "sub"),
        P(("book", "seq"), "sub"),
        P("book", "sub"),
        P("sub"),
        P(("book", "seq"), None),
        P(None, "sub"),
        P("sub", None),
    )
    return jax.shard_map(
        on_device,
        mesh=mesh,
        in_specs=placed,
        out_specs=(P(("book", "seq"), "sub"), P(("book", "seq"), None)),
        check_vma=False,
    )
```

time: 103 us -> 87 us (0.84)
  starting transfers between devices: 39.2 us -> 24.1 us
  waiting for transfers between devices: 31.1 us -> 16.3 us
  Pallas kernels: 25.1 us -> 35.8 us
  other arithmetic: 1 us -> 5.2 us
  local copies, waits for them, and re-layouts: 5.57 us -> 4.27 us
    ppermute x26 -> x17, starting transfers between devices: 39.2 us -> 24.1 us  [partner(): lax.ppermute(x, axis, [(i, i ^ flip) for i in range(lax.axis_size(axis))])]
    ppermute x26 -> x17, waiting for transfers between devices: 31.1 us -> 16.3 us  [partner(): lax.ppermute(x, axis, [(i, i ^ flip) for i in range(lax.axis_size(axis))])]
    pallas_call x9 -> x10, Pallas kernels: 25.1 us -> 35.8 us  [the longest x4 19.1 us: attention_piece(): pl.pallas_call(functools.partial(attention_kernel, heads, head, width, fi...]
    convert_element_type x3 -> x6, other arithmetic: 0.14 us -> 2.45 us  [the longest x1 2.2 us: scan_memory(): jnp.where(later, before_me * got + prior.astype(jnp.float32), prior.astyp...]
    unnamed x24 -> x22, local copies, waits for them, and re-layouts: 5.5 us -> 4.07 us
    convert_element_type x2 -> x1, other arithmetic: 0.59 us -> 2.02 us  [scan_memory(): jnp.where(later, product(mine) * got + kept, product(theirs) * kept + got)]
  transfers between devices with their start and end apart: 26 -> 17, of which waited for: 14 -> 8; matrix products, arithmetic and copies ran while one was open for 0% -> 5% of each run, Pallas kernels for 17% -> 27%
where the time goes in v4:
time: 87 us; the launch traced here: 86.6 us
  Pallas kernels  35.8 us (41%)
  starting transfers between devices  24.1 us (28%)
  waiting for transfers between devices  16.3 us (19%)
  other arithmetic  5.2 us (6%)
  local copies, waits for them, and re-layouts  4.27 us (5%)
  between operations  0.94 us (1%)
    ppermute x17, starting transfers between devices, partner(): lax.ppermute(x, axis, [(i, i ^ flip) for i in range(lax.axis_size(axis))])  24.1 us
    pallas_call x4, Pallas kernels, attention_piece(): pl.pallas_call(functools.partial(attention_kernel, heads, head, width, fi...  19.1 us
    ppermute x17, waiting for transfers between devices, partner(): lax.ppermute(x, axis, [(i, i ^ flip) for i in range(lax.axis_size(axis))])  16.3 us
    pallas_call x3, Pallas kernels, wide_step(): pl.pallas_call(functools.partial(wide_kernel, heads, width, slices), in_s...  7.08 us
    pallas_call x1, Pallas kernels, memory_update(): pl.pallas_call(functools.partial(update_kernel, heads, width, UPDATE_ROWS...  4.93 us
    unnamed x22, local copies, waits for them, and re-layouts  4.07 us
    pallas_call x1, Pallas kernels, lifted_query(): pl.pallas_call(query_kernel, grid=(4,), in_specs=[pl.BlockSpec((rows, blo...  2.92 us
    convert_element_type x1, other arithmetic, scan_memory(): jnp.where(later, before_me * got + prior.astype(jnp.float32), prior.astyp...  2.2 us
  transfers between devices with their start and end apart: 17, of which 8 were waited for; matrix products, arithmetic and copies ran while one was open for 5% of the time, Pallas kernels for 27%

profile of v4, /device:TPU:0, one launch (start us, length us, event | category | flops | bytes accessed | tf_op | source)
XLA Modules:
  0.0 86.6 jit_solution(8855565615386308193)
XLA Ops:
  1.3 4.9 %shard_map.96 = (bf16[2,272,256]{2,1,0:T(8,128)(2,1)}, bf16[512,512]{1,0:T(8,128)(2,1)}, bf16[512,512]{1,0:T(8,128)(2,1)}) custom-call(s32[2]{0:T(128)} %pad_add_fusion.place_ref, bf16[2048,512]{1,0:T(8,128)(2,1)} %k_ref.7, bf16[2048,512]{1,0:T(8,128)(2,1)} %v_ref.7, bf16[2048,512]{1,0:T(8,128)(2,1)} %wq_ref.5, bf16[512,2048]{1,0:T(8,128)(2,1)} %wo_ref.7), custom_call_target="tpu_custom_call" | custom-call | flops 536870912 | bytes 4194304 | tf_op jit(solution)/shard_map/pallas_call | solution.py:75
  6.2 3.1 %collective-permute-start.4 = (bf16[512,512]{1,0:T(8,128)(2,1)}, bf16[512,512]{1,0:T(8,128)(2,1)S(1)}, u32[]{:S(2)}, u32[]{:S(2)}) collective-permute-start(bf16[512,512]{1,0:T(8,128)(2,1)} %get-tuple-element.65), channel_id=1, source_target_pairs={{0,1},{1,0},{2,3},{3,2},{4,5},{5,4},{6,7},{7,6},{8,9},{9,8},{10,11... | collective-permute-start | bytes 1572872 | tf_op jit(solution)/shard_map/ppermute | solution.py:285
  9.4 15.2 %conditional.1 = (bf16[2,272,256]{2,1,0:T(8,128)(2,1)S(1)}, bf16[2,272,256]{2,1,0:T(8,128)(2,1)}, bf16[64,512]{1,0:T(8,128)(2,1)S(1)}) conditional(s32[]{:T(128)} %bitcast.3, () %tuple.30, (f32[4,2]{0,1:T(2,128)S(1)}, bf16[2,272,256]{2,1,0:T(8,128)(2,1)}, bf16[64,2048]{1,0:T(8,128)(2,1)}, bf16[2048,512]{1,0:T(8,128)(2,1)}) %tuple.61), branch_computations={%region_0.1_spmd, %region_1.8_spmd} | conditional | flops 137699552 | bytes 7668509 | solution.py:368
  11.3 2.0 %fusion.1 = bf16[2,272,256]{2,1,0:T(8,128)(2,1)} fusion(bf16[2,272,256]{2,1,0:T(8,128)(2,1)} %get-tuple-element.9, bf16[2,272,256]{2,1,0:T(8,128)(2,1)S(1)} %collective-permute-done, f32[2]{0:T(128)S(1)} %get-tuple-element.105, f32[2]{0:T(128)S(1)} %get-tuple-element.106, pred[]{:T(512)S(6)} %ne.80), kind=kLoop, calls=%fused_computation.12 | loop fusion | flops 1114112 | bytes 835601 | tf_op jit(solution)/shard_map/cond/branch_1_fun/convert_element_type | solution.py:312
  13.3 1.9 %collective-permute-start.1 = (bf16[2,272,256]{2,1,0:T(8,128)(2,1)}, bf16[2,272,256]{2,1,0:T(8,128)(2,1)}, u32[]{:S(2)}, u32[]{:S(2)}) collective-permute-start(bf16[2,272,256]{2,1,0:T(8,128)(2,1)} %fusion.1), channel_id=1, source_target_pairs={{0,8},{4,12},{8,0},{12,4},{1,9},{5,13},{9,1},{13,5},{2,10},{6,14},... | collective-permute-start | bytes 835592 | tf_op jit(solution)/shard_map/cond/branch_1_fun/ppermute | solution.py:285
  15.2 2.9 %branch_1_fun.1 = bf16[64,512]{1,0:T(8,128)(2,1)S(1)} custom-call(bf16[64,2048]{1,0:T(8,128)(2,1)} %get-tuple-element.11.s_ref, bf16[2048,512]{1,0:T(8,128)(2,1)} %get-tuple-element.12.w_ref), custom_call_target="tpu_custom_call" | custom-call | flops 134217728 | bytes 2097152 | tf_op jit(solution)/shard_map/cond/branch_1_fun/pallas_call | solution.py:103
  18.1 4.3 %collective-permute-done.1 = bf16[2,272,256]{2,1,0:T(8,128)(2,1)} collective-permute-done((bf16[2,272,256]{2,1,0:T(8,128)(2,1)}, bf16[2,272,256]{2,1,0:T(8,128)(2,1)}, u32[]{:S(2)}, u32[]{:S(2)}) %collective-permute-start.1) | collective-permute-done | bytes 278560 | tf_op jit(solution)/shard_map/cond/branch_1_fun/ppermute | solution.py:285
  22.4 2.2 %fusion.6 = (bf16[2,272,256]{2,1,0:T(8,128)(2,1)}, bf16[2,272,256]{2,1,0:T(8,128)(2,1)S(1)}) fusion(bf16[2,272,256]{2,1,0:T(8,128)(2,1)} %collective-permute-done.1, bf16[2,272,256]{2,1,0:T(8,128)(2,1)} %copy-done.9, f32[2]{0:T(128)S(1)} %get-tuple-element.108, f32[2]{0:T(128)S(1)} %get-tuple-element.103, pred[]{:T(512)S(6)} %ne.80, pred[]{:T(512)S(6)} %ne.74, ...), kind=kLoop, calls=%fused_computation.17 | loop fusion | flops 2367488 | bytes 1392674 | tf_op jit(solution)/shard_map/cond/branch_1_fun/convert_element_type | solution.py:309
  28.1 1.9 %collective-permute-start.2 = (bf16[32,2048]{1,0:T(8,128)(2,1)S(1)}, bf16[32,2048]{1,0:T(8,128)(2,1)S(1)}, u32[]{:S(2)}, u32[]{:S(2)}) collective-permute-start(bf16[32,2048]{1,0:T(8,128)(2,1)S(1)} %get-tuple-element.62), channel_id=1, source_target_pairs={{0,1},{1,0},{2,3},{3,2},{4,5},{5,4},{6,7},{7,6},{8,9},{9,8},{10,11... | collective-permute-start | bytes 393224 | tf_op jit(solution)/shard_map/ppermute | solution.py:285
  30.2 1.8 %collective-permute-start.5 = (bf16[512,512]{1,0:T(8,128)(2,1)S(1)}, bf16[512,512]{1,0:T(8,128)(2,1)S(1)}, u32[]{:S(2)}, u32[]{:S(2)}) collective-permute-start(bf16[512,512]{1,0:T(8,128)(2,1)S(1)} %collective-permute-done.4.rest_0_), channel_id=1, source_target_pairs={{0,16},{16,0},{1,17},{17,1},{2,18},{18,2},{3,19},{19,3},{4,20},{20... | collective-permute-start | bytes 1572872 | tf_op jit(solution)/shard_map/ppermute | solution.py:285
  33.5 2.0 %collective-permute-start.7 = (bf16[512,512]{1,0:T(8,128)(2,1)S(1)}, bf16[512,512]{1,0:T(8,128)(2,1)S(1)}, u32[]{:S(2)}, u32[]{:S(2)}) collective-permute-start(bf16[512,512]{1,0:T(8,128)(2,1)S(1)} %collective-permute-done.6.rest_4_), channel_id=1, source_target_pairs={{0,8},{4,12},{8,0},{12,4},{1,9},{5,13},{9,1},{13,5},{2,10},{6,14},... | collective-permute-start | bytes 1572872 | tf_op jit(solution)/shard_map/ppermute | solution.py:285
  36.3 4.1 %collective-permute-start.3 = (bf16[32,2048]{1,0:T(8,128)(2,1)S(1)}, bf16[32,2048]{1,0:T(8,128)(2,1)S(1)}, u32[]{:S(2)}, u32[]{:S(2)}) collective-permute-start(bf16[32,2048]{1,0:T(8,128)(2,1)S(1)} %add_convert_fusion.4), channel_id=1, source_target_pairs={{0,3},{1,2},{2,1},{3,0},{4,7},{5,6},{6,5},{7,4},{8,11},{9,10},{10,... | collective-permute-start | bytes 393224 | tf_op jit(solution)/shard_map/ppermute | solution.py:285
  42.1 4.2 %shard_map.98.rest_0_ = bf16[2048,512]{1,0:T(8,128)(2,1)} custom-call(f32[2]{0:T(128)S(1)} %copy-done.6, bf16[2048,512]{1,0:T(8,128)(2,1)S(1)} %copy-done.4, bf16[2048,512]{1,0:T(8,128)(2,1)S(1)} %copy-done, bf16[2048,512]{1,0:T(8,128)(2,1)S(1)} %copy-done.1, bf16[2,272,256]{2,1,0:T(8,128)(2,1)} %get-tuple-element.64.m_ref), custom_call_target="tpu_custom_call" | custom-call | flops 1073741824 | bytes 3145728 | tf_op jit(solution)/shard_map/pallas_call | solution.py:184
  47.4 3.4 %shard_map.99.rest_0_ = bf16[2048,512]{1,0:T(8,128)(2,1)} custom-call(f32[2]{0:T(128)S(1)} %copy-done.6, bf16[2048,512]{1,0:T(8,128)(2,1)S(1)} %copy-done.4, bf16[2048,512]{1,0:T(8,128)(2,1)S(1)} %copy-done, bf16[2048,512]{1,0:T(8,128)(2,1)S(1)} %copy-done.1, bf16[2,272,256]{2,1,0:T(8,128)(2,1)} %get-tuple-element.64.m_ref, ...), custom_call_target="tpu_custom_call", output_to_operand_aliasing={{}: (5, {})} | custom-call | flops 536870912 | bytes 2097152 | tf_op jit(solution)/shard_map/pallas_call | solution.py:184
  50.9 2.4 %shard_map.100 = bf16[32,2048]{1,0:T(8,128)(2,1)S(1)} custom-call(s32[2]{0:T(128)S(1)} %copy-done.7, bf16[32,2048]{1,0:T(8,128)(2,1)S(1)} %add_convert_fusion.3.state_ref, bf16[2048,512]{1,0:T(8,128)(2,1)S(1)} %copy-done.8, bf16[512,2048]{1,0:T(8,128)(2,1)S(1)} %copy-done.3, bf16[2,272,256]{2,1,0:T(8,128)(2,1)S(1)} %get-tuple-element.69.m_ref, ...), custom_call_target="tpu_custom_call" | custom-call | flops 268435456 | bytes 8650752 | tf_op jit(solution)/shard_map/pallas_call | solution.py:269
  53.3 2.4 %collective-permute-start.13 = (bf16[32,2048]{1,0:T(8,128)(2,1)S(1)}, bf16[32,2048]{1,0:T(8,128)(2,1)S(1)}, u32[]{:S(2)}, u32[]{:S(2)}) collective-permute-start(bf16[32,2048]{1,0:T(8,128)(2,1)S(1)} %shard_map.100), channel_id=1, source_target_pairs={{0,3},{1,2},{2,1},{3,0},{4,7},{5,6},{6,5},{7,4},{8,11},{9,10},{10,... | collective-permute-start | bytes 393224 | tf_op jit(solution)/shard_map/ppermute | solution.py:285
  55.8 6.1 %shard_map.101.rest_0_ = bf16[2048,512]{1,0:T(8,128)(2,1)} custom-call(f32[2]{0:T(128)S(1)} %copy-done.6, bf16[2048,512]{1,0:T(8,128)(2,1)S(1)} %copy-done.5, bf16[2048,512]{1,0:T(8,128)(2,1)S(1)} %copy-done, bf16[2048,512]{1,0:T(8,128)(2,1)S(1)} %copy-done.1, bf16[2,272,256]{2,1,0:T(8,128)(2,1)} %get-tuple-element.64.m_ref, ...), custom_call_target="tpu_custom_call", output_to_operand_aliasing={{}: (5, {})} | custom-call | flops 2147483648 | bytes 5242880 | tf_op jit(solution)/shard_map/pallas_call | solution.py:184
  62.0 2.4 %shard_map.102 = bf16[32,2048]{1,0:T(8,128)(2,1)S(1)} custom-call(s32[2]{0:T(128)S(1)} %copy-done.7, bf16[32,2048]{1,0:T(8,128)(2,1)S(1)} %add_convert_fusion.2.state_ref, bf16[2048,512]{1,0:T(8,128)(2,1)S(1)} %copy-done.8, bf16[512,2048]{1,0:T(8,128)(2,1)S(1)} %copy-done.3, bf16[2,272,256]{2,1,0:T(8,128)(2,1)S(1)} %get-tuple-element.69.m_ref, ...), custom_call_target="tpu_custom_call" | custom-call | flops 268435456 | bytes 8650752 | tf_op jit(solution)/shard_map/pallas_call | solution.py:269
  65.8 5.4 %shard_map.103 = bf16[2048,512]{1,0:T(8,128)(2,1)} custom-call(f32[2]{0:T(128)S(1)} %copy-done.6, bf16[2048,512]{1,0:T(8,128)(2,1)S(1)} %copy-done.5, bf16[2048,512]{1,0:T(8,128)(2,1)S(1)} %copy-done, bf16[2048,512]{1,0:T(8,128)(2,1)S(1)} %copy-done.1, bf16[2,272,256]{2,1,0:T(8,128)(2,1)} %get-tuple-element.64.m_ref, ...), custom_call_target="tpu_custom_call", output_to_operand_aliasing={{}: (5, {})} | custom-call | flops 1610612736 | bytes 4194304 | tf_op jit(solution)/shard_map/pallas_call | solution.py:184
  71.5 2.4 %shard_map.104 = bf16[32,2048]{1,0:T(8,128)(2,1)S(1)} custom-call(s32[2]{0:T(128)S(1)} %copy-done.7, bf16[32,2048]{1,0:T(8,128)(2,1)S(1)} %add_convert_fusion.1.state_ref, bf16[2048,512]{1,0:T(8,128)(2,1)S(1)} %copy-done.8, bf16[512,2048]{1,0:T(8,128)(2,1)S(1)} %copy-done.3, bf16[2,272,256]{2,1,0:T(8,128)(2,1)S(1)} %get-tuple-element.69.m_ref, ...), custom_call_target="tpu_custom_call" | custom-call | flops 268435456 | bytes 8650752 | tf_op jit(solution)/shard_map/pallas_call | solution.py:269
  73.9 2.3 %collective-permute-start.15 = (bf16[32,2048]{1,0:T(8,128)(2,1)S(1)}, bf16[32,2048]{1,0:T(8,128)(2,1)S(1)}, u32[]{:S(2)}, u32[]{:S(2)}) collective-permute-start(bf16[32,2048]{1,0:T(8,128)(2,1)S(1)} %shard_map.104), channel_id=1, source_target_pairs={{0,3},{1,2},{2,1},{3,0},{4,7},{5,6},{6,5},{7,4},{8,11},{9,10},{10,... | collective-permute-start | bytes 393224 | tf_op jit(solution)/shard_map/ppermute | solution.py:285
  76.2 4.6 %collective-permute-done.15 = bf16[32,2048]{1,0:T(8,128)(2,1)S(1)} collective-permute-done((bf16[32,2048]{1,0:T(8,128)(2,1)S(1)}, bf16[32,2048]{1,0:T(8,128)(2,1)S(1)}, u32[]{:S(2)}, u32[]{:S(2)}) %collective-permute-start.15) | collective-permute-done | bytes 131104 | tf_op jit(solution)/shard_map/ppermute | solution.py:285
  80.8 1.8 %collective-permute-start.16 = (bf16[32,2048]{1,0:T(8,128)(2,1)S(1)}, bf16[32,2048]{1,0:T(8,128)(2,1)S(1)}, u32[]{:S(2)}, u32[]{:S(2)}) collective-permute-start(bf16[32,2048]{1,0:T(8,128)(2,1)S(1)} %add_convert_fusion), channel_id=1, source_target_pairs={{0,1},{1,0},{2,3},{3,2},{4,5},{5,4},{6,7},{7,6},{8,9},{9,8},{10,11... | collective-permute-start | bytes 393224 | tf_op jit(solution)/shard_map/ppermute | solution.py:285
  82.7 3.2 %collective-permute-done.16 = bf16[32,2048]{1,0:T(8,128)(2,1)S(1)} collective-permute-done((bf16[32,2048]{1,0:T(8,128)(2,1)S(1)}, bf16[32,2048]{1,0:T(8,128)(2,1)S(1)}, u32[]{:S(2)}, u32[]{:S(2)}) %collective-permute-start.16) | collective-permute-done | bytes 131104 | tf_op jit(solution)/shard_map/ppermute | solution.py:285
  (67 shorter events, 13.9 us)
Async XLA Ops:
  1.3 8.1 %copy-start.6 = (f32[2]{0:T(128)S(1)}, f32[2]{0:T(128)}, u32[]{:S(2)}) copy-start(f32[2]{0:T(128)} %gate_ref.3) | copy-start | bytes 28
  1.3 8.2 %copy-start.11 = (f32[4,2]{0,1:T(2,128)S(1)}, f32[4,2]{0,1:T(2,128)}, u32[]{:S(2)}) copy-start(f32[4,2]{0,1:T(2,128)} %param.13) | copy-start | bytes 100
  6.2 24.0 %collective-permute-start.4 = (bf16[512,512]{1,0:T(8,128)(2,1)}, bf16[512,512]{1,0:T(8,128)(2,1)S(1)}, u32[]{:S(2)}, u32[]{:S(2)}) collective-permute-start(bf16[512,512]{1,0:T(8,128)(2,1)} %get-tuple-element.65), channel_id=1, source_target_pairs={{0,1},{1,0},{2,3},{3,2},{4,5},{5,4},{6,7},{7,6},{8,9},{9,8},{10,11... | collective-permute-start | bytes 1572872 | tf_op jit(solution)/shard_map/ppermute | solution.py:285
  9.3 24.2 %collective-permute-start.6 = (bf16[512,512]{1,0:T(8,128)(2,1)}, bf16[512,512]{1,0:T(8,128)(2,1)S(1)}, u32[]{:S(2)}, u32[]{:S(2)}) collective-permute-start(bf16[512,512]{1,0:T(8,128)(2,1)} %get-tuple-element.67), channel_id=1, source_target_pairs={{0,1},{1,0},{2,3},{3,2},{4,5},{5,4},{6,7},{7,6},{8,9},{9,8},{10,11... | collective-permute-start | bytes 1572872 | tf_op jit(solution)/shard_map/ppermute | solution.py:285
  9.4 31.1 %copy-start.1 = (bf16[2048,512]{1,0:T(8,128)(2,1)S(1)}, bf16[2048,512]{1,0:T(8,128)(2,1)}, u32[]{:S(2)}) copy-start(bf16[2048,512]{1,0:T(8,128)(2,1)} %v_ref.7) | copy-start | bytes 6291460
  9.5 1.8 %collective-permute-start = (bf16[2,272,256]{2,1,0:T(8,128)(2,1)}, bf16[2,272,256]{2,1,0:T(8,128)(2,1)S(1)}, u32[]{:S(2)}, u32[]{:S(2)}) collective-permute-start(bf16[2,272,256]{2,1,0:T(8,128)(2,1)} %get-tuple-element.9), channel_id=1, source_target_pairs={{0,4},{4,0},{8,12},{12,8},{1,5},{5,1},{9,13},{13,9},{2,6},{6,2},{1... | collective-permute-start | bytes 835592 | tf_op jit(solution)/shard_map/cond/branch_1_fun/ppermute | solution.py:285
  11.3 11.2 %copy-start.9 = (bf16[2,272,256]{2,1,0:T(8,128)(2,1)}, bf16[2,272,256]{2,1,0:T(8,128)(2,1)S(1)}, u32[]{:S(2)}) copy-start(bf16[2,272,256]{2,1,0:T(8,128)(2,1)S(1)} %collective-permute-done) | copy-start | bytes 835588 | tf_op jit(solution)/shard_map/cond
  13.3 9.1 %collective-permute-start.1 = (bf16[2,272,256]{2,1,0:T(8,128)(2,1)}, bf16[2,272,256]{2,1,0:T(8,128)(2,1)}, u32[]{:S(2)}, u32[]{:S(2)}) collective-permute-start(bf16[2,272,256]{2,1,0:T(8,128)(2,1)} %fusion.1), channel_id=1, source_target_pairs={{0,8},{4,12},{8,0},{12,4},{1,9},{5,13},{9,1},{13,5},{2,10},{6,14},... | collective-permute-start | bytes 835592 | tf_op jit(solution)/shard_map/cond/branch_1_fun/ppermute | solution.py:285
  24.7 15.8 %copy-start = (bf16[2048,512]{1,0:T(8,128)(2,1)S(1)}, bf16[2048,512]{1,0:T(8,128)(2,1)}, u32[]{:S(2)}) copy-start(bf16[2048,512]{1,0:T(8,128)(2,1)} %k_ref.7) | copy-start | bytes 6291460
  28.1 8.2 %collective-permute-start.2 = (bf16[32,2048]{1,0:T(8,128)(2,1)S(1)}, bf16[32,2048]{1,0:T(8,128)(2,1)S(1)}, u32[]{:S(2)}, u32[]{:S(2)}) collective-permute-start(bf16[32,2048]{1,0:T(8,128)(2,1)S(1)} %get-tuple-element.62), channel_id=1, source_target_pairs={{0,1},{1,0},{2,3},{3,2},{4,5},{5,4},{6,7},{7,6},{8,9},{9,8},{10,11... | collective-permute-start | bytes 393224 | tf_op jit(solution)/shard_map/ppermute | solution.py:285
  30.0 16.8 %collective-permute-start.8 = (bf16[2,272,256]{2,1,0:T(8,128)(2,1)S(1)}, bf16[2,272,256]{2,1,0:T(8,128)(2,1)S(1)}, u32[]{:S(2)}, u32[]{:S(2)}) collective-permute-start(bf16[2,272,256]{2,1,0:T(8,128)(2,1)S(1)} %get-tuple-element.69.m_ref), channel_id=1, source_target_pairs={{0,1},{1,0},{2,3},{3,2},{4,5},{5,4},{6,7},{7,6},{8,9},{9,8},{10,11... | collective-permute-start | bytes 835592 | tf_op jit(solution)/shard_map/ppermute | solution.py:285
  30.2 16.6 %collective-permute-start.5 = (bf16[512,512]{1,0:T(8,128)(2,1)S(1)}, bf16[512,512]{1,0:T(8,128)(2,1)S(1)}, u32[]{:S(2)}, u32[]{:S(2)}) collective-permute-start(bf16[512,512]{1,0:T(8,128)(2,1)S(1)} %collective-permute-done.4.rest_0_), channel_id=1, source_target_pairs={{0,16},{16,0},{1,17},{17,1},{2,18},{18,2},{3,19},{19,3},{4,20},{20... | collective-permute-start | bytes 1572872 | tf_op jit(solution)/shard_map/ppermute | solution.py:285
  33.5 13.3 %collective-permute-start.7 = (bf16[512,512]{1,0:T(8,128)(2,1)S(1)}, bf16[512,512]{1,0:T(8,128)(2,1)S(1)}, u32[]{:S(2)}, u32[]{:S(2)}) collective-permute-start(bf16[512,512]{1,0:T(8,128)(2,1)S(1)} %collective-permute-done.6.rest_4_), channel_id=1, source_target_pairs={{0,8},{4,12},{8,0},{12,4},{1,9},{5,13},{9,1},{13,5},{2,10},{6,14},... | collective-permute-start | bytes 1572872 | tf_op jit(solution)/shard_map/ppermute | solution.py:285
  36.3 10.1 %collective-permute-start.3 = (bf16[32,2048]{1,0:T(8,128)(2,1)S(1)}, bf16[32,2048]{1,0:T(8,128)(2,1)S(1)}, u32[]{:S(2)}, u32[]{:S(2)}) collective-permute-start(bf16[32,2048]{1,0:T(8,128)(2,1)S(1)} %add_convert_fusion.4), channel_id=1, source_target_pairs={{0,3},{1,2},{2,1},{3,0},{4,7},{5,6},{6,5},{7,4},{8,11},{9,10},{10,... | collective-permute-start | bytes 393224 | tf_op jit(solution)/shard_map/ppermute | solution.py:285
  46.2 4.6 %collective-permute-start.11 = (bf16[512,512]{1,0:T(8,128)(2,1)S(1)}, bf16[512,512]{1,0:T(8,128)(2,1)S(1)}, u32[]{:S(2)}, u32[]{:S(2)}) collective-permute-start(bf16[512,512]{1,0:T(8,128)(2,1)S(1)} %collective-permute-done.6.rest_4_), channel_id=1, source_target_pairs={{0,4},{4,0},{8,12},{12,8},{1,5},{5,1},{9,13},{13,9},{2,6},{6,2},{1... | collective-permute-start | bytes 1572872 | tf_op jit(solution)/shard_map/ppermute | solution.py:285
  46.4 4.5 %collective-permute-start.9 = (bf16[512,512]{1,0:T(8,128)(2,1)S(1)}, bf16[512,512]{1,0:T(8,128)(2,1)S(1)}, u32[]{:S(2)}, u32[]{:S(2)}) collective-permute-start(bf16[512,512]{1,0:T(8,128)(2,1)S(1)} %collective-permute-done.4.rest_0_), channel_id=1, source_target_pairs={{0,4},{4,0},{8,12},{12,8},{1,5},{5,1},{9,13},{13,9},{2,6},{6,2},{1... | collective-permute-start | bytes 1572872 | tf_op jit(solution)/shard_map/ppermute | solution.py:285
  46.8 4.1 %collective-permute-start.10 = (bf16[512,512]{1,0:T(8,128)(2,1)S(1)}, bf16[512,512]{1,0:T(8,128)(2,1)S(1)}, u32[]{:S(2)}, u32[]{:S(2)}) collective-permute-start(bf16[512,512]{1,0:T(8,128)(2,1)S(1)} %collective-permute-done.5.rest_1_), channel_id=1, source_target_pairs={{0,4},{4,0},{8,12},{12,8},{1,5},{5,1},{9,13},{13,9},{2,6},{6,2},{1... | collective-permute-start | bytes 1572872 | tf_op jit(solution)/shard_map/ppermute | solution.py:285
  47.0 3.9 %collective-permute-start.12 = (bf16[512,512]{1,0:T(8,128)(2,1)S(1)}, bf16[512,512]{1,0:T(8,128)(2,1)S(1)}, u32[]{:S(2)}, u32[]{:S(2)}) collective-permute-start(bf16[512,512]{1,0:T(8,128)(2,1)S(1)} %collective-permute-done.7.rest_5_), channel_id=1, source_target_pairs={{0,4},{4,0},{8,12},{12,8},{1,5},{5,1},{9,13},{13,9},{2,6},{6,2},{1... | collective-permute-start | bytes 1572872 | tf_op jit(solution)/shard_map/ppermute | solution.py:285
  47.4 3.6 %copy-start.3 = (bf16[512,2048]{1,0:T(8,128)(2,1)S(1)}, bf16[512,2048]{1,0:T(8,128)(2,1)}, u32[]{:S(2)}) copy-start(bf16[512,2048]{1,0:T(8,128)(2,1)} %wo_ref.7) | copy-start | bytes 6291460
  50.9 4.9 %copy-start.5 = (bf16[2048,512]{1,0:T(8,128)(2,1)S(1)}, bf16[2048,512]{1,0:T(8,128)(2,1)}, u32[]{:S(2)}) copy-start(bf16[2048,512]{1,0:T(8,128)(2,1)} %q_ref.7) | copy-start | bytes 6291460
  53.3 8.6 %collective-permute-start.13 = (bf16[32,2048]{1,0:T(8,128)(2,1)S(1)}, bf16[32,2048]{1,0:T(8,128)(2,1)S(1)}, u32[]{:S(2)}, u32[]{:S(2)}) collective-permute-start(bf16[32,2048]{1,0:T(8,128)(2,1)S(1)} %shard_map.100), channel_id=1, source_target_pairs={{0,3},{1,2},{2,1},{3,0},{4,7},{5,6},{6,5},{7,4},{8,11},{9,10},{10,... | collective-permute-start | bytes 393224 | tf_op jit(solution)/shard_map/ppermute | solution.py:285
  64.3 7.1 %collective-permute-start.14 = (bf16[32,2048]{1,0:T(8,128)(2,1)S(1)}, bf16[32,2048]{1,0:T(8,128)(2,1)S(1)}, u32[]{:S(2)}, u32[]{:S(2)}) collective-permute-start(bf16[32,2048]{1,0:T(8,128)(2,1)S(1)} %shard_map.102), channel_id=1, source_target_pairs={{0,3},{1,2},{2,1},{3,0},{4,7},{5,6},{6,5},{7,4},{8,11},{9,10},{10,... | collective-permute-start | bytes 393224 | tf_op jit(solution)/shard_map/ppermute | solution.py:285
  73.9 6.9 %collective-permute-start.15 = (bf16[32,2048]{1,0:T(8,128)(2,1)S(1)}, bf16[32,2048]{1,0:T(8,128)(2,1)S(1)}, u32[]{:S(2)}, u32[]{:S(2)}) collective-permute-start(bf16[32,2048]{1,0:T(8,128)(2,1)S(1)} %shard_map.104), channel_id=1, source_target_pairs={{0,3},{1,2},{2,1},{3,0},{4,7},{5,6},{6,5},{7,4},{8,11},{9,10},{10,... | collective-permute-start | bytes 393224 | tf_op jit(solution)/shard_map/ppermute | solution.py:285
  80.8 5.0 %collective-permute-start.16 = (bf16[32,2048]{1,0:T(8,128)(2,1)S(1)}, bf16[32,2048]{1,0:T(8,128)(2,1)S(1)}, u32[]{:S(2)}, u32[]{:S(2)}) collective-permute-start(bf16[32,2048]{1,0:T(8,128)(2,1)S(1)} %add_convert_fusion), channel_id=1, source_target_pairs={{0,1},{1,0},{2,3},{3,2},{4,5},{5,4},{6,7},{7,6},{8,9},{9,8},{10,11... | collective-permute-start | bytes 393224 | tf_op jit(solution)/shard_map/ppermute | solution.py:285
  (5 other events, 11.1 us)

commit v5 on v4

--- a/solution.py
+++ b/solution.py
@@ -26,7 +26,8 @@
 
 
 def update_kernel(
-    heads, width, block, depth, place_ref, k_hbm, v_hbm, wq_hbm, wo_hbm, u_ref, query_ref, output_ref, k_ref, v_ref, acc, norm, sems
+    heads, width, block, depth, place_ref, k_hbm, v_hbm, wq_hbm, wo_hbm, u_ref, query_hbm, output_hbm,
+    k_ref, v_ref, query_ref, output_ref, acc, norm, sems
 ):
     count = k_hbm.shape[0] // block
     at = [pl.multiple_of(place_ref[i] * depth, depth) for i in range(2)]
@@ -34,6 +35,12 @@
         pltpu.make_async_copy(wq_hbm.at[pl.ds(at[0], depth), :], query_ref, sems.at[2 * count]),
         pltpu.make_async_copy(wo_hbm.at[:, pl.ds(at[1], depth)], output_ref, sems.at[2 * count + 1]),
     ]
+    backs = [
+        pltpu.make_async_copy(query_ref, query_hbm, sems.at[2 * count + 2]),
+        pltpu.make_async_copy(output_ref, output_hbm, sems.at[2 * count + 3]),
+    ]
+    for copy in slices:
+        copy.start()
     copies = []
     for i in range(count):
         part = pl.ds(i * block, block)
@@ -44,12 +51,14 @@
         pair[0].start()
         pair[1].start()
         copies.append(pair)
-    for copy in slices:
-        copy.start()
     for i in range(count):
         part = slice(i * block, (i + 1) * block)
         copies[i][0].wait()
         copies[i][1].wait()
+        if i == 0:
+            for copy, back in zip(slices, backs):
+                copy.wait()
+                back.start()
         for h in range(heads):
             cols = slice(h * width, (h + 1) * width)
             lifted = lift(k_ref[part, cols].astype(jnp.float32))
@@ -64,7 +73,7 @@
     for h in range(heads):
         u_ref[h, :width, :] = acc[h].astype(jnp.bfloat16)
         u_ref[h, width:, :] = jnp.broadcast_to(norm[h, 0:1, :], (PAD, width)).astype(jnp.bfloat16)
-    for copy in slices:
+    for copy in backs:
         copy.wait()
 
 
@@ -75,7 +84,7 @@
     return pl.pallas_call(
         functools.partial(update_kernel, heads, width, UPDATE_ROWS, depth),
         in_specs=[pl.BlockSpec(memory_space=pltpu.SMEM)] + [hbm] * 4,
-        out_specs=[pl.BlockSpec(memory_space=pltpu.VMEM)] * 3,
+        out_specs=[pl.BlockSpec(memory_space=pltpu.VMEM), hbm, hbm],
         out_shape=[
             jax.ShapeDtypeStruct((heads, width + PAD, width), jnp.bfloat16),
             jax.ShapeDtypeStruct((depth, wq.shape[1]), wq.dtype),
@@ -84,9 +93,11 @@
         scratch_shapes=[
             pltpu.VMEM((rows, lanes), jnp.bfloat16),
             pltpu.VMEM((rows, lanes), jnp.bfloat16),
+            pltpu.VMEM((depth, wq.shape[1]), wq.dtype),
+            pltpu.VMEM((wo.shape[0], depth), wo.dtype),
             pltpu.VMEM((heads, width, width), jnp.float32),
             pltpu.VMEM((heads, 8, width), jnp.float32),
-            pltpu.SemaphoreType.DMA((2 * count + 2,)),
+            pltpu.SemaphoreType.DMA((2 * count + 4,)),
         ],
         compiler_params=pltpu.CompilerParams(vmem_limit_bytes=60 << 20),
         cost_estimate=pl.CostEstimate(
@@ -213,10 +224,23 @@
     )
 
 
-def first_kernel(heads, width, parts, flips, me_ref, state_ref, lifted_ref, wo_ref, m_ref, half_ref, kept_ref, sent_ref, acc):
+def first_kernel(
+    heads, width, flips, parts, me_ref, coef_ref, state_ref, lifted_ref, total_ref, got_ref, early_ref, wo_hbm,
+    half_ref, kept_ref, sent_ref, final_ref, prior_ref, wo_ref, acc, sems
+):
     rows = state_ref.shape[0] // parts
-    reads = read_heads(lifted_ref[...], m_ref, heads, width)
-    acc[...] = dot(reads, wo_ref[...], ((1,), (0,)))
+    copies = []
+    for h in range(heads):
+        part = pl.ds(h * width, width)
+        copies.append(pltpu.make_async_copy(wo_hbm.at[part], wo_ref.at[part], sems.at[h]))
+        copies[h].start()
+    combine_kernel(heads, coef_ref, total_ref, got_ref, early_ref, final_ref, prior_ref)
+    for h in range(heads):
+        part = slice(h * width, (h + 1) * width)
+        read = read_memory(lifted_ref[:, part], final_ref, h, width)
+        copies[h].wait()
+        product = dot(read, wo_ref[part, :], ((1,), (0,)))
+        acc[...] = product if h == 0 else acc[...] + product
     for k, f in enumerate(flips):
         at = pl.multiple_of((me_ref[0] ^ f) * rows, rows)
         half_ref[k * rows : (k + 1) * rows, :] = state_ref[pl.ds(at, rows), :]
@@ -225,23 +249,28 @@
             ref[k * rows : (k + 1) * rows, :] = acc[pl.ds(at, rows), :].astype(jnp.bfloat16)
 
 
-def first_step(me, state, lifted, wo, memory, heads, width, parts, flips):
+def first_step(me, coef, state, lifted, total, got, early, wo, heads, width, parts, flips):
     rows, lanes = state.shape
-    vmem = pl.BlockSpec(memory_space=pltpu.VMEM)
+    vmem, smem = pl.BlockSpec(memory_space=pltpu.VMEM), pl.BlockSpec(memory_space=pltpu.SMEM)
     shape = jax.ShapeDtypeStruct((rows // parts * len(flips), lanes), jnp.bfloat16)
+    memory = jax.ShapeDtypeStruct(total.shape, jnp.bfloat16)
     return pl.pallas_call(
-        functools.partial(first_kernel, heads, width, parts, flips),
-        in_specs=[pl.BlockSpec(memory_space=pltpu.SMEM)] + [vmem] * 4,
-        out_specs=[vmem] * 3,
-        out_shape=[shape] * 3,
-        scratch_shapes=[pltpu.VMEM((rows, lanes), jnp.float32)],
-        compiler_params=pltpu.CompilerParams(vmem_limit_bytes=12 << 20),
+        functools.partial(first_kernel, heads, width, flips, parts),
+        in_specs=[smem, smem] + [vmem] * 5 + [pl.BlockSpec(memory_space=pltpu.HBM)],
+        out_specs=[vmem] * 5,
+        out_shape=[shape] * 3 + [memory] * 2,
+        scratch_shapes=[
+            pltpu.VMEM(wo.shape, wo.dtype),
+            pltpu.VMEM((rows, lanes), jnp.float32),
+            pltpu.SemaphoreType.DMA((heads,)),
+        ],
+        compiler_params=pltpu.CompilerParams(vmem_limit_bytes=16 << 20),
         cost_estimate=pl.CostEstimate(
             flops=2 * rows * wo.size,
             transcendentals=rows * heads * width,
             bytes_accessed=2 * wo.size + 4 * rows * lanes,
         ),
-    )(me, state, lifted, wo, memory)
+    )(me, coef, state, lifted, total, got, early, wo)
 
 
 def wide_kernel(heads, width, slices, place_ref, state_ref, wq_ref, wo_ref, m_ref, mx_ref, *rest):
@@ -285,33 +314,64 @@
     return lax.ppermute(x, axis, [(i, i ^ flip) for i in range(lax.axis_size(axis))])
 
 
-def scan_memory(own, decay, axis, beside):
+def combine_kernel(heads, coef_ref, total_ref, got_ref, prior_ref, new_total_ref, new_prior_ref):
+    for h in range(heads):
+        got = got_ref[h].astype(jnp.float32)
+        new_total_ref[h] = (
+            coef_ref[0, h] * total_ref[h].astype(jnp.float32) + coef_ref[1, h] * got
+        ).astype(jnp.bfloat16)
+        new_prior_ref[h] = (coef_ref[2, h] * got + prior_ref[h].astype(jnp.float32)).astype(jnp.bfloat16)
+
+
+def combine(coef, total, got, prior):
+    vmem = pl.BlockSpec(memory_space=pltpu.VMEM)
+    return pl.pallas_call(
+        functools.partial(combine_kernel, total.shape[0]),
+        in_specs=[pl.BlockSpec(memory_space=pltpu.SMEM)] + [vmem] * 3,
+        out_specs=[vmem] * 2,
+        out_shape=[jax.ShapeDtypeStruct(total.shape, jnp.bfloat16)] * 2,
+        compiler_params=pltpu.CompilerParams(vmem_limit_bytes=8 << 20),
+        cost_estimate=pl.CostEstimate(flops=4 * total.size, transcendentals=0, bytes_accessed=10 * total.size),
+    )(coef, total, got, prior)
+
+
+def scan_levels(decay, axis):
     count, me = lax.axis_size(axis), lax.axis_index(axis)
-    shape = own.shape
-    total, prior = own, jnp.zeros_like(own)
     order = jnp.arange(count)
+    levels = []
     level = 1
     while level < count:
         mine = (order // level) == (me // level)
         theirs = (order // level) == ((me ^ level) // level)
 
         def product(mask):
-            return jnp.prod(jnp.where(mask[:, None], decay, 1.0), axis=0)[:, None, None]
-
-        got = partner(total, axis, level)
-        if 2 * level >= count:
-            extra = beside(total)
-            got, extra = lax.optimization_barrier((got, extra))
-        got = got.astype(jnp.float32)
+            return jnp.prod(jnp.where(mask[:, None], decay, 1.0), axis=0)
+
         later = (me & level) != 0
-        before_me = product(mine & (order < me))
-        kept = total.astype(jnp.float32)
-        prior = jnp.where(later, before_me * got + prior.astype(jnp.float32), prior.astype(jnp.float32)).astype(
-            jnp.bfloat16
+        one = jnp.ones_like(decay[0])
+        levels.append(
+            (
+                level,
+                jnp.stack(
+                    [
+                        jnp.where(later, one, product(theirs)),
+                        jnp.where(later, product(mine), one),
+                        jnp.where(later, product(mine & (order < me)), 0.0 * one),
+                    ]
+                ),
+            )
         )
-        total = jnp.where(later, product(mine) * got + kept, product(theirs) * kept + got).astype(jnp.bfloat16)
         level *= 2
-    return total, prior, extra
+    return levels
+
+
+def scan_memory(own, levels, axis, beside):
+    total, prior = own, jnp.zeros_like(own)
+    for level, coef in levels[:-1]:
+        total, prior = combine(coef, total, partner(total, axis, level), prior)
+    got = partner(total, axis, levels[-1][0])
+    got, extra = lax.optimization_barrier((got, beside(total)))
+    return total, got, prior, extra
 
 
 def widen(held, axis, flip):
@@ -356,16 +416,18 @@
     query_block = partner(query_block, "sub", 1)
     output_block = partner(output_block, "sub", 1)
 
+    levels = scan_levels(decay, "seq")
+
     def scan():
         return scan_memory(
-            own, decay, "seq", lambda event: lifted_query(after(summary, event), wq_sum)
+            own, levels, "seq", lambda event: lifted_query(after(summary, event), wq_sum)
         )
 
     def skip():
         empty = jnp.zeros((heads, width + PAD, width), jnp.bfloat16)
-        return empty, empty, jnp.zeros((summary.shape[0], heads * width), jnp.bfloat16)
-
-    final, prior, lifted = lax.cond(gate[0] == gate[0], scan, skip)
+        return empty, empty, empty, jnp.zeros((summary.shape[0], heads * width), jnp.bfloat16)
+
+    total, got, early, lifted = lax.cond(gate[0] == gate[0], scan, skip)
 
     chunk = 512
 
@@ -387,8 +449,8 @@
         terms = [terms[0]] + [swap(t, f) for t, f in zip(terms[1:], flips[1:])]
         return (state.astype(jnp.float32) + wide_sum(terms)).astype(jnp.bfloat16)
 
-    state, kept, sent = first_step(
-        me.reshape(1), summary, lifted, wo_sum, final, heads, width, parts, flips
+    state, kept, sent, final, prior = first_step(
+        me.reshape(1), levels[-1][1], summary, lifted, total, got, early, wo_sum, heads, width, parts, flips
     )
     got = partner(sent, "sub", 1)
     query_other = partner(after(query_block, kept), *QUERY_STAGES[0])

time: 87 us -> 85.9 us (0.987)
  other arithmetic: 5.2 us -> 1.07 us
  waiting for transfers between devices: 16.3 us -> 19.1 us
  Pallas kernels: 35.8 us -> 36.7 us
    convert_element_type x2 -> x0, other arithmetic: 4.22 us -> none  [the longest x1 2.2 us: scan_memory(): jnp.where(later, before_me * got + prior.astype(jnp.float32), prior.astyp...]
    ppermute x17, waiting for transfers between devices: 16.3 us -> 19.1 us  [partner(): lax.ppermute(x, axis, [(i, i ^ flip) for i in range(lax.axis_size(axis))])]
    pallas_call x1 -> x2, Pallas kernels: 1.69 us -> 4.41 us  [the longest x1 2.62 us: first_step(): pl.pallas_call(functools.partial(first_kernel, heads, width, flips, parts...]
    pallas_call x4, Pallas kernels: 19.1 us -> 17.3 us  [attention_piece(): pl.pallas_call(functools.partial(attention_kernel, heads, head, width, fi...]
  transfers between devices with their start and end apart: 17 -> 17, of which waited for: 8 -> 8; matrix products, arithmetic and copies ran while one was open for 5% -> 0% of each run, Pallas kernels for 27% -> 29%
where the time goes in v5:
time: 85.9 us; the launch traced here: 85.6 us
  Pallas kernels  36.7 us (43%)
  starting transfers between devices  23.5 us (27%)
  waiting for transfers between devices  19.1 us (22%)
  local copies, waits for them, and re-layouts  4.19 us (5%)
  other arithmetic  1.07 us (1%)
  between operations  1.02 us (1%)
    ppermute x17, starting transfers between devices, partner(): lax.ppermute(x, axis, [(i, i ^ flip) for i in range(lax.axis_size(axis))])  23.5 us
    ppermute x17, waiting for transfers between devices, partner(): lax.ppermute(x, axis, [(i, i ^ flip) for i in range(lax.axis_size(axis))])  19.1 us
    pallas_call x4, Pallas kernels, attention_piece(): pl.pallas_call(functools.partial(attention_kernel, heads, head, width, fi...  17.3 us
    pallas_call x3, Pallas kernels, wide_step(): pl.pallas_call(functools.partial(wide_kernel, heads, width, slices), in_s...  7.1 us
    pallas_call x1, Pallas kernels, memory_update(): pl.pallas_call(functools.partial(update_kernel, heads, width, UPDATE_ROWS...  4.91 us
    unnamed x22, local copies, waits for them, and re-layouts  4.06 us
    pallas_call x1, Pallas kernels, lifted_query(): pl.pallas_call(query_kernel, grid=(4,), in_specs=[pl.BlockSpec((rows, blo...  2.92 us
    pallas_call x1, Pallas kernels, first_step(): pl.pallas_call(functools.partial(first_kernel, heads, width, flips, parts...  2.62 us
  transfers between devices with their start and end apart: 17, of which 8 were waited for; matrix products, arithmetic and copies ran while one was open for 0% of the time, Pallas kernels for 29%

profile of v5, /device:TPU:0, one launch (start us, length us, event | category | flops | bytes accessed | tf_op | source)
XLA Modules:
  0.0 85.6 jit_solution(10304965975862896396)
XLA Ops:
  1.2 4.9 %shard_map.95 = (bf16[2,272,256]{2,1,0:T(8,128)(2,1)}, bf16[512,512]{1,0:T(8,128)(2,1)}, bf16[512,512]{1,0:T(8,128)(2,1)}) custom-call(s32[2]{0:T(128)} %pad_add_fusion.place_ref, bf16[2048,512]{1,0:T(8,128)(2,1)} %k_ref.7, bf16[2048,512]{1,0:T(8,128)(2,1)} %v_ref.7, bf16[2048,512]{1,0:T(8,128)(2,1)} %wq_ref.5, bf16[512,2048]{1,0:T(8,128)(2,1)} %wo_ref.5), custom_call_target="tpu_custom_call" | custom-call | flops 536870912 | bytes 4194304 | tf_op jit(solution)/shard_map/pallas_call | solution.py:84
  6.1 3.1 %collective-permute-start.4 = (bf16[512,512]{1,0:T(8,128)(2,1)}, bf16[512,512]{1,0:T(8,128)(2,1)S(1)}, u32[]{:S(2)}, u32[]{:S(2)}) collective-permute-start(bf16[512,512]{1,0:T(8,128)(2,1)} %get-tuple-element.72), channel_id=1, source_target_pairs={{0,1},{1,0},{2,3},{3,2},{4,5},{5,4},{6,7},{7,6},{8,9},{9,8},{10,11... | collective-permute-start | bytes 1572872 | tf_op jit(solution)/shard_map/ppermute | solution.py:314
  9.7 12.8 %conditional.1 = (bf16[2,272,256]{2,1,0:T(8,128)(2,1)}, bf16[2,272,256]{2,1,0:T(8,128)(2,1)}, bf16[2,272,256]{2,1,0:T(8,128)(2,1)S(1)}, bf16[64,512]{1,0:T(8,128)(2,1)S(1)}) conditional(s32[]{:T(128)} %bitcast.6, () %tuple.30, (bf16[2,272,256]{2,1,0:T(8,128)(2,1)}, f32[3,2]{1,0:T(4,128)S(1)}, bf16[64,2048]{1,0:T(8,128)(2,1)}, ...), branch_computations={%region_6.7_spmd, %region_7.8_spmd} | conditional | flops 134774784 | bytes 5996658 | solution.py:430
  11.5 1.8 %branch_1_fun.2 = (bf16[2,272,256]{2,1,0:T(8,128)(2,1)}, bf16[2,272,256]{2,1,0:T(8,128)(2,1)S(1)}) custom-call(f32[3,2]{1,0:T(4,128)S(1)} %get-tuple-element.8.coef_ref, bf16[2,272,256]{2,1,0:T(8,128)(2,1)} %get-tuple-element.9.total_ref, bf16[2,272,256]{2,1,0:T(8,128)(2,1)S(1)} %collective-permute-done.got_ref, ...), custom_call_target="tpu_custom_call" | custom-call | flops 557056 | bytes 1392640 | tf_op jit(solution)/shard_map/cond/branch_1_fun/pallas_call | solution.py:328
  13.3 1.9 %collective-permute-start.1 = (bf16[2,272,256]{2,1,0:T(8,128)(2,1)}, bf16[2,272,256]{2,1,0:T(8,128)(2,1)}, u32[]{:S(2)}, u32[]{:S(2)}) collective-permute-start(bf16[2,272,256]{2,1,0:T(8,128)(2,1)} %get-tuple-element.129), channel_id=1, source_target_pairs={{0,8},{4,12},{8,0},{12,4},{1,9},{5,13},{9,1},{13,5},{2,10},{6,14},... | collective-permute-start | bytes 835592 | tf_op jit(solution)/shard_map/cond/branch_1_fun/ppermute | solution.py:314
  15.2 2.9 %branch_1_fun.3 = bf16[64,512]{1,0:T(8,128)(2,1)S(1)} custom-call(bf16[64,2048]{1,0:T(8,128)(2,1)} %get-tuple-element.12.s_ref, bf16[2048,512]{1,0:T(8,128)(2,1)} %get-tuple-element.13.w_ref), custom_call_target="tpu_custom_call" | custom-call | flops 134217728 | bytes 2097152 | tf_op jit(solution)/shard_map/cond/branch_1_fun/pallas_call | solution.py:114
  18.1 4.3 %collective-permute-done.1 = bf16[2,272,256]{2,1,0:T(8,128)(2,1)} collective-permute-done((bf16[2,272,256]{2,1,0:T(8,128)(2,1)}, bf16[2,272,256]{2,1,0:T(8,128)(2,1)}, u32[]{:S(2)}, u32[]{:S(2)}) %collective-permute-start.1) | collective-permute-done | bytes 278560 | tf_op jit(solution)/shard_map/cond/branch_1_fun/ppermute | solution.py:314
  24.2 2.6 %shard_map.96 = (bf16[32,2048]{1,0:T(8,128)(2,1)S(1)}, bf16[32,2048]{1,0:T(8,128)(2,1)S(1)}, bf16[32,2048]{1,0:T(8,128)(2,1)S(1)}, bf16[2,272,256]{2,1,0:T(8,128)(2,1)S(1)}, bf16[2,272,256]{2,1,0:T(8,128)(2,1)S(1)}) custom-call(s32[1]{0:T(128)} %bitcast.2.me_ref, f32[3,2]{1,0:T(4,128)S(1)} %pad_maximum_fusion.coef_ref, bf16[64,2048]{1,0:T(8,128)(2,1)} %state_ref.1, ...), custom_call_target="tpu_custom_call" | custom-call | flops 134217728 | bytes 2621440 | tf_op jit(solution)/shard_map/pallas_call | solution.py:257
  26.9 1.9 %collective-permute-start.2 = (bf16[32,2048]{1,0:T(8,128)(2,1)S(1)}, bf16[32,2048]{1,0:T(8,128)(2,1)S(1)}, u32[]{:S(2)}, u32[]{:S(2)}) collective-permute-start(bf16[32,2048]{1,0:T(8,128)(2,1)S(1)} %get-tuple-element.69), channel_id=1, source_target_pairs={{0,1},{1,0},{2,3},{3,2},{4,5},{5,4},{6,7},{7,6},{8,9},{9,8},{10,11... | collective-permute-start | bytes 393224 | tf_op jit(solution)/shard_map/ppermute | solution.py:314
  29.0 1.8 %collective-permute-start.5 = (bf16[512,512]{1,0:T(8,128)(2,1)S(1)}, bf16[512,512]{1,0:T(8,128)(2,1)S(1)}, u32[]{:S(2)}, u32[]{:S(2)}) collective-permute-start(bf16[512,512]{1,0:T(8,128)(2,1)S(1)} %collective-permute-done.4.rest_0_), channel_id=1, source_target_pairs={{0,16},{16,0},{1,17},{17,1},{2,18},{18,2},{3,19},{19,3},{4,20},{20... | collective-permute-start | bytes 1572872 | tf_op jit(solution)/shard_map/ppermute | solution.py:314
  30.7 2.7 %collective-permute-done.6.rest_4_ = bf16[512,512]{1,0:T(8,128)(2,1)S(1)} collective-permute-done((bf16[512,512]{1,0:T(8,128)(2,1)}, bf16[512,512]{1,0:T(8,128)(2,1)S(1)}, u32[]{:S(2)}, u32[]{:S(2)}) %collective-permute-start.6) | collective-permute-done | bytes 524320 | tf_op jit(solution)/shard_map/ppermute | solution.py:314
  33.4 2.0 %collective-permute-start.7 = (bf16[512,512]{1,0:T(8,128)(2,1)S(1)}, bf16[512,512]{1,0:T(8,128)(2,1)S(1)}, u32[]{:S(2)}, u32[]{:S(2)}) collective-permute-start(bf16[512,512]{1,0:T(8,128)(2,1)S(1)} %collective-permute-done.6.rest_4_), channel_id=1, source_target_pairs={{0,8},{4,12},{8,0},{12,4},{1,9},{5,13},{9,1},{13,5},{2,10},{6,14},... | collective-permute-start | bytes 1572872 | tf_op jit(solution)/shard_map/ppermute | solution.py:314
  36.3 4.2 %collective-permute-start.3 = (bf16[32,2048]{1,0:T(8,128)(2,1)S(1)}, bf16[32,2048]{1,0:T(8,128)(2,1)S(1)}, u32[]{:S(2)}, u32[]{:S(2)}) collective-permute-start(bf16[32,2048]{1,0:T(8,128)(2,1)S(1)} %add_convert_fusion.4), channel_id=1, source_target_pairs={{0,3},{1,2},{2,1},{3,0},{4,7},{5,6},{6,5},{7,4},{8,11},{9,10},{10,... | collective-permute-start | bytes 393224 | tf_op jit(solution)/shard_map/ppermute | solution.py:314
  42.0 3.8 %shard_map.97.rest_0_ = bf16[2048,512]{1,0:T(8,128)(2,1)} custom-call(f32[2]{0:T(128)S(1)} %copy-done.6, bf16[2048,512]{1,0:T(8,128)(2,1)S(1)} %copy-done.4, bf16[2048,512]{1,0:T(8,128)(2,1)S(1)} %copy-done, bf16[2048,512]{1,0:T(8,128)(2,1)S(1)} %copy-done.1, bf16[2,272,256]{2,1,0:T(8,128)(2,1)S(1)} %get-tuple-element.71.m_ref), custom_call_target="tpu_custom_call" | custom-call | flops 1073741824 | bytes 3145728 | tf_op jit(solution)/shard_map/pallas_call | solution.py:195
  47.1 2.8 %shard_map.98.rest_0_ = bf16[2048,512]{1,0:T(8,128)(2,1)} custom-call(f32[2]{0:T(128)S(1)} %copy-done.6, bf16[2048,512]{1,0:T(8,128)(2,1)S(1)} %copy-done.4, bf16[2048,512]{1,0:T(8,128)(2,1)S(1)} %copy-done, bf16[2048,512]{1,0:T(8,128)(2,1)S(1)} %copy-done.1, bf16[2,272,256]{2,1,0:T(8,128)(2,1)S(1)} %get-tuple-element.71.m_ref, ...), custom_call_target="tpu_custom_call", output_to_operand_aliasing={{}: (5, {})} | custom-call | flops 536870912 | bytes 2097152 | tf_op jit(solution)/shard_map/pallas_call | solution.py:195
  50.0 2.4 %shard_map.99 = bf16[32,2048]{1,0:T(8,128)(2,1)S(1)} custom-call(s32[2]{0:T(128)S(1)} %copy-done.7, bf16[32,2048]{1,0:T(8,128)(2,1)S(1)} %add_convert_fusion.3.state_ref, bf16[2048,512]{1,0:T(8,128)(2,1)S(1)} %copy-done.8, bf16[512,2048]{1,0:T(8,128)(2,1)S(1)} %copy-done.3, bf16[2,272,256]{2,1,0:T(8,128)(2,1)S(1)} %get-tuple-element.77.m_ref, ...), custom_call_target="tpu_custom_call" | custom-call | flops 268435456 | bytes 8650752 | tf_op jit(solution)/shard_map/pallas_call | solution.py:298
  52.4 2.7 %collective-permute-start.13 = (bf16[32,2048]{1,0:T(8,128)(2,1)S(1)}, bf16[32,2048]{1,0:T(8,128)(2,1)S(1)}, u32[]{:S(2)}, u32[]{:S(2)}) collective-permute-start(bf16[32,2048]{1,0:T(8,128)(2,1)S(1)} %shard_map.99), channel_id=1, source_target_pairs={{0,3},{1,2},{2,1},{3,0},{4,7},{5,6},{6,5},{7,4},{8,11},{9,10},{10,... | collective-permute-start | bytes 393224 | tf_op jit(solution)/shard_map/ppermute | solution.py:314
  55.1 5.7 %shard_map.100.rest_0_ = bf16[2048,512]{1,0:T(8,128)(2,1)} custom-call(f32[2]{0:T(128)S(1)} %copy-done.6, bf16[2048,512]{1,0:T(8,128)(2,1)S(1)} %copy-done.5, bf16[2048,512]{1,0:T(8,128)(2,1)S(1)} %copy-done, bf16[2048,512]{1,0:T(8,128)(2,1)S(1)} %copy-done.1, bf16[2,272,256]{2,1,0:T(8,128)(2,1)S(1)} %get-tuple-element.71.m_ref, ...), custom_call_target="tpu_custom_call", output_to_operand_aliasing={{}: (5, {})} | custom-call | flops 2147483648 | bytes 5242880 | tf_op jit(solution)/shard_map/pallas_call | solution.py:195
  60.9 2.4 %shard_map.101 = bf16[32,2048]{1,0:T(8,128)(2,1)S(1)} custom-call(s32[2]{0:T(128)S(1)} %copy-done.7, bf16[32,2048]{1,0:T(8,128)(2,1)S(1)} %add_convert_fusion.2.state_ref, bf16[2048,512]{1,0:T(8,128)(2,1)S(1)} %copy-done.8, bf16[512,2048]{1,0:T(8,128)(2,1)S(1)} %copy-done.3, bf16[2,272,256]{2,1,0:T(8,128)(2,1)S(1)} %get-tuple-element.77.m_ref, ...), custom_call_target="tpu_custom_call" | custom-call | flops 268435456 | bytes 8650752 | tf_op jit(solution)/shard_map/pallas_call | solution.py:298
  64.9 5.0 %shard_map.102 = bf16[2048,512]{1,0:T(8,128)(2,1)} custom-call(f32[2]{0:T(128)S(1)} %copy-done.6, bf16[2048,512]{1,0:T(8,128)(2,1)S(1)} %copy-done.5, bf16[2048,512]{1,0:T(8,128)(2,1)S(1)} %copy-done, bf16[2048,512]{1,0:T(8,128)(2,1)S(1)} %copy-done.1, bf16[2,272,256]{2,1,0:T(8,128)(2,1)S(1)} %get-tuple-element.71.m_ref, ...), custom_call_target="tpu_custom_call", output_to_operand_aliasing={{}: (5, {})} | custom-call | flops 1610612736 | bytes 4194304 | tf_op jit(solution)/shard_map/pallas_call | solution.py:195
  70.5 2.4 %shard_map.103 = bf16[32,2048]{1,0:T(8,128)(2,1)S(1)} custom-call(s32[2]{0:T(128)S(1)} %copy-done.7, bf16[32,2048]{1,0:T(8,128)(2,1)S(1)} %add_convert_fusion.1.state_ref, bf16[2048,512]{1,0:T(8,128)(2,1)S(1)} %copy-done.8, bf16[512,2048]{1,0:T(8,128)(2,1)S(1)} %copy-done.3, bf16[2,272,256]{2,1,0:T(8,128)(2,1)S(1)} %get-tuple-element.77.m_ref, ...), custom_call_target="tpu_custom_call" | custom-call | flops 268435456 | bytes 8650752 | tf_op jit(solution)/shard_map/pallas_call | solution.py:298
  72.8 1.9 %collective-permute-start.15 = (bf16[32,2048]{1,0:T(8,128)(2,1)S(1)}, bf16[32,2048]{1,0:T(8,128)(2,1)S(1)}, u32[]{:S(2)}, u32[]{:S(2)}) collective-permute-start(bf16[32,2048]{1,0:T(8,128)(2,1)S(1)} %shard_map.103), channel_id=1, source_target_pairs={{0,3},{1,2},{2,1},{3,0},{4,7},{5,6},{6,5},{7,4},{8,11},{9,10},{10,... | collective-permute-start | bytes 393224 | tf_op jit(solution)/shard_map/ppermute | solution.py:314
  74.7 5.0 %collective-permute-done.15 = bf16[32,2048]{1,0:T(8,128)(2,1)S(1)} collective-permute-done((bf16[32,2048]{1,0:T(8,128)(2,1)S(1)}, bf16[32,2048]{1,0:T(8,128)(2,1)S(1)}, u32[]{:S(2)}, u32[]{:S(2)}) %collective-permute-start.15) | collective-permute-done | bytes 131104 | tf_op jit(solution)/shard_map/ppermute | solution.py:314
  81.3 3.5 %collective-permute-done.16 = bf16[32,2048]{1,0:T(8,128)(2,1)S(1)} collective-permute-done((bf16[32,2048]{1,0:T(8,128)(2,1)S(1)}, bf16[32,2048]{1,0:T(8,128)(2,1)S(1)}, u32[]{:S(2)}, u32[]{:S(2)}) %collective-permute-start.16) | collective-permute-done | bytes 131104 | tf_op jit(solution)/shard_map/ppermute | solution.py:314
  (72 shorter events, 13.0 us)
Async XLA Ops:
  1.2 8.1 %copy-start.10 = (f32[4,2]{0,1:T(2,128)S(1)}, f32[4,2]{0,1:T(2,128)}, u32[]{:S(2)}) copy-start(f32[4,2]{0,1:T(2,128)} %param.13) | copy-start | bytes 100
  1.2 8.4 %copy-start.6 = (f32[2]{0:T(128)S(1)}, f32[2]{0:T(128)}, u32[]{:S(2)}) copy-start(f32[2]{0:T(128)} %gate_ref.3) | copy-start | bytes 28
  6.1 22.8 %collective-permute-start.4 = (bf16[512,512]{1,0:T(8,128)(2,1)}, bf16[512,512]{1,0:T(8,128)(2,1)S(1)}, u32[]{:S(2)}, u32[]{:S(2)}) collective-permute-start(bf16[512,512]{1,0:T(8,128)(2,1)} %get-tuple-element.72), channel_id=1, source_target_pairs={{0,1},{1,0},{2,3},{3,2},{4,5},{5,4},{6,7},{7,6},{8,9},{9,8},{10,11... | collective-permute-start | bytes 1572872 | tf_op jit(solution)/shard_map/ppermute | solution.py:314
  9.2 24.2 %collective-permute-start.6 = (bf16[512,512]{1,0:T(8,128)(2,1)}, bf16[512,512]{1,0:T(8,128)(2,1)S(1)}, u32[]{:S(2)}, u32[]{:S(2)}) collective-permute-start(bf16[512,512]{1,0:T(8,128)(2,1)} %get-tuple-element.74), channel_id=1, source_target_pairs={{0,1},{1,0},{2,3},{3,2},{4,5},{5,4},{6,7},{7,6},{8,9},{9,8},{10,11... | collective-permute-start | bytes 1572872 | tf_op jit(solution)/shard_map/ppermute | solution.py:314
  9.7 30.8 %copy-start.1 = (bf16[2048,512]{1,0:T(8,128)(2,1)S(1)}, bf16[2048,512]{1,0:T(8,128)(2,1)}, u32[]{:S(2)}) copy-start(bf16[2048,512]{1,0:T(8,128)(2,1)} %v_ref.7) | copy-start | bytes 6291460
  9.7 1.8 %collective-permute-start = (bf16[2,272,256]{2,1,0:T(8,128)(2,1)}, bf16[2,272,256]{2,1,0:T(8,128)(2,1)S(1)}, u32[]{:S(2)}, u32[]{:S(2)}) collective-permute-start(bf16[2,272,256]{2,1,0:T(8,128)(2,1)} %get-tuple-element.9.total_ref), channel_id=1, source_target_pairs={{0,4},{4,0},{8,12},{12,8},{1,5},{5,1},{9,13},{13,9},{2,6},{6,2},{1... | collective-permute-start | bytes 835592 | tf_op jit(solution)/shard_map/cond/branch_1_fun/ppermute | solution.py:314
  13.3 9.1 %collective-permute-start.1 = (bf16[2,272,256]{2,1,0:T(8,128)(2,1)}, bf16[2,272,256]{2,1,0:T(8,128)(2,1)}, u32[]{:S(2)}, u32[]{:S(2)}) collective-permute-start(bf16[2,272,256]{2,1,0:T(8,128)(2,1)} %get-tuple-element.129), channel_id=1, source_target_pairs={{0,8},{4,12},{8,0},{12,4},{1,9},{5,13},{9,1},{13,5},{2,10},{6,14},... | collective-permute-start | bytes 835592 | tf_op jit(solution)/shard_map/cond/branch_1_fun/ppermute | solution.py:314
  22.5 17.9 %copy-start = (bf16[2048,512]{1,0:T(8,128)(2,1)S(1)}, bf16[2048,512]{1,0:T(8,128)(2,1)}, u32[]{:S(2)}) copy-start(bf16[2048,512]{1,0:T(8,128)(2,1)} %k_ref.7) | copy-start | bytes 6291460
  26.9 9.4 %collective-permute-start.2 = (bf16[32,2048]{1,0:T(8,128)(2,1)S(1)}, bf16[32,2048]{1,0:T(8,128)(2,1)S(1)}, u32[]{:S(2)}, u32[]{:S(2)}) collective-permute-start(bf16[32,2048]{1,0:T(8,128)(2,1)S(1)} %get-tuple-element.69), channel_id=1, source_target_pairs={{0,1},{1,0},{2,3},{3,2},{4,5},{5,4},{6,7},{7,6},{8,9},{9,8},{10,11... | collective-permute-start | bytes 393224 | tf_op jit(solution)/shard_map/ppermute | solution.py:314
  28.7 17.6 %collective-permute-start.8 = (bf16[2,272,256]{2,1,0:T(8,128)(2,1)S(1)}, bf16[2,272,256]{2,1,0:T(8,128)(2,1)S(1)}, u32[]{:S(2)}, u32[]{:S(2)}) collective-permute-start(bf16[2,272,256]{2,1,0:T(8,128)(2,1)S(1)} %get-tuple-element.77.m_ref), channel_id=1, source_target_pairs={{0,1},{1,0},{2,3},{3,2},{4,5},{5,4},{6,7},{7,6},{8,9},{9,8},{10,11... | collective-permute-start | bytes 835592 | tf_op jit(solution)/shard_map/ppermute | solution.py:314
  29.0 17.4 %collective-permute-start.5 = (bf16[512,512]{1,0:T(8,128)(2,1)S(1)}, bf16[512,512]{1,0:T(8,128)(2,1)S(1)}, u32[]{:S(2)}, u32[]{:S(2)}) collective-permute-start(bf16[512,512]{1,0:T(8,128)(2,1)S(1)} %collective-permute-done.4.rest_0_), channel_id=1, source_target_pairs={{0,16},{16,0},{1,17},{17,1},{2,18},{18,2},{3,19},{19,3},{4,20},{20... | collective-permute-start | bytes 1572872 | tf_op jit(solution)/shard_map/ppermute | solution.py:314
  33.4 13.0 %collective-permute-start.7 = (bf16[512,512]{1,0:T(8,128)(2,1)S(1)}, bf16[512,512]{1,0:T(8,128)(2,1)S(1)}, u32[]{:S(2)}, u32[]{:S(2)}) collective-permute-start(bf16[512,512]{1,0:T(8,128)(2,1)S(1)} %collective-permute-done.6.rest_4_), channel_id=1, source_target_pairs={{0,8},{4,12},{8,0},{12,4},{1,9},{5,13},{9,1},{13,5},{2,10},{6,14},... | collective-permute-start | bytes 1572872 | tf_op jit(solution)/shard_map/ppermute | solution.py:314
  36.3 10.1 %collective-permute-start.3 = (bf16[32,2048]{1,0:T(8,128)(2,1)S(1)}, bf16[32,2048]{1,0:T(8,128)(2,1)S(1)}, u32[]{:S(2)}, u32[]{:S(2)}) collective-permute-start(bf16[32,2048]{1,0:T(8,128)(2,1)S(1)} %add_convert_fusion.4), channel_id=1, source_target_pairs={{0,3},{1,2},{2,1},{3,0},{4,7},{5,6},{6,5},{7,4},{8,11},{9,10},{10,... | collective-permute-start | bytes 393224 | tf_op jit(solution)/shard_map/ppermute | solution.py:314
  45.8 4.2 %collective-permute-start.11 = (bf16[512,512]{1,0:T(8,128)(2,1)S(1)}, bf16[512,512]{1,0:T(8,128)(2,1)S(1)}, u32[]{:S(2)}, u32[]{:S(2)}) collective-permute-start(bf16[512,512]{1,0:T(8,128)(2,1)S(1)} %collective-permute-done.6.rest_4_), channel_id=1, source_target_pairs={{0,4},{4,0},{8,12},{12,8},{1,5},{5,1},{9,13},{13,9},{2,6},{6,2},{1... | collective-permute-start | bytes 1572872 | tf_op jit(solution)/shard_map/ppermute | solution.py:314
  46.4 3.6 %collective-permute-start.9 = (bf16[512,512]{1,0:T(8,128)(2,1)S(1)}, bf16[512,512]{1,0:T(8,128)(2,1)S(1)}, u32[]{:S(2)}, u32[]{:S(2)}) collective-permute-start(bf16[512,512]{1,0:T(8,128)(2,1)S(1)} %collective-permute-done.4.rest_0_), channel_id=1, source_target_pairs={{0,4},{4,0},{8,12},{12,8},{1,5},{5,1},{9,13},{13,9},{2,6},{6,2},{1... | collective-permute-start | bytes 1572872 | tf_op jit(solution)/shard_map/ppermute | solution.py:314
  46.4 3.6 %collective-permute-start.10 = (bf16[512,512]{1,0:T(8,128)(2,1)S(1)}, bf16[512,512]{1,0:T(8,128)(2,1)S(1)}, u32[]{:S(2)}, u32[]{:S(2)}) collective-permute-start(bf16[512,512]{1,0:T(8,128)(2,1)S(1)} %collective-permute-done.5.rest_1_), channel_id=1, source_target_pairs={{0,4},{4,0},{8,12},{12,8},{1,5},{5,1},{9,13},{13,9},{2,6},{6,2},{1... | collective-permute-start | bytes 1572872 | tf_op jit(solution)/shard_map/ppermute | solution.py:314
  46.9 3.1 %collective-permute-start.12 = (bf16[512,512]{1,0:T(8,128)(2,1)S(1)}, bf16[512,512]{1,0:T(8,128)(2,1)S(1)}, u32[]{:S(2)}, u32[]{:S(2)}) collective-permute-start(bf16[512,512]{1,0:T(8,128)(2,1)S(1)} %collective-permute-done.7.rest_5_), channel_id=1, source_target_pairs={{0,4},{4,0},{8,12},{12,8},{1,5},{5,1},{9,13},{13,9},{2,6},{6,2},{1... | collective-permute-start | bytes 1572872 | tf_op jit(solution)/shard_map/ppermute | solution.py:314
  47.0 3.0 %copy-start.3 = (bf16[512,2048]{1,0:T(8,128)(2,1)S(1)}, bf16[512,2048]{1,0:T(8,128)(2,1)}, u32[]{:S(2)}) copy-start(bf16[512,2048]{1,0:T(8,128)(2,1)} %wo_ref.5) | copy-start | bytes 6291460
  47.0 3.0 %copy-start.7 = (s32[2]{0:T(128)S(1)}, s32[2]{0:T(128)}, u32[]{:S(2)}) copy-start(s32[2]{0:T(128)} %pad_add_fusion.place_ref) | copy-start | bytes 28
  50.0 5.2 %copy-start.5 = (bf16[2048,512]{1,0:T(8,128)(2,1)S(1)}, bf16[2048,512]{1,0:T(8,128)(2,1)}, u32[]{:S(2)}) copy-start(bf16[2048,512]{1,0:T(8,128)(2,1)} %q_ref.7) | copy-start | bytes 6291460
  52.4 8.4 %collective-permute-start.13 = (bf16[32,2048]{1,0:T(8,128)(2,1)S(1)}, bf16[32,2048]{1,0:T(8,128)(2,1)S(1)}, u32[]{:S(2)}, u32[]{:S(2)}) collective-permute-start(bf16[32,2048]{1,0:T(8,128)(2,1)S(1)} %shard_map.99), channel_id=1, source_target_pairs={{0,3},{1,2},{2,1},{3,0},{4,7},{5,6},{6,5},{7,4},{8,11},{9,10},{10,... | collective-permute-start | bytes 393224 | tf_op jit(solution)/shard_map/ppermute | solution.py:314
  63.3 7.1 %collective-permute-start.14 = (bf16[32,2048]{1,0:T(8,128)(2,1)S(1)}, bf16[32,2048]{1,0:T(8,128)(2,1)S(1)}, u32[]{:S(2)}, u32[]{:S(2)}) collective-permute-start(bf16[32,2048]{1,0:T(8,128)(2,1)S(1)} %shard_map.101), channel_id=1, source_target_pairs={{0,3},{1,2},{2,1},{3,0},{4,7},{5,6},{6,5},{7,4},{8,11},{9,10},{10,... | collective-permute-start | bytes 393224 | tf_op jit(solution)/shard_map/ppermute | solution.py:314
  72.8 6.9 %collective-permute-start.15 = (bf16[32,2048]{1,0:T(8,128)(2,1)S(1)}, bf16[32,2048]{1,0:T(8,128)(2,1)S(1)}, u32[]{:S(2)}, u32[]{:S(2)}) collective-permute-start(bf16[32,2048]{1,0:T(8,128)(2,1)S(1)} %shard_map.103), channel_id=1, source_target_pairs={{0,3},{1,2},{2,1},{3,0},{4,7},{5,6},{6,5},{7,4},{8,11},{9,10},{10,... | collective-permute-start | bytes 393224 | tf_op jit(solution)/shard_map/ppermute | solution.py:314
  79.8 5.0 %collective-permute-start.16 = (bf16[32,2048]{1,0:T(8,128)(2,1)S(1)}, bf16[32,2048]{1,0:T(8,128)(2,1)S(1)}, u32[]{:S(2)}, u32[]{:S(2)}) collective-permute-start(bf16[32,2048]{1,0:T(8,128)(2,1)S(1)} %add_convert_fusion), channel_id=1, source_target_pairs={{0,1},{1,0},{2,3},{3,2},{4,5},{5,4},{6,7},{7,6},{8,9},{9,8},{10,11... | collective-permute-start | bytes 393224 | tf_op jit(solution)/shard_map/ppermute | solution.py:314
  (4 other events, 7.0 us)

commit v6 on v5

--- a/solution.py
+++ b/solution.py
@@ -25,22 +25,49 @@
     return lax.dot_general(a, b, (dims, ((), ())), preferred_element_type=jnp.float32)
 
 
-def update_kernel(
-    heads, width, block, depth, place_ref, k_hbm, v_hbm, wq_hbm, wo_hbm, u_ref, query_hbm, output_hbm,
-    k_ref, v_ref, query_ref, output_ref, acc, norm, sems
-):
+def slice_kernel(depth, pieces, place_ref, wq_hbm, wo_hbm, query_hbm, output_hbm, query_ref, output_ref, sems):
+    at = [pl.multiple_of(place_ref[i] * depth, depth) for i in range(2)]
+    tall, wide = depth // pieces, wo_hbm.shape[0] // pieces
+    moves = []
+    for i in range(pieces):
+        part, block = pl.ds(i * tall, tall), pl.ds(i * wide, wide)
+        moves.append(
+            (
+                pltpu.make_async_copy(wq_hbm.at[pl.ds(at[0] + i * tall, tall)], query_ref.at[part], sems.at[4 * i]),
+                pltpu.make_async_copy(query_ref.at[part], query_hbm.at[part], sems.at[4 * i + 1]),
+            )
+        )
+        moves.append(
+            (
+                pltpu.make_async_copy(wo_hbm.at[block, pl.ds(at[1], depth)], output_ref.at[block], sems.at[4 * i + 2]),
+                pltpu.make_async_copy(output_ref.at[block], output_hbm.at[block], sems.at[4 * i + 3]),
+            )
+        )
+    for fetch, _ in moves:
+        fetch.start()
+    for fetch, back in moves:
+        fetch.wait()
+        back.start()
+    for _, back in moves:
+        back.wait()
+
+
+def weight_slices(place, wq, wo, depth):
+    pieces = 4
+    hbm = pl.BlockSpec(memory_space=pltpu.HBM)
+    shapes = ((depth, wq.shape[1]), (wo.shape[0], depth))
+    return pl.pallas_call(
+        functools.partial(slice_kernel, depth, pieces),
+        in_specs=[pl.BlockSpec(memory_space=pltpu.SMEM), hbm, hbm],
+        out_specs=[hbm, hbm],
+        out_shape=[jax.ShapeDtypeStruct(shape, wq.dtype) for shape in shapes],
+        scratch_shapes=[pltpu.VMEM(shape, wq.dtype) for shape in shapes] + [pltpu.SemaphoreType.DMA((4 * pieces,))],
+        compiler_params=pltpu.CompilerParams(vmem_limit_bytes=60 << 20),
+    )(place, wq, wo)
+
+
+def update_kernel(heads, width, block, k_hbm, v_hbm, u_ref, k_ref, v_ref, acc, norm, sems):
     count = k_hbm.shape[0] // block
-    at = [pl.multiple_of(place_ref[i] * depth, depth) for i in range(2)]
-    slices = [
-        pltpu.make_async_copy(wq_hbm.at[pl.ds(at[0], depth), :], query_ref, sems.at[2 * count]),
-        pltpu.make_async_copy(wo_hbm.at[:, pl.ds(at[1], depth)], output_ref, sems.at[2 * count + 1]),
-    ]
-    backs = [
-        pltpu.make_async_copy(query_ref, query_hbm, sems.at[2 * count + 2]),
-        pltpu.make_async_copy(output_ref, output_hbm, sems.at[2 * count + 3]),
-    ]
-    for copy in slices:
-        copy.start()
     copies = []
     for i in range(count):
         part = pl.ds(i * block, block)
@@ -55,10 +82,6 @@
         part = slice(i * block, (i + 1) * block)
         copies[i][0].wait()
         copies[i][1].wait()
-        if i == 0:
-            for copy, back in zip(slices, backs):
-                copy.wait()
-                back.start()
         for h in range(heads):
             cols = slice(h * width, (h + 1) * width)
             lifted = lift(k_ref[part, cols].astype(jnp.float32))
@@ -73,39 +96,31 @@
     for h in range(heads):
         u_ref[h, :width, :] = acc[h].astype(jnp.bfloat16)
         u_ref[h, width:, :] = jnp.broadcast_to(norm[h, 0:1, :], (PAD, width)).astype(jnp.bfloat16)
-    for copy in backs:
-        copy.wait()
-
-
-def memory_update(place, keys, values, wq, wo, depth, heads, width):
+
+
+def memory_update(keys, values, heads, width):
     rows, lanes = keys.shape
     count = rows // UPDATE_ROWS
     hbm = pl.BlockSpec(memory_space=pltpu.HBM)
     return pl.pallas_call(
-        functools.partial(update_kernel, heads, width, UPDATE_ROWS, depth),
-        in_specs=[pl.BlockSpec(memory_space=pltpu.SMEM)] + [hbm] * 4,
-        out_specs=[pl.BlockSpec(memory_space=pltpu.VMEM), hbm, hbm],
-        out_shape=[
-            jax.ShapeDtypeStruct((heads, width + PAD, width), jnp.bfloat16),
-            jax.ShapeDtypeStruct((depth, wq.shape[1]), wq.dtype),
-            jax.ShapeDtypeStruct((wo.shape[0], depth), wo.dtype),
-        ],
+        functools.partial(update_kernel, heads, width, UPDATE_ROWS),
+        in_specs=[hbm, hbm],
+        out_specs=pl.BlockSpec(memory_space=pltpu.VMEM),
+        out_shape=jax.ShapeDtypeStruct((heads, width + PAD, width), jnp.bfloat16),
         scratch_shapes=[
             pltpu.VMEM((rows, lanes), jnp.bfloat16),
             pltpu.VMEM((rows, lanes), jnp.bfloat16),
-            pltpu.VMEM((depth, wq.shape[1]), wq.dtype),
-            pltpu.VMEM((wo.shape[0], depth), wo.dtype),
             pltpu.VMEM((heads, width, width), jnp.float32),
             pltpu.VMEM((heads, 8, width), jnp.float32),
-            pltpu.SemaphoreType.DMA((2 * count + 4,)),
+            pltpu.SemaphoreType.DMA((2 * count,)),
         ],
-        compiler_params=pltpu.CompilerParams(vmem_limit_bytes=60 << 20),
+        compiler_params=pltpu.CompilerParams(vmem_limit_bytes=12 << 20),
         cost_estimate=pl.CostEstimate(
             flops=2 * rows * heads * width * width,
             transcendentals=rows * heads * width,
             bytes_accessed=4 * rows * heads * width,
         ),
-    )(place, keys, values, wq, wo)
+    )(keys, values)
 
 
 def lifted_query(state, wq):
@@ -410,15 +425,14 @@
 
     depth = model >> len(QUERY_STAGES)
     place = jnp.stack([slice_index(QUERY_STAGES), slice_index(OUTPUT_STAGES)])
-    own, query_block, output_block = memory_update(
-        place, keys, values, wq_sum, wo_sum, depth, heads, width
-    )
+    query_block, output_block = weight_slices(place, wq_sum, wo_sum, depth)
     query_block = partner(query_block, "sub", 1)
     output_block = partner(output_block, "sub", 1)
 
     levels = scan_levels(decay, "seq")
 
     def scan():
+        own = memory_update(keys, values, heads, width)
         return scan_memory(
             own, levels, "seq", lambda event: lifted_query(after(summary, event), wq_sum)
         )

time: 85.9 us -> 83.8 us (0.976)
  local copies, waits for them, and re-layouts: 4.19 us -> 0.87 us
  waiting for transfers between devices: 19.1 us -> 20.4 us
    unnamed x22 -> x18, local copies, waits for them, and re-layouts: 4.06 us -> 0.73 us
    pallas_call x0 -> x1, Pallas kernels: none -> 2.88 us  [weight_slices(): pl.pallas_call(functools.partial(slice_kernel, depth, pieces), in_specs=[...]
    pallas_call x1, Pallas kernels: 2.92 us -> 1.01 us  [lifted_query(): pl.pallas_call(query_kernel, grid=(4,), in_specs=[pl.BlockSpec((rows, blo...]
    pallas_call x1, Pallas kernels: 4.91 us -> 3.2 us  [memory_update(): pl.pallas_call(functools.partial(update_kernel, heads, width, UPDATE_ROWS...]
    ppermute x17, waiting for transfers between devices: 19.1 us -> 20.4 us  [partner(): lax.ppermute(x, axis, [(i, i ^ flip) for i in range(lax.axis_size(axis))])]
    pallas_call x4, Pallas kernels: 17.3 us -> 18.4 us  [attention_piece(): pl.pallas_call(functools.partial(attention_kernel, heads, head, width, fi...]
  transfers between devices with their start and end apart: 17 -> 17, of which waited for: 8 -> 8; matrix products, arithmetic and copies ran while one was open for 0% -> 0% of each run, Pallas kernels for 29% -> 32%
where the time goes in v6:
time: 83.8 us; the launch traced here: 83.6 us
  Pallas kernels  36.7 us (44%)
  starting transfers between devices  23.4 us (28%)
  waiting for transfers between devices  20.4 us (24%)
  other arithmetic  1.11 us (1%)
  between operations  1.01 us (1%)
  local copies, waits for them, and re-layouts  0.87 us (1%)
    ppermute x17, starting transfers between devices, partner(): lax.ppermute(x, axis, [(i, i ^ flip) for i in range(lax.axis_size(axis))])  23.4 us
    ppermute x17, waiting for transfers between devices, partner(): lax.ppermute(x, axis, [(i, i ^ flip) for i in range(lax.axis_size(axis))])  20.4 us
    pallas_call x4, Pallas kernels, attention_piece(): pl.pallas_call(functools.partial(attention_kernel, heads, head, width, fi...  18.4 us
    pallas_call x3, Pallas kernels, wide_step(): pl.pallas_call(functools.partial(wide_kernel, heads, width, slices), in_s...  7.09 us
    pallas_call x1, Pallas kernels, memory_update(): pl.pallas_call(functools.partial(update_kernel, heads, width, UPDATE_ROWS...  3.2 us
    pallas_call x1, Pallas kernels, weight_slices(): pl.pallas_call(functools.partial(slice_kernel, depth, pieces), in_specs=[...  2.88 us
    pallas_call x1, Pallas kernels, first_step(): pl.pallas_call(functools.partial(first_kernel, heads, width, flips, parts...  2.77 us
  transfers between devices with their start and end apart: 17, of which 8 were waited for; matrix products, arithmetic and copies ran while one was open for 0% of the time, Pallas kernels for 32%

profile of v6, /device:TPU:0, one launch (start us, length us, event | category | flops | bytes accessed | tf_op | source)
XLA Modules:
  0.0 83.6 jit_solution(6621823035335685540)
XLA Ops:
  1.3 2.9 %shard_map.97 = (bf16[512,512]{1,0:T(8,128)(2,1)}, bf16[512,512]{1,0:T(8,128)(2,1)}) custom-call(s32[2]{0:T(128)} %pad_add_fusion.place_ref, bf16[2048,512]{1,0:T(8,128)(2,1)} %wq_ref.5, bf16[512,2048]{1,0:T(8,128)(2,1)} %wo_ref.5), custom_call_target="tpu_custom_call" | custom-call | tf_op jit(solution)/shard_map/pallas_call | solution.py:59
  4.1 3.1 %collective-permute-start.4 = (bf16[512,512]{1,0:T(8,128)(2,1)}, bf16[512,512]{1,0:T(8,128)(2,1)S(1)}, u32[]{:S(2)}, u32[]{:S(2)}) collective-permute-start(bf16[512,512]{1,0:T(8,128)(2,1)} %get-tuple-element.73), channel_id=1, source_target_pairs={{0,1},{1,0},{2,3},{3,2},{4,5},{5,4},{6,7},{7,6},{8,9},{9,8},{10,11... | collective-permute-start | bytes 1572872 | tf_op jit(solution)/shard_map/ppermute | solution.py:329
  7.7 15.4 %conditional.1 = (bf16[2,272,256]{2,1,0:T(8,128)(2,1)}, bf16[2,272,256]{2,1,0:T(8,128)(2,1)}, bf16[2,272,256]{2,1,0:T(8,128)(2,1)S(1)}, bf16[64,512]{1,0:T(8,128)(2,1)S(1)}) conditional(s32[]{:T(128)} %bitcast.6, () %tuple.30, (bf16[2048,512]{1,0:T(8,128)(2,1)}, bf16[2048,512]{1,0:T(8,128)(2,1)}, f32[3,2]{1,0:T(4,128)S(1)}, ...), branch_computations={%region_6.7_spmd, %region_7.8_spmd} | conditional | flops 671645696 | bytes 19628202 | solution.py:444
  7.7 3.2 %branch_1_fun.3.total_ref = bf16[2,272,256]{2,1,0:T(8,128)(2,1)S(1)} custom-call(bf16[2048,512]{1,0:T(8,128)(2,1)} %get-tuple-element.11.k_hbm, bf16[2048,512]{1,0:T(8,128)(2,1)} %get-tuple-element.12.v_hbm), custom_call_target="tpu_custom_call" | custom-call | flops 536870912 | bytes 4194304 | tf_op jit(solution)/shard_map/cond/branch_1_fun/pallas_call | solution.py:105
  14.0 1.9 %collective-permute-start.1 = (bf16[2,272,256]{2,1,0:T(8,128)(2,1)}, bf16[2,272,256]{2,1,0:T(8,128)(2,1)}, u32[]{:S(2)}, u32[]{:S(2)}) collective-permute-start(bf16[2,272,256]{2,1,0:T(8,128)(2,1)} %get-tuple-element.130), channel_id=1, source_target_pairs={{0,8},{4,12},{8,0},{12,4},{1,9},{5,13},{9,1},{13,5},{2,10},{6,14},... | collective-permute-start | bytes 835592 | tf_op jit(solution)/shard_map/cond/branch_1_fun/ppermute | solution.py:329
  16.8 6.3 %collective-permute-done.1 = bf16[2,272,256]{2,1,0:T(8,128)(2,1)} collective-permute-done((bf16[2,272,256]{2,1,0:T(8,128)(2,1)}, bf16[2,272,256]{2,1,0:T(8,128)(2,1)}, u32[]{:S(2)}, u32[]{:S(2)}) %collective-permute-start.1) | collective-permute-done | bytes 278560 | tf_op jit(solution)/shard_map/cond/branch_1_fun/ppermute | solution.py:329
  23.1 2.8 %shard_map.95 = (bf16[32,2048]{1,0:T(8,128)(2,1)S(1)}, bf16[32,2048]{1,0:T(8,128)(2,1)S(1)}, bf16[32,2048]{1,0:T(8,128)(2,1)S(1)}, bf16[2,272,256]{2,1,0:T(8,128)(2,1)S(1)}, bf16[2,272,256]{2,1,0:T(8,128)(2,1)S(1)}) custom-call(s32[1]{0:T(128)} %bitcast.2.me_ref, f32[3,2]{1,0:T(4,128)S(1)} %pad_maximum_fusion.coef_ref, bf16[64,2048]{1,0:T(8,128)(2,1)} %state_ref.1, ...), custom_call_target="tpu_custom_call" | custom-call | flops 134217728 | bytes 2621440 | tf_op jit(solution)/shard_map/pallas_call | solution.py:272
  25.9 1.9 %collective-permute-start.2 = (bf16[32,2048]{1,0:T(8,128)(2,1)S(1)}, bf16[32,2048]{1,0:T(8,128)(2,1)S(1)}, u32[]{:S(2)}, u32[]{:S(2)}) collective-permute-start(bf16[32,2048]{1,0:T(8,128)(2,1)S(1)} %get-tuple-element.70), channel_id=1, source_target_pairs={{0,1},{1,0},{2,3},{3,2},{4,5},{5,4},{6,7},{7,6},{8,9},{9,8},{10,11... | collective-permute-start | bytes 393224 | tf_op jit(solution)/shard_map/ppermute | solution.py:329
  28.0 1.8 %collective-permute-start.5 = (bf16[512,512]{1,0:T(8,128)(2,1)S(1)}, bf16[512,512]{1,0:T(8,128)(2,1)S(1)}, u32[]{:S(2)}, u32[]{:S(2)}) collective-permute-start(bf16[512,512]{1,0:T(8,128)(2,1)S(1)} %collective-permute-done.4.rest_0_), channel_id=1, source_target_pairs={{0,16},{16,0},{1,17},{17,1},{2,18},{18,2},{3,19},{19,3},{4,20},{20... | collective-permute-start | bytes 1572872 | tf_op jit(solution)/shard_map/ppermute | solution.py:329
  29.8 1.7 %collective-permute-done.6.rest_4_ = bf16[512,512]{1,0:T(8,128)(2,1)S(1)} collective-permute-done((bf16[512,512]{1,0:T(8,128)(2,1)}, bf16[512,512]{1,0:T(8,128)(2,1)S(1)}, u32[]{:S(2)}, u32[]{:S(2)}) %collective-permute-start.6) | collective-permute-done | bytes 524320 | tf_op jit(solution)/shard_map/ppermute | solution.py:329
  31.4 2.0 %collective-permute-start.7 = (bf16[512,512]{1,0:T(8,128)(2,1)S(1)}, bf16[512,512]{1,0:T(8,128)(2,1)S(1)}, u32[]{:S(2)}, u32[]{:S(2)}) collective-permute-start(bf16[512,512]{1,0:T(8,128)(2,1)S(1)} %collective-permute-done.6.rest_4_), channel_id=1, source_target_pairs={{0,8},{4,12},{8,0},{12,4},{1,9},{5,13},{9,1},{13,5},{2,10},{6,14},... | collective-permute-start | bytes 1572872 | tf_op jit(solution)/shard_map/ppermute | solution.py:329
  34.3 4.1 %collective-permute-start.3 = (bf16[32,2048]{1,0:T(8,128)(2,1)S(1)}, bf16[32,2048]{1,0:T(8,128)(2,1)S(1)}, u32[]{:S(2)}, u32[]{:S(2)}) collective-permute-start(bf16[32,2048]{1,0:T(8,128)(2,1)S(1)} %add_convert_fusion.4), channel_id=1, source_target_pairs={{0,3},{1,2},{2,1},{3,0},{4,7},{5,6},{6,5},{7,4},{8,11},{9,10},{10,... | collective-permute-start | bytes 393224 | tf_op jit(solution)/shard_map/ppermute | solution.py:329
  38.4 4.9 %shard_map.96.rest_0_ = bf16[2048,512]{1,0:T(8,128)(2,1)} custom-call(f32[2]{0:T(128)S(1)} %copy-done.2, bf16[2048,512]{1,0:T(8,128)(2,1)S(1)} %copy-done.1, bf16[2048,512]{1,0:T(8,128)(2,1)} %k_ref.7, bf16[2048,512]{1,0:T(8,128)(2,1)} %v_ref.7, bf16[2,272,256]{2,1,0:T(8,128)(2,1)S(1)} %get-tuple-element.72.m_ref), custom_call_target="tpu_custom_call" | custom-call | flops 1073741824 | bytes 3145728 | tf_op jit(solution)/shard_map/pallas_call | solution.py:210
  45.1 2.8 %shard_map.98.rest_0_ = bf16[2048,512]{1,0:T(8,128)(2,1)} custom-call(f32[2]{0:T(128)S(1)} %copy-done.2, bf16[2048,512]{1,0:T(8,128)(2,1)S(1)} %copy-done.1, bf16[2048,512]{1,0:T(8,128)(2,1)S(1)} %copy-done.4, bf16[2048,512]{1,0:T(8,128)(2,1)S(1)} %copy-done.5, bf16[2,272,256]{2,1,0:T(8,128)(2,1)S(1)} %get-tuple-element.72.m_ref, ...), custom_call_target="tpu_custom_call", output_to_operand_aliasing={{}: (5, {})} | custom-call | flops 536870912 | bytes 2097152 | tf_op jit(solution)/shard_map/pallas_call | solution.py:210
  48.0 2.4 %shard_map.99 = bf16[32,2048]{1,0:T(8,128)(2,1)S(1)} custom-call(s32[2]{0:T(128)S(1)} %copy-done.3, bf16[32,2048]{1,0:T(8,128)(2,1)S(1)} %add_convert_fusion.3.state_ref, bf16[2048,512]{1,0:T(8,128)(2,1)S(1)} %copy-done.6, bf16[512,2048]{1,0:T(8,128)(2,1)S(1)} %copy-done, bf16[2,272,256]{2,1,0:T(8,128)(2,1)S(1)} %get-tuple-element.78.m_ref, ...), custom_call_target="tpu_custom_call" | custom-call | flops 268435456 | bytes 8650752 | tf_op jit(solution)/shard_map/pallas_call | solution.py:313
  50.4 2.7 %collective-permute-start.13 = (bf16[32,2048]{1,0:T(8,128)(2,1)S(1)}, bf16[32,2048]{1,0:T(8,128)(2,1)S(1)}, u32[]{:S(2)}, u32[]{:S(2)}) collective-permute-start(bf16[32,2048]{1,0:T(8,128)(2,1)S(1)} %shard_map.99), channel_id=1, source_target_pairs={{0,3},{1,2},{2,1},{3,0},{4,7},{5,6},{6,5},{7,4},{8,11},{9,10},{10,... | collective-permute-start | bytes 393224 | tf_op jit(solution)/shard_map/ppermute | solution.py:329
  53.1 5.7 %shard_map.100.rest_0_ = bf16[2048,512]{1,0:T(8,128)(2,1)} custom-call(f32[2]{0:T(128)S(1)} %copy-done.2, bf16[2048,512]{1,0:T(8,128)(2,1)S(1)} %copy-done.1, bf16[2048,512]{1,0:T(8,128)(2,1)S(1)} %copy-done.4, bf16[2048,512]{1,0:T(8,128)(2,1)S(1)} %copy-done.5, bf16[2,272,256]{2,1,0:T(8,128)(2,1)S(1)} %get-tuple-element.72.m_ref, ...), custom_call_target="tpu_custom_call", output_to_operand_aliasing={{}: (5, {})} | custom-call | flops 2147483648 | bytes 5242880 | tf_op jit(solution)/shard_map/pallas_call | solution.py:210
  58.9 2.4 %shard_map.101 = bf16[32,2048]{1,0:T(8,128)(2,1)S(1)} custom-call(s32[2]{0:T(128)S(1)} %copy-done.3, bf16[32,2048]{1,0:T(8,128)(2,1)S(1)} %add_convert_fusion.2.state_ref, bf16[2048,512]{1,0:T(8,128)(2,1)S(1)} %copy-done.6, bf16[512,2048]{1,0:T(8,128)(2,1)S(1)} %copy-done, bf16[2,272,256]{2,1,0:T(8,128)(2,1)S(1)} %get-tuple-element.78.m_ref, ...), custom_call_target="tpu_custom_call" | custom-call | flops 268435456 | bytes 8650752 | tf_op jit(solution)/shard_map/pallas_call | solution.py:313
  61.3 1.7 %collective-permute-start.14 = (bf16[32,2048]{1,0:T(8,128)(2,1)S(1)}, bf16[32,2048]{1,0:T(8,128)(2,1)S(1)}, u32[]{:S(2)}, u32[]{:S(2)}) collective-permute-start(bf16[32,2048]{1,0:T(8,128)(2,1)S(1)} %shard_map.101), channel_id=1, source_target_pairs={{0,3},{1,2},{2,1},{3,0},{4,7},{5,6},{6,5},{7,4},{8,11},{9,10},{10,... | collective-permute-start | bytes 393224 | tf_op jit(solution)/shard_map/ppermute | solution.py:329
  62.9 5.0 %shard_map.102 = bf16[2048,512]{1,0:T(8,128)(2,1)} custom-call(f32[2]{0:T(128)S(1)} %copy-done.2, bf16[2048,512]{1,0:T(8,128)(2,1)S(1)} %copy-done.1, bf16[2048,512]{1,0:T(8,128)(2,1)S(1)} %copy-done.4, bf16[2048,512]{1,0:T(8,128)(2,1)S(1)} %copy-done.5, bf16[2,272,256]{2,1,0:T(8,128)(2,1)S(1)} %get-tuple-element.72.m_ref, ...), custom_call_target="tpu_custom_call", output_to_operand_aliasing={{}: (5, {})} | custom-call | flops 1610612736 | bytes 4194304 | tf_op jit(solution)/shard_map/pallas_call | solution.py:210
  68.5 2.4 %shard_map.103 = bf16[32,2048]{1,0:T(8,128)(2,1)S(1)} custom-call(s32[2]{0:T(128)S(1)} %copy-done.3, bf16[32,2048]{1,0:T(8,128)(2,1)S(1)} %add_convert_fusion.1.state_ref, bf16[2048,512]{1,0:T(8,128)(2,1)S(1)} %copy-done.6, bf16[512,2048]{1,0:T(8,128)(2,1)S(1)} %copy-done, bf16[2,272,256]{2,1,0:T(8,128)(2,1)S(1)} %get-tuple-element.78.m_ref, ...), custom_call_target="tpu_custom_call" | custom-call | flops 268435456 | bytes 8650752 | tf_op jit(solution)/shard_map/pallas_call | solution.py:313
  70.8 1.9 %collective-permute-start.15 = (bf16[32,2048]{1,0:T(8,128)(2,1)S(1)}, bf16[32,2048]{1,0:T(8,128)(2,1)S(1)}, u32[]{:S(2)}, u32[]{:S(2)}) collective-permute-start(bf16[32,2048]{1,0:T(8,128)(2,1)S(1)} %shard_map.103), channel_id=1, source_target_pairs={{0,3},{1,2},{2,1},{3,0},{4,7},{5,6},{6,5},{7,4},{8,11},{9,10},{10,... | collective-permute-start | bytes 393224 | tf_op jit(solution)/shard_map/ppermute | solution.py:329
  72.7 5.0 %collective-permute-done.15 = bf16[32,2048]{1,0:T(8,128)(2,1)S(1)} collective-permute-done((bf16[32,2048]{1,0:T(8,128)(2,1)S(1)}, bf16[32,2048]{1,0:T(8,128)(2,1)S(1)}, u32[]{:S(2)}, u32[]{:S(2)}) %collective-permute-start.15) | collective-permute-done | bytes 131104 | tf_op jit(solution)/shard_map/ppermute | solution.py:329
  79.3 3.5 %collective-permute-done.16 = bf16[32,2048]{1,0:T(8,128)(2,1)S(1)} collective-permute-done((bf16[32,2048]{1,0:T(8,128)(2,1)S(1)}, bf16[32,2048]{1,0:T(8,128)(2,1)S(1)}, u32[]{:S(2)}, u32[]{:S(2)}) %collective-permute-start.16) | collective-permute-done | bytes 131104 | tf_op jit(solution)/shard_map/ppermute | solution.py:329
  (73 shorter events, 10.7 us)
Async XLA Ops:
  1.3 6.4 %copy-start.2 = (f32[2]{0:T(128)S(1)}, f32[2]{0:T(128)}, u32[]{:S(2)}) copy-start(f32[2]{0:T(128)} %gate_ref.3) | copy-start | bytes 28
  4.1 23.9 %collective-permute-start.4 = (bf16[512,512]{1,0:T(8,128)(2,1)}, bf16[512,512]{1,0:T(8,128)(2,1)S(1)}, u32[]{:S(2)}, u32[]{:S(2)}) collective-permute-start(bf16[512,512]{1,0:T(8,128)(2,1)} %get-tuple-element.73), channel_id=1, source_target_pairs={{0,1},{1,0},{2,3},{3,2},{4,5},{5,4},{6,7},{7,6},{8,9},{9,8},{10,11... | collective-permute-start | bytes 1572872 | tf_op jit(solution)/shard_map/ppermute | solution.py:329
  7.2 24.2 %collective-permute-start.6 = (bf16[512,512]{1,0:T(8,128)(2,1)}, bf16[512,512]{1,0:T(8,128)(2,1)S(1)}, u32[]{:S(2)}, u32[]{:S(2)}) collective-permute-start(bf16[512,512]{1,0:T(8,128)(2,1)} %get-tuple-element.75), channel_id=1, source_target_pairs={{0,1},{1,0},{2,3},{3,2},{4,5},{5,4},{6,7},{7,6},{8,9},{9,8},{10,11... | collective-permute-start | bytes 1572872 | tf_op jit(solution)/shard_map/ppermute | solution.py:329
  7.7 15.4 %copy-start = (bf16[512,2048]{1,0:T(8,128)(2,1)S(1)}, bf16[512,2048]{1,0:T(8,128)(2,1)}, u32[]{:S(2)}) copy-start(bf16[512,2048]{1,0:T(8,128)(2,1)} %wo_ref.5) | copy-start | bytes 6291460
  7.7 8.1 %copy-start.7 = (bf16[2048,512]{1,0:T(8,128)(2,1)S(1)}, bf16[2048,512]{1,0:T(8,128)(2,1)}, u32[]{:S(2)}) copy-start(bf16[2048,512]{1,0:T(8,128)(2,1)} %get-tuple-element.16.w_ref) | copy-start | bytes 6291460 | tf_op jit(solution)/shard_map/cond
  7.7 8.1 %copy-start.8 = (bf16[64,2048]{1,0:T(8,128)(2,1)S(1)}, bf16[64,2048]{1,0:T(8,128)(2,1)}, u32[]{:S(2)}) copy-start(bf16[64,2048]{1,0:T(8,128)(2,1)} %get-tuple-element.15.s_ref) | copy-start | bytes 786436 | tf_op jit(solution)/shard_map/cond
  10.9 1.6 %collective-permute-start = (bf16[2,272,256]{2,1,0:T(8,128)(2,1)S(1)}, bf16[2,272,256]{2,1,0:T(8,128)(2,1)S(1)}, u32[]{:S(2)}, u32[]{:S(2)}) collective-permute-start(bf16[2,272,256]{2,1,0:T(8,128)(2,1)S(1)} %branch_1_fun.3.total_ref), channel_id=1, source_target_pairs={{0,4},{4,0},{8,12},{12,8},{1,5},{5,1},{9,13},{13,9},{2,6},{6,2},{1... | collective-permute-start | bytes 835592 | tf_op jit(solution)/shard_map/cond/branch_1_fun/ppermute | solution.py:329
  14.0 9.1 %collective-permute-start.1 = (bf16[2,272,256]{2,1,0:T(8,128)(2,1)}, bf16[2,272,256]{2,1,0:T(8,128)(2,1)}, u32[]{:S(2)}, u32[]{:S(2)}) collective-permute-start(bf16[2,272,256]{2,1,0:T(8,128)(2,1)} %get-tuple-element.130), channel_id=1, source_target_pairs={{0,8},{4,12},{8,0},{12,4},{1,9},{5,13},{9,1},{13,5},{2,10},{6,14},... | collective-permute-start | bytes 835592 | tf_op jit(solution)/shard_map/cond/branch_1_fun/ppermute | solution.py:329
  23.1 15.3 %copy-start.1 = (bf16[2048,512]{1,0:T(8,128)(2,1)S(1)}, bf16[2048,512]{1,0:T(8,128)(2,1)}, u32[]{:S(2)}) copy-start(bf16[2048,512]{1,0:T(8,128)(2,1)} %q_ref.7) | copy-start | bytes 6291460
  25.9 8.3 %collective-permute-start.2 = (bf16[32,2048]{1,0:T(8,128)(2,1)S(1)}, bf16[32,2048]{1,0:T(8,128)(2,1)S(1)}, u32[]{:S(2)}, u32[]{:S(2)}) collective-permute-start(bf16[32,2048]{1,0:T(8,128)(2,1)S(1)} %get-tuple-element.70), channel_id=1, source_target_pairs={{0,1},{1,0},{2,3},{3,2},{4,5},{5,4},{6,7},{7,6},{8,9},{9,8},{10,11... | collective-permute-start | bytes 393224 | tf_op jit(solution)/shard_map/ppermute | solution.py:329
  27.8 16.6 %collective-permute-start.8 = (bf16[2,272,256]{2,1,0:T(8,128)(2,1)S(1)}, bf16[2,272,256]{2,1,0:T(8,128)(2,1)S(1)}, u32[]{:S(2)}, u32[]{:S(2)}) collective-permute-start(bf16[2,272,256]{2,1,0:T(8,128)(2,1)S(1)} %get-tuple-element.78.m_ref), channel_id=1, source_target_pairs={{0,1},{1,0},{2,3},{3,2},{4,5},{5,4},{6,7},{7,6},{8,9},{9,8},{10,11... | collective-permute-start | bytes 835592 | tf_op jit(solution)/shard_map/ppermute | solution.py:329
  28.0 16.4 %collective-permute-start.5 = (bf16[512,512]{1,0:T(8,128)(2,1)S(1)}, bf16[512,512]{1,0:T(8,128)(2,1)S(1)}, u32[]{:S(2)}, u32[]{:S(2)}) collective-permute-start(bf16[512,512]{1,0:T(8,128)(2,1)S(1)} %collective-permute-done.4.rest_0_), channel_id=1, source_target_pairs={{0,16},{16,0},{1,17},{17,1},{2,18},{18,2},{3,19},{19,3},{4,20},{20... | collective-permute-start | bytes 1572872 | tf_op jit(solution)/shard_map/ppermute | solution.py:329
  31.4 13.0 %collective-permute-start.7 = (bf16[512,512]{1,0:T(8,128)(2,1)S(1)}, bf16[512,512]{1,0:T(8,128)(2,1)S(1)}, u32[]{:S(2)}, u32[]{:S(2)}) collective-permute-start(bf16[512,512]{1,0:T(8,128)(2,1)S(1)} %collective-permute-done.6.rest_4_), channel_id=1, source_target_pairs={{0,8},{4,12},{8,0},{12,4},{1,9},{5,13},{9,1},{13,5},{2,10},{6,14},... | collective-permute-start | bytes 1572872 | tf_op jit(solution)/shard_map/ppermute | solution.py:329
  34.3 10.1 %collective-permute-start.3 = (bf16[32,2048]{1,0:T(8,128)(2,1)S(1)}, bf16[32,2048]{1,0:T(8,128)(2,1)S(1)}, u32[]{:S(2)}, u32[]{:S(2)}) collective-permute-start(bf16[32,2048]{1,0:T(8,128)(2,1)S(1)} %add_convert_fusion.4), channel_id=1, source_target_pairs={{0,3},{1,2},{2,1},{3,0},{4,7},{5,6},{6,5},{7,4},{8,11},{9,10},{10,... | collective-permute-start | bytes 393224 | tf_op jit(solution)/shard_map/ppermute | solution.py:329
  38.4 6.6 %copy-start.4 = (bf16[2048,512]{1,0:T(8,128)(2,1)S(1)}, bf16[2048,512]{1,0:T(8,128)(2,1)}, u32[]{:S(2)}) copy-start(bf16[2048,512]{1,0:T(8,128)(2,1)} %k_ref.7) | copy-start | bytes 6291460
  38.4 6.6 %copy-start.5 = (bf16[2048,512]{1,0:T(8,128)(2,1)S(1)}, bf16[2048,512]{1,0:T(8,128)(2,1)}, u32[]{:S(2)}) copy-start(bf16[2048,512]{1,0:T(8,128)(2,1)} %v_ref.7) | copy-start | bytes 6291460
  43.3 4.7 %collective-permute-start.11 = (bf16[512,512]{1,0:T(8,128)(2,1)S(1)}, bf16[512,512]{1,0:T(8,128)(2,1)S(1)}, u32[]{:S(2)}, u32[]{:S(2)}) collective-permute-start(bf16[512,512]{1,0:T(8,128)(2,1)S(1)} %collective-permute-done.6.rest_4_), channel_id=1, source_target_pairs={{0,4},{4,0},{8,12},{12,8},{1,5},{5,1},{9,13},{13,9},{2,6},{6,2},{1... | collective-permute-start | bytes 1572872 | tf_op jit(solution)/shard_map/ppermute | solution.py:329
  44.4 3.6 %collective-permute-start.9 = (bf16[512,512]{1,0:T(8,128)(2,1)S(1)}, bf16[512,512]{1,0:T(8,128)(2,1)S(1)}, u32[]{:S(2)}, u32[]{:S(2)}) collective-permute-start(bf16[512,512]{1,0:T(8,128)(2,1)S(1)} %collective-permute-done.4.rest_0_), channel_id=1, source_target_pairs={{0,4},{4,0},{8,12},{12,8},{1,5},{5,1},{9,13},{13,9},{2,6},{6,2},{1... | collective-permute-start | bytes 1572872 | tf_op jit(solution)/shard_map/ppermute | solution.py:329
  44.4 3.6 %collective-permute-start.10 = (bf16[512,512]{1,0:T(8,128)(2,1)S(1)}, bf16[512,512]{1,0:T(8,128)(2,1)S(1)}, u32[]{:S(2)}, u32[]{:S(2)}) collective-permute-start(bf16[512,512]{1,0:T(8,128)(2,1)S(1)} %collective-permute-done.5.rest_1_), channel_id=1, source_target_pairs={{0,4},{4,0},{8,12},{12,8},{1,5},{5,1},{9,13},{13,9},{2,6},{6,2},{1... | collective-permute-start | bytes 1572872 | tf_op jit(solution)/shard_map/ppermute | solution.py:329
  45.0 3.0 %collective-permute-start.12 = (bf16[512,512]{1,0:T(8,128)(2,1)S(1)}, bf16[512,512]{1,0:T(8,128)(2,1)S(1)}, u32[]{:S(2)}, u32[]{:S(2)}) collective-permute-start(bf16[512,512]{1,0:T(8,128)(2,1)S(1)} %collective-permute-done.7.rest_5_), channel_id=1, source_target_pairs={{0,4},{4,0},{8,12},{12,8},{1,5},{5,1},{9,13},{13,9},{2,6},{6,2},{1... | collective-permute-start | bytes 1572872 | tf_op jit(solution)/shard_map/ppermute | solution.py:329
  50.4 8.4 %collective-permute-start.13 = (bf16[32,2048]{1,0:T(8,128)(2,1)S(1)}, bf16[32,2048]{1,0:T(8,128)(2,1)S(1)}, u32[]{:S(2)}, u32[]{:S(2)}) collective-permute-start(bf16[32,2048]{1,0:T(8,128)(2,1)S(1)} %shard_map.99), channel_id=1, source_target_pairs={{0,3},{1,2},{2,1},{3,0},{4,7},{5,6},{6,5},{7,4},{8,11},{9,10},{10,... | collective-permute-start | bytes 393224 | tf_op jit(solution)/shard_map/ppermute | solution.py:329
  61.3 7.1 %collective-permute-start.14 = (bf16[32,2048]{1,0:T(8,128)(2,1)S(1)}, bf16[32,2048]{1,0:T(8,128)(2,1)S(1)}, u32[]{:S(2)}, u32[]{:S(2)}) collective-permute-start(bf16[32,2048]{1,0:T(8,128)(2,1)S(1)} %shard_map.101), channel_id=1, source_target_pairs={{0,3},{1,2},{2,1},{3,0},{4,7},{5,6},{6,5},{7,4},{8,11},{9,10},{10,... | collective-permute-start | bytes 393224 | tf_op jit(solution)/shard_map/ppermute | solution.py:329
  70.8 6.9 %collective-permute-start.15 = (bf16[32,2048]{1,0:T(8,128)(2,1)S(1)}, bf16[32,2048]{1,0:T(8,128)(2,1)S(1)}, u32[]{:S(2)}, u32[]{:S(2)}) collective-permute-start(bf16[32,2048]{1,0:T(8,128)(2,1)S(1)} %shard_map.103), channel_id=1, source_target_pairs={{0,3},{1,2},{2,1},{3,0},{4,7},{5,6},{6,5},{7,4},{8,11},{9,10},{10,... | collective-permute-start | bytes 393224 | tf_op jit(solution)/shard_map/ppermute | solution.py:329
  77.8 5.0 %collective-permute-start.16 = (bf16[32,2048]{1,0:T(8,128)(2,1)S(1)}, bf16[32,2048]{1,0:T(8,128)(2,1)S(1)}, u32[]{:S(2)}, u32[]{:S(2)}) collective-permute-start(bf16[32,2048]{1,0:T(8,128)(2,1)S(1)} %add_convert_fusion), channel_id=1, source_target_pairs={{0,1},{1,0},{2,3},{3,2},{4,5},{5,4},{6,7},{7,6},{8,9},{9,8},{10,11... | collective-permute-start | bytes 393224 | tf_op jit(solution)/shard_map/ppermute | solution.py:329
  (4 other events, 12.7 us)

commit v7 on v6

--- a/solution.py
+++ b/solution.py
@@ -25,8 +25,8 @@
     return lax.dot_general(a, b, (dims, ((), ())), preferred_element_type=jnp.float32)
 
 
-def slice_kernel(depth, pieces, place_ref, wq_hbm, wo_hbm, query_hbm, output_hbm, query_ref, output_ref, sems):
-    at = [pl.multiple_of(place_ref[i] * depth, depth) for i in range(2)]
+def slice_kernel(depth, pieces, wq_hbm, wo_hbm, query_hbm, output_hbm, query_ref, output_ref, sems):
+    at = [pl.multiple_of(slice_index(stages) * depth, depth) for stages in (QUERY_STAGES, OUTPUT_STAGES)]
     tall, wide = depth // pieces, wo_hbm.shape[0] // pieces
     moves = []
     for i in range(pieces):
@@ -52,18 +52,18 @@
         back.wait()
 
 
-def weight_slices(place, wq, wo, depth):
+def weight_slices(wq, wo, depth):
     pieces = 4
     hbm = pl.BlockSpec(memory_space=pltpu.HBM)
     shapes = ((depth, wq.shape[1]), (wo.shape[0], depth))
     return pl.pallas_call(
         functools.partial(slice_kernel, depth, pieces),
-        in_specs=[pl.BlockSpec(memory_space=pltpu.SMEM), hbm, hbm],
+        in_specs=[hbm, hbm],
         out_specs=[hbm, hbm],
         out_shape=[jax.ShapeDtypeStruct(shape, wq.dtype) for shape in shapes],
         scratch_shapes=[pltpu.VMEM(shape, wq.dtype) for shape in shapes] + [pltpu.SemaphoreType.DMA((4 * pieces,))],
         compiler_params=pltpu.CompilerParams(vmem_limit_bytes=60 << 20),
-    )(place, wq, wo)
+    )(wq, wo)
 
 
 def update_kernel(heads, width, block, k_hbm, v_hbm, u_ref, k_ref, v_ref, acc, norm, sems):
@@ -288,7 +288,7 @@
     )(me, coef, state, lifted, total, got, early, wo)
 
 
-def wide_kernel(heads, width, slices, place_ref, state_ref, wq_ref, wo_ref, m_ref, mx_ref, *rest):
+def wide_kernel(heads, width, slices, state_ref, wq_ref, wo_ref, m_ref, mx_ref, *rest):
     query_refs, output_refs, (out_ref, acc) = rest[:slices], rest[slices : 2 * slices], rest[2 * slices :]
     group = heads * width
     depth = state_ref.shape[1] // slices
@@ -296,23 +296,23 @@
     own = read_heads(lift(dot(state_ref[...], wq_ref[...], ((1,), (0,)))).astype(jnp.bfloat16), m_ref, heads, width)
     query = jnp.zeros((state_ref.shape[0], group), jnp.float32)
     for j in range(slices):
-        at = pl.multiple_of((place_ref[0] ^ j) * depth, depth)
+        at = pl.multiple_of((slice_index(QUERY_STAGES) ^ j) * depth, depth)
         query += dot(state_ref[:, pl.ds(at, depth)], query_refs[j][...], ((1,), (0,)))
     other = read_heads(lift(query).astype(jnp.bfloat16), mx_ref, heads, width)
     acc[...] = dot(own, wo_ref[...], ((1,), (0,)))
     for j in range(slices):
-        at = pl.multiple_of((place_ref[1] ^ j) * depth, depth)
+        at = pl.multiple_of((slice_index(OUTPUT_STAGES) ^ j) * depth, depth)
         acc[:, pl.ds(at, depth)] += dot(other, output_refs[j][...], ((1,), (0,)))
     out_ref[...] = acc[...].astype(jnp.bfloat16)
 
 
-def wide_step(place, state, wq, wo, memory, query_side, output_side, other_memory, heads, width):
+def wide_step(state, wq, wo, memory, query_side, output_side, other_memory, heads, width):
     rows, lanes = state.shape
     slices = len(query_side)
     vmem = pl.BlockSpec(memory_space=pltpu.VMEM)
     return pl.pallas_call(
         functools.partial(wide_kernel, heads, width, slices),
-        in_specs=[pl.BlockSpec(memory_space=pltpu.SMEM)] + [vmem] * (5 + 2 * slices),
+        in_specs=[vmem] * (5 + 2 * slices),
         out_specs=vmem,
         out_shape=jax.ShapeDtypeStruct((rows, lanes), jnp.bfloat16),
         scratch_shapes=[pltpu.VMEM((rows, lanes), jnp.float32)],
@@ -322,7 +322,7 @@
             transcendentals=2 * rows * heads * width,
             bytes_accessed=4 * (wq.size + wo.size) + 4 * rows * lanes,
         ),
-    )(place, state, wq, wo, memory, other_memory, *query_side, *output_side)
+    )(state, wq, wo, memory, other_memory, *query_side, *output_side)
 
 
 def partner(x, axis, flip):
@@ -424,8 +424,7 @@
     flips = tuple((k << 1) | (k.bit_count() & 1) for k in range(parts // 2))
 
     depth = model >> len(QUERY_STAGES)
-    place = jnp.stack([slice_index(QUERY_STAGES), slice_index(OUTPUT_STAGES)])
-    query_block, output_block = weight_slices(place, wq_sum, wo_sum, depth)
+    query_block, output_block = weight_slices(wq_sum, wo_sum, depth)
     query_block = partner(query_block, "sub", 1)
     output_block = partner(output_block, "sub", 1)
 
@@ -485,7 +484,7 @@
     last = [[(3 * chunk, 0, heads)], [(2 * chunk, 0, heads)], []]
     for step in range(1, STEPS):
         partial = wide_step(
-            place, state, wq_sum, wo_sum, final, query_side, output_side, other_final, heads, width
+            state, wq_sum, wo_sum, final, query_side, output_side, other_final, heads, width
         )
         terms = exchange(partial)
         attended = fill(partial, attended, *last[step - 1])

time: 83.8 us -> 80.7 us (0.963)
  Pallas kernels: 36.7 us -> 34.3 us
    pallas_call x3, Pallas kernels: 7.09 us -> 5.46 us  [wide_step(): pl.pallas_call(functools.partial(wide_kernel, heads, width, slices), in_s...]
  transfers between devices with their start and end apart: 17 -> 17, of which waited for: 8 -> 8; matrix products, arithmetic and copies ran while one was open for 0% -> 1% of each run, Pallas kernels for 32% -> 33%
where the time goes in v7:
time: 80.7 us; the launch traced here: 80.5 us
  Pallas kernels  34.3 us (43%)
  starting transfers between devices  23.4 us (29%)
  waiting for transfers between devices  20.4 us (25%)
  between operations  0.99 us (1%)
  local copies, waits for them, and re-layouts  0.87 us (1%)
    ppermute x17, starting transfers between devices, partner(): lax.ppermute(x, axis, [(i, i ^ flip) for i in range(lax.axis_size(axis))])  23.4 us
    ppermute x17, waiting for transfers between devices, partner(): lax.ppermute(x, axis, [(i, i ^ flip) for i in range(lax.axis_size(axis))])  20.4 us
    pallas_call x4, Pallas kernels, attention_piece(): pl.pallas_call(functools.partial(attention_kernel, heads, head, width, fi...  18.4 us
    pallas_call x3, Pallas kernels, wide_step(): pl.pallas_call(functools.partial(wide_kernel, heads, width, slices), in_s...  5.46 us
    pallas_call x1, Pallas kernels, memory_update(): pl.pallas_call(functools.partial(update_kernel, heads, width, UPDATE_ROWS...  3.19 us
    pallas_call x1, Pallas kernels, first_step(): pl.pallas_call(functools.partial(first_kernel, heads, width, flips, parts...  2.77 us
    pallas_call x1, Pallas kernels, weight_slices(): pl.pallas_call(functools.partial(slice_kernel, depth, pieces), in_specs=[...  2.1 us
  transfers between devices with their start and end apart: 17, of which 8 were waited for; matrix products, arithmetic and copies ran while one was open for 1% of the time, Pallas kernels for 33%

profile of v7, /device:TPU:0, one launch (start us, length us, event | category | flops | bytes accessed | tf_op | source)
XLA Modules:
  0.0 80.5 jit_solution(8694664918591612689)
XLA Ops:
  0.6 2.1 %shard_map.97 = (bf16[512,512]{1,0:T(8,128)(2,1)}, bf16[512,512]{1,0:T(8,128)(2,1)}) custom-call(bf16[2048,512]{1,0:T(8,128)(2,1)} %wq_ref.5, bf16[512,2048]{1,0:T(8,128)(2,1)} %wo_ref.5), custom_call_target="tpu_custom_call" | custom-call | tf_op jit(solution)/shard_map/pallas_call | solution.py:59
  2.8 3.1 %collective-permute-start.4 = (bf16[512,512]{1,0:T(8,128)(2,1)}, bf16[512,512]{1,0:T(8,128)(2,1)S(1)}, u32[]{:S(2)}, u32[]{:S(2)}) collective-permute-start(bf16[512,512]{1,0:T(8,128)(2,1)} %get-tuple-element.73), channel_id=1, source_target_pairs={{0,1},{1,0},{2,3},{3,2},{4,5},{5,4},{6,7},{7,6},{8,9},{9,8},{10,11... | collective-permute-start | bytes 1572872 | tf_op jit(solution)/shard_map/ppermute | solution.py:329
  6.3 15.4 %conditional.1 = (bf16[2,272,256]{2,1,0:T(8,128)(2,1)}, bf16[2,272,256]{2,1,0:T(8,128)(2,1)}, bf16[2,272,256]{2,1,0:T(8,128)(2,1)S(1)}, bf16[64,512]{1,0:T(8,128)(2,1)S(1)}) conditional(s32[]{:T(128)} %bitcast.4, () %tuple.30, (bf16[2048,512]{1,0:T(8,128)(2,1)}, bf16[2048,512]{1,0:T(8,128)(2,1)}, f32[3,2]{1,0:T(4,128)S(1)}, ...), branch_computations={%region_6.7_spmd, %region_7.8_spmd} | conditional | flops 671645696 | bytes 19628202 | solution.py:443
  6.3 3.2 %branch_1_fun.3.total_ref = bf16[2,272,256]{2,1,0:T(8,128)(2,1)S(1)} custom-call(bf16[2048,512]{1,0:T(8,128)(2,1)} %get-tuple-element.11.k_hbm, bf16[2048,512]{1,0:T(8,128)(2,1)} %get-tuple-element.12.v_hbm), custom_call_target="tpu_custom_call" | custom-call | flops 536870912 | bytes 4194304 | tf_op jit(solution)/shard_map/cond/branch_1_fun/pallas_call | solution.py:105
  12.6 1.9 %collective-permute-start.1 = (bf16[2,272,256]{2,1,0:T(8,128)(2,1)}, bf16[2,272,256]{2,1,0:T(8,128)(2,1)}, u32[]{:S(2)}, u32[]{:S(2)}) collective-permute-start(bf16[2,272,256]{2,1,0:T(8,128)(2,1)} %get-tuple-element.130), channel_id=1, source_target_pairs={{0,8},{4,12},{8,0},{12,4},{1,9},{5,13},{9,1},{13,5},{2,10},{6,14},... | collective-permute-start | bytes 835592 | tf_op jit(solution)/shard_map/cond/branch_1_fun/ppermute | solution.py:329
  15.5 6.3 %collective-permute-done.1 = bf16[2,272,256]{2,1,0:T(8,128)(2,1)} collective-permute-done((bf16[2,272,256]{2,1,0:T(8,128)(2,1)}, bf16[2,272,256]{2,1,0:T(8,128)(2,1)}, u32[]{:S(2)}, u32[]{:S(2)}) %collective-permute-start.1) | collective-permute-done | bytes 278560 | tf_op jit(solution)/shard_map/cond/branch_1_fun/ppermute | solution.py:329
  21.7 2.8 %shard_map.95 = (bf16[32,2048]{1,0:T(8,128)(2,1)S(1)}, bf16[32,2048]{1,0:T(8,128)(2,1)S(1)}, bf16[32,2048]{1,0:T(8,128)(2,1)S(1)}, bf16[2,272,256]{2,1,0:T(8,128)(2,1)S(1)}, bf16[2,272,256]{2,1,0:T(8,128)(2,1)S(1)}) custom-call(s32[1]{0:T(128)} %bitcast.me_ref, f32[3,2]{1,0:T(4,128)S(1)} %pad_maximum_fusion.coef_ref, bf16[64,2048]{1,0:T(8,128)(2,1)} %state_ref.1, ...), custom_call_target="tpu_custom_call" | custom-call | flops 134217728 | bytes 2621440 | tf_op jit(solution)/shard_map/pallas_call | solution.py:272
  24.5 1.9 %collective-permute-start.2 = (bf16[32,2048]{1,0:T(8,128)(2,1)S(1)}, bf16[32,2048]{1,0:T(8,128)(2,1)S(1)}, u32[]{:S(2)}, u32[]{:S(2)}) collective-permute-start(bf16[32,2048]{1,0:T(8,128)(2,1)S(1)} %get-tuple-element.70), channel_id=1, source_target_pairs={{0,1},{1,0},{2,3},{3,2},{4,5},{5,4},{6,7},{7,6},{8,9},{9,8},{10,11... | collective-permute-start | bytes 393224 | tf_op jit(solution)/shard_map/ppermute | solution.py:329
  26.6 1.8 %collective-permute-start.5 = (bf16[512,512]{1,0:T(8,128)(2,1)S(1)}, bf16[512,512]{1,0:T(8,128)(2,1)S(1)}, u32[]{:S(2)}, u32[]{:S(2)}) collective-permute-start(bf16[512,512]{1,0:T(8,128)(2,1)S(1)} %collective-permute-done.4.rest_0_), channel_id=1, source_target_pairs={{0,16},{16,0},{1,17},{17,1},{2,18},{18,2},{3,19},{19,3},{4,20},{20... | collective-permute-start | bytes 1572872 | tf_op jit(solution)/shard_map/ppermute | solution.py:329
  28.4 1.7 %collective-permute-done.6.rest_4_ = bf16[512,512]{1,0:T(8,128)(2,1)S(1)} collective-permute-done((bf16[512,512]{1,0:T(8,128)(2,1)}, bf16[512,512]{1,0:T(8,128)(2,1)S(1)}, u32[]{:S(2)}, u32[]{:S(2)}) %collective-permute-start.6) | collective-permute-done | bytes 524320 | tf_op jit(solution)/shard_map/ppermute | solution.py:329
  30.0 2.0 %collective-permute-start.7 = (bf16[512,512]{1,0:T(8,128)(2,1)S(1)}, bf16[512,512]{1,0:T(8,128)(2,1)S(1)}, u32[]{:S(2)}, u32[]{:S(2)}) collective-permute-start(bf16[512,512]{1,0:T(8,128)(2,1)S(1)} %collective-permute-done.6.rest_4_), channel_id=1, source_target_pairs={{0,8},{4,12},{8,0},{12,4},{1,9},{5,13},{9,1},{13,5},{2,10},{6,14},... | collective-permute-start | bytes 1572872 | tf_op jit(solution)/shard_map/ppermute | solution.py:329
  32.9 4.1 %collective-permute-start.3 = (bf16[32,2048]{1,0:T(8,128)(2,1)S(1)}, bf16[32,2048]{1,0:T(8,128)(2,1)S(1)}, u32[]{:S(2)}, u32[]{:S(2)}) collective-permute-start(bf16[32,2048]{1,0:T(8,128)(2,1)S(1)} %add_convert_fusion.4), channel_id=1, source_target_pairs={{0,3},{1,2},{2,1},{3,0},{4,7},{5,6},{6,5},{7,4},{8,11},{9,10},{10,... | collective-permute-start | bytes 393224 | tf_op jit(solution)/shard_map/ppermute | solution.py:329
  37.0 4.9 %shard_map.96.rest_0_ = bf16[2048,512]{1,0:T(8,128)(2,1)} custom-call(f32[2]{0:T(128)S(1)} %copy-done.2, bf16[2048,512]{1,0:T(8,128)(2,1)S(1)} %copy-done.1, bf16[2048,512]{1,0:T(8,128)(2,1)} %k_ref.7, bf16[2048,512]{1,0:T(8,128)(2,1)} %v_ref.7, bf16[2,272,256]{2,1,0:T(8,128)(2,1)S(1)} %get-tuple-element.72.m_ref), custom_call_target="tpu_custom_call" | custom-call | flops 1073741824 | bytes 3145728 | tf_op jit(solution)/shard_map/pallas_call | solution.py:210
  43.7 2.8 %shard_map.98.rest_0_ = bf16[2048,512]{1,0:T(8,128)(2,1)} custom-call(f32[2]{0:T(128)S(1)} %copy-done.2, bf16[2048,512]{1,0:T(8,128)(2,1)S(1)} %copy-done.1, bf16[2048,512]{1,0:T(8,128)(2,1)S(1)} %copy-done.3, bf16[2048,512]{1,0:T(8,128)(2,1)S(1)} %copy-done.4, bf16[2,272,256]{2,1,0:T(8,128)(2,1)S(1)} %get-tuple-element.72.m_ref, ...), custom_call_target="tpu_custom_call", output_to_operand_aliasing={{}: (5, {})} | custom-call | flops 536870912 | bytes 2097152 | tf_op jit(solution)/shard_map/pallas_call | solution.py:210
  46.6 1.8 %shard_map.99 = bf16[32,2048]{1,0:T(8,128)(2,1)S(1)} custom-call(bf16[32,2048]{1,0:T(8,128)(2,1)S(1)} %add_convert_fusion.3.state_ref, bf16[2048,512]{1,0:T(8,128)(2,1)S(1)} %copy-done.5, bf16[512,2048]{1,0:T(8,128)(2,1)S(1)} %copy-done, bf16[2,272,256]{2,1,0:T(8,128)(2,1)S(1)} %get-tuple-element.78.m_ref, ...), custom_call_target="tpu_custom_call" | custom-call | flops 268435456 | bytes 8650752 | tf_op jit(solution)/shard_map/pallas_call | solution.py:313
  48.5 2.7 %collective-permute-start.13 = (bf16[32,2048]{1,0:T(8,128)(2,1)S(1)}, bf16[32,2048]{1,0:T(8,128)(2,1)S(1)}, u32[]{:S(2)}, u32[]{:S(2)}) collective-permute-start(bf16[32,2048]{1,0:T(8,128)(2,1)S(1)} %shard_map.99), channel_id=1, source_target_pairs={{0,3},{1,2},{2,1},{3,0},{4,7},{5,6},{6,5},{7,4},{8,11},{9,10},{10,... | collective-permute-start | bytes 393224 | tf_op jit(solution)/shard_map/ppermute | solution.py:329
  51.1 5.7 %shard_map.100.rest_0_ = bf16[2048,512]{1,0:T(8,128)(2,1)} custom-call(f32[2]{0:T(128)S(1)} %copy-done.2, bf16[2048,512]{1,0:T(8,128)(2,1)S(1)} %copy-done.1, bf16[2048,512]{1,0:T(8,128)(2,1)S(1)} %copy-done.3, bf16[2048,512]{1,0:T(8,128)(2,1)S(1)} %copy-done.4, bf16[2,272,256]{2,1,0:T(8,128)(2,1)S(1)} %get-tuple-element.72.m_ref, ...), custom_call_target="tpu_custom_call", output_to_operand_aliasing={{}: (5, {})} | custom-call | flops 2147483648 | bytes 5242880 | tf_op jit(solution)/shard_map/pallas_call | solution.py:210
  56.9 1.8 %shard_map.101 = bf16[32,2048]{1,0:T(8,128)(2,1)S(1)} custom-call(bf16[32,2048]{1,0:T(8,128)(2,1)S(1)} %add_convert_fusion.2.state_ref, bf16[2048,512]{1,0:T(8,128)(2,1)S(1)} %copy-done.5, bf16[512,2048]{1,0:T(8,128)(2,1)S(1)} %copy-done, bf16[2,272,256]{2,1,0:T(8,128)(2,1)S(1)} %get-tuple-element.78.m_ref, ...), custom_call_target="tpu_custom_call" | custom-call | flops 268435456 | bytes 8650752 | tf_op jit(solution)/shard_map/pallas_call | solution.py:313
  58.8 1.7 %collective-permute-start.14 = (bf16[32,2048]{1,0:T(8,128)(2,1)S(1)}, bf16[32,2048]{1,0:T(8,128)(2,1)S(1)}, u32[]{:S(2)}, u32[]{:S(2)}) collective-permute-start(bf16[32,2048]{1,0:T(8,128)(2,1)S(1)} %shard_map.101), channel_id=1, source_target_pairs={{0,3},{1,2},{2,1},{3,0},{4,7},{5,6},{6,5},{7,4},{8,11},{9,10},{10,... | collective-permute-start | bytes 393224 | tf_op jit(solution)/shard_map/ppermute | solution.py:329
  60.4 5.0 %shard_map.102 = bf16[2048,512]{1,0:T(8,128)(2,1)} custom-call(f32[2]{0:T(128)S(1)} %copy-done.2, bf16[2048,512]{1,0:T(8,128)(2,1)S(1)} %copy-done.1, bf16[2048,512]{1,0:T(8,128)(2,1)S(1)} %copy-done.3, bf16[2048,512]{1,0:T(8,128)(2,1)S(1)} %copy-done.4, bf16[2,272,256]{2,1,0:T(8,128)(2,1)S(1)} %get-tuple-element.72.m_ref, ...), custom_call_target="tpu_custom_call", output_to_operand_aliasing={{}: (5, {})} | custom-call | flops 1610612736 | bytes 4194304 | tf_op jit(solution)/shard_map/pallas_call | solution.py:210
  65.9 1.8 %shard_map.103 = bf16[32,2048]{1,0:T(8,128)(2,1)S(1)} custom-call(bf16[32,2048]{1,0:T(8,128)(2,1)S(1)} %add_convert_fusion.1.state_ref, bf16[2048,512]{1,0:T(8,128)(2,1)S(1)} %copy-done.5, bf16[512,2048]{1,0:T(8,128)(2,1)S(1)} %copy-done, bf16[2,272,256]{2,1,0:T(8,128)(2,1)S(1)} %get-tuple-element.78.m_ref, ...), custom_call_target="tpu_custom_call" | custom-call | flops 268435456 | bytes 8650752 | tf_op jit(solution)/shard_map/pallas_call | solution.py:313
  67.8 1.9 %collective-permute-start.15 = (bf16[32,2048]{1,0:T(8,128)(2,1)S(1)}, bf16[32,2048]{1,0:T(8,128)(2,1)S(1)}, u32[]{:S(2)}, u32[]{:S(2)}) collective-permute-start(bf16[32,2048]{1,0:T(8,128)(2,1)S(1)} %shard_map.103), channel_id=1, source_target_pairs={{0,3},{1,2},{2,1},{3,0},{4,7},{5,6},{6,5},{7,4},{8,11},{9,10},{10,... | collective-permute-start | bytes 393224 | tf_op jit(solution)/shard_map/ppermute | solution.py:329
  69.6 5.0 %collective-permute-done.15 = bf16[32,2048]{1,0:T(8,128)(2,1)S(1)} collective-permute-done((bf16[32,2048]{1,0:T(8,128)(2,1)S(1)}, bf16[32,2048]{1,0:T(8,128)(2,1)S(1)}, u32[]{:S(2)}, u32[]{:S(2)}) %collective-permute-start.15) | collective-permute-done | bytes 131104 | tf_op jit(solution)/shard_map/ppermute | solution.py:329
  76.3 3.5 %collective-permute-done.16 = bf16[32,2048]{1,0:T(8,128)(2,1)S(1)} collective-permute-done((bf16[32,2048]{1,0:T(8,128)(2,1)S(1)}, bf16[32,2048]{1,0:T(8,128)(2,1)S(1)}, u32[]{:S(2)}, u32[]{:S(2)}) %collective-permute-start.16) | collective-permute-done | bytes 131104 | tf_op jit(solution)/shard_map/ppermute | solution.py:329
  (70 shorter events, 10.1 us)
Async XLA Ops:
  0.6 5.6 %copy-start.2 = (f32[2]{0:T(128)S(1)}, f32[2]{0:T(128)}, u32[]{:S(2)}) copy-start(f32[2]{0:T(128)} %gate_ref.3) | copy-start | bytes 28
  2.8 23.9 %collective-permute-start.4 = (bf16[512,512]{1,0:T(8,128)(2,1)}, bf16[512,512]{1,0:T(8,128)(2,1)S(1)}, u32[]{:S(2)}, u32[]{:S(2)}) collective-permute-start(bf16[512,512]{1,0:T(8,128)(2,1)} %get-tuple-element.73), channel_id=1, source_target_pairs={{0,1},{1,0},{2,3},{3,2},{4,5},{5,4},{6,7},{7,6},{8,9},{9,8},{10,11... | collective-permute-start | bytes 1572872 | tf_op jit(solution)/shard_map/ppermute | solution.py:329
  5.8 24.2 %collective-permute-start.6 = (bf16[512,512]{1,0:T(8,128)(2,1)}, bf16[512,512]{1,0:T(8,128)(2,1)S(1)}, u32[]{:S(2)}, u32[]{:S(2)}) collective-permute-start(bf16[512,512]{1,0:T(8,128)(2,1)} %get-tuple-element.75), channel_id=1, source_target_pairs={{0,1},{1,0},{2,3},{3,2},{4,5},{5,4},{6,7},{7,6},{8,9},{9,8},{10,11... | collective-permute-start | bytes 1572872 | tf_op jit(solution)/shard_map/ppermute | solution.py:329
  6.3 15.4 %copy-start = (bf16[512,2048]{1,0:T(8,128)(2,1)S(1)}, bf16[512,2048]{1,0:T(8,128)(2,1)}, u32[]{:S(2)}) copy-start(bf16[512,2048]{1,0:T(8,128)(2,1)} %wo_ref.5) | copy-start | bytes 6291460
  6.3 8.1 %copy-start.6 = (bf16[2048,512]{1,0:T(8,128)(2,1)S(1)}, bf16[2048,512]{1,0:T(8,128)(2,1)}, u32[]{:S(2)}) copy-start(bf16[2048,512]{1,0:T(8,128)(2,1)} %get-tuple-element.16.w_ref) | copy-start | bytes 6291460 | tf_op jit(solution)/shard_map/cond
  6.3 8.1 %copy-start.7 = (bf16[64,2048]{1,0:T(8,128)(2,1)S(1)}, bf16[64,2048]{1,0:T(8,128)(2,1)}, u32[]{:S(2)}) copy-start(bf16[64,2048]{1,0:T(8,128)(2,1)} %get-tuple-element.15.s_ref) | copy-start | bytes 786436 | tf_op jit(solution)/shard_map/cond
  9.6 1.6 %collective-permute-start = (bf16[2,272,256]{2,1,0:T(8,128)(2,1)S(1)}, bf16[2,272,256]{2,1,0:T(8,128)(2,1)S(1)}, u32[]{:S(2)}, u32[]{:S(2)}) collective-permute-start(bf16[2,272,256]{2,1,0:T(8,128)(2,1)S(1)} %branch_1_fun.3.total_ref), channel_id=1, source_target_pairs={{0,4},{4,0},{8,12},{12,8},{1,5},{5,1},{9,13},{13,9},{2,6},{6,2},{1... | collective-permute-start | bytes 835592 | tf_op jit(solution)/shard_map/cond/branch_1_fun/ppermute | solution.py:329
  12.6 9.1 %collective-permute-start.1 = (bf16[2,272,256]{2,1,0:T(8,128)(2,1)}, bf16[2,272,256]{2,1,0:T(8,128)(2,1)}, u32[]{:S(2)}, u32[]{:S(2)}) collective-permute-start(bf16[2,272,256]{2,1,0:T(8,128)(2,1)} %get-tuple-element.130), channel_id=1, source_target_pairs={{0,8},{4,12},{8,0},{12,4},{1,9},{5,13},{9,1},{13,5},{2,10},{6,14},... | collective-permute-start | bytes 835592 | tf_op jit(solution)/shard_map/cond/branch_1_fun/ppermute | solution.py:329
  21.7 15.3 %copy-start.1 = (bf16[2048,512]{1,0:T(8,128)(2,1)S(1)}, bf16[2048,512]{1,0:T(8,128)(2,1)}, u32[]{:S(2)}) copy-start(bf16[2048,512]{1,0:T(8,128)(2,1)} %q_ref.7) | copy-start | bytes 6291460
  24.5 8.3 %collective-permute-start.2 = (bf16[32,2048]{1,0:T(8,128)(2,1)S(1)}, bf16[32,2048]{1,0:T(8,128)(2,1)S(1)}, u32[]{:S(2)}, u32[]{:S(2)}) collective-permute-start(bf16[32,2048]{1,0:T(8,128)(2,1)S(1)} %get-tuple-element.70), channel_id=1, source_target_pairs={{0,1},{1,0},{2,3},{3,2},{4,5},{5,4},{6,7},{7,6},{8,9},{9,8},{10,11... | collective-permute-start | bytes 393224 | tf_op jit(solution)/shard_map/ppermute | solution.py:329
  26.4 16.6 %collective-permute-start.8 = (bf16[2,272,256]{2,1,0:T(8,128)(2,1)S(1)}, bf16[2,272,256]{2,1,0:T(8,128)(2,1)S(1)}, u32[]{:S(2)}, u32[]{:S(2)}) collective-permute-start(bf16[2,272,256]{2,1,0:T(8,128)(2,1)S(1)} %get-tuple-element.78.m_ref), channel_id=1, source_target_pairs={{0,1},{1,0},{2,3},{3,2},{4,5},{5,4},{6,7},{7,6},{8,9},{9,8},{10,11... | collective-permute-start | bytes 835592 | tf_op jit(solution)/shard_map/ppermute | solution.py:329
  26.6 16.4 %collective-permute-start.5 = (bf16[512,512]{1,0:T(8,128)(2,1)S(1)}, bf16[512,512]{1,0:T(8,128)(2,1)S(1)}, u32[]{:S(2)}, u32[]{:S(2)}) collective-permute-start(bf16[512,512]{1,0:T(8,128)(2,1)S(1)} %collective-permute-done.4.rest_0_), channel_id=1, source_target_pairs={{0,16},{16,0},{1,17},{17,1},{2,18},{18,2},{3,19},{19,3},{4,20},{20... | collective-permute-start | bytes 1572872 | tf_op jit(solution)/shard_map/ppermute | solution.py:329
  30.0 13.0 %collective-permute-start.7 = (bf16[512,512]{1,0:T(8,128)(2,1)S(1)}, bf16[512,512]{1,0:T(8,128)(2,1)S(1)}, u32[]{:S(2)}, u32[]{:S(2)}) collective-permute-start(bf16[512,512]{1,0:T(8,128)(2,1)S(1)} %collective-permute-done.6.rest_4_), channel_id=1, source_target_pairs={{0,8},{4,12},{8,0},{12,4},{1,9},{5,13},{9,1},{13,5},{2,10},{6,14},... | collective-permute-start | bytes 1572872 | tf_op jit(solution)/shard_map/ppermute | solution.py:329
  32.9 10.1 %collective-permute-start.3 = (bf16[32,2048]{1,0:T(8,128)(2,1)S(1)}, bf16[32,2048]{1,0:T(8,128)(2,1)S(1)}, u32[]{:S(2)}, u32[]{:S(2)}) collective-permute-start(bf16[32,2048]{1,0:T(8,128)(2,1)S(1)} %add_convert_fusion.4), channel_id=1, source_target_pairs={{0,3},{1,2},{2,1},{3,0},{4,7},{5,6},{6,5},{7,4},{8,11},{9,10},{10,... | collective-permute-start | bytes 393224 | tf_op jit(solution)/shard_map/ppermute | solution.py:329
  37.0 6.6 %copy-start.3 = (bf16[2048,512]{1,0:T(8,128)(2,1)S(1)}, bf16[2048,512]{1,0:T(8,128)(2,1)}, u32[]{:S(2)}) copy-start(bf16[2048,512]{1,0:T(8,128)(2,1)} %k_ref.7) | copy-start | bytes 6291460
  37.0 6.6 %copy-start.4 = (bf16[2048,512]{1,0:T(8,128)(2,1)S(1)}, bf16[2048,512]{1,0:T(8,128)(2,1)}, u32[]{:S(2)}) copy-start(bf16[2048,512]{1,0:T(8,128)(2,1)} %v_ref.7) | copy-start | bytes 6291460
  41.9 4.7 %collective-permute-start.11 = (bf16[512,512]{1,0:T(8,128)(2,1)S(1)}, bf16[512,512]{1,0:T(8,128)(2,1)S(1)}, u32[]{:S(2)}, u32[]{:S(2)}) collective-permute-start(bf16[512,512]{1,0:T(8,128)(2,1)S(1)} %collective-permute-done.6.rest_4_), channel_id=1, source_target_pairs={{0,4},{4,0},{8,12},{12,8},{1,5},{5,1},{9,13},{13,9},{2,6},{6,2},{1... | collective-permute-start | bytes 1572872 | tf_op jit(solution)/shard_map/ppermute | solution.py:329
  43.0 3.6 %collective-permute-start.9 = (bf16[512,512]{1,0:T(8,128)(2,1)S(1)}, bf16[512,512]{1,0:T(8,128)(2,1)S(1)}, u32[]{:S(2)}, u32[]{:S(2)}) collective-permute-start(bf16[512,512]{1,0:T(8,128)(2,1)S(1)} %collective-permute-done.4.rest_0_), channel_id=1, source_target_pairs={{0,4},{4,0},{8,12},{12,8},{1,5},{5,1},{9,13},{13,9},{2,6},{6,2},{1... | collective-permute-start | bytes 1572872 | tf_op jit(solution)/shard_map/ppermute | solution.py:329
  43.0 3.6 %collective-permute-start.10 = (bf16[512,512]{1,0:T(8,128)(2,1)S(1)}, bf16[512,512]{1,0:T(8,128)(2,1)S(1)}, u32[]{:S(2)}, u32[]{:S(2)}) collective-permute-start(bf16[512,512]{1,0:T(8,128)(2,1)S(1)} %collective-permute-done.5.rest_1_), channel_id=1, source_target_pairs={{0,4},{4,0},{8,12},{12,8},{1,5},{5,1},{9,13},{13,9},{2,6},{6,2},{1... | collective-permute-start | bytes 1572872 | tf_op jit(solution)/shard_map/ppermute | solution.py:329
  43.6 3.0 %collective-permute-start.12 = (bf16[512,512]{1,0:T(8,128)(2,1)S(1)}, bf16[512,512]{1,0:T(8,128)(2,1)S(1)}, u32[]{:S(2)}, u32[]{:S(2)}) collective-permute-start(bf16[512,512]{1,0:T(8,128)(2,1)S(1)} %collective-permute-done.7.rest_5_), channel_id=1, source_target_pairs={{0,4},{4,0},{8,12},{12,8},{1,5},{5,1},{9,13},{13,9},{2,6},{6,2},{1... | collective-permute-start | bytes 1572872 | tf_op jit(solution)/shard_map/ppermute | solution.py:329
  48.5 8.4 %collective-permute-start.13 = (bf16[32,2048]{1,0:T(8,128)(2,1)S(1)}, bf16[32,2048]{1,0:T(8,128)(2,1)S(1)}, u32[]{:S(2)}, u32[]{:S(2)}) collective-permute-start(bf16[32,2048]{1,0:T(8,128)(2,1)S(1)} %shard_map.99), channel_id=1, source_target_pairs={{0,3},{1,2},{2,1},{3,0},{4,7},{5,6},{6,5},{7,4},{8,11},{9,10},{10,... | collective-permute-start | bytes 393224 | tf_op jit(solution)/shard_map/ppermute | solution.py:329
  58.8 7.1 %collective-permute-start.14 = (bf16[32,2048]{1,0:T(8,128)(2,1)S(1)}, bf16[32,2048]{1,0:T(8,128)(2,1)S(1)}, u32[]{:S(2)}, u32[]{:S(2)}) collective-permute-start(bf16[32,2048]{1,0:T(8,128)(2,1)S(1)} %shard_map.101), channel_id=1, source_target_pairs={{0,3},{1,2},{2,1},{3,0},{4,7},{5,6},{6,5},{7,4},{8,11},{9,10},{10,... | collective-permute-start | bytes 393224 | tf_op jit(solution)/shard_map/ppermute | solution.py:329
  67.8 6.9 %collective-permute-start.15 = (bf16[32,2048]{1,0:T(8,128)(2,1)S(1)}, bf16[32,2048]{1,0:T(8,128)(2,1)S(1)}, u32[]{:S(2)}, u32[]{:S(2)}) collective-permute-start(bf16[32,2048]{1,0:T(8,128)(2,1)S(1)} %shard_map.103), channel_id=1, source_target_pairs={{0,3},{1,2},{2,1},{3,0},{4,7},{5,6},{6,5},{7,4},{8,11},{9,10},{10,... | collective-permute-start | bytes 393224 | tf_op jit(solution)/shard_map/ppermute | solution.py:329
  74.7 5.0 %collective-permute-start.16 = (bf16[32,2048]{1,0:T(8,128)(2,1)S(1)}, bf16[32,2048]{1,0:T(8,128)(2,1)S(1)}, u32[]{:S(2)}, u32[]{:S(2)}) collective-permute-start(bf16[32,2048]{1,0:T(8,128)(2,1)S(1)} %add_convert_fusion), channel_id=1, source_target_pairs={{0,1},{1,0},{2,3},{3,2},{4,5},{5,4},{6,7},{7,6},{8,9},{9,8},{10,11... | collective-permute-start | bytes 393224 | tf_op jit(solution)/shard_map/ppermute | solution.py:329
  (3 other events, 9.0 us)
